TPU v7x, 512 devices: a whole 4x8x8 slice. The times are simulated.
512 devices in a mesh: node: 64 (over y_hi, z, x), head: 8 (over y_lo, core).
Axes of the slice: x: 4, y: 8 (y_hi: 2, y_lo: 4; y = y_hi * 4 + y_lo), z: 8, core: 2. Of those that a mesh axis runs over, the one named last changes fastest.
Arguments:
- features: bfloat16 [8192, 128], P('node'), may hold values from -1201 to 1201
- proj_weight: bfloat16 [128, 1024], P(None, 'head'), may hold values from -1 to 1
- score_source: float32 [8, 128], P('head'), may hold values from -1 to 1
- score_target: float32 [8, 128], P('head'), may hold values from -1 to 1
- out_weight: bfloat16 [1024, 256], P('head'), may hold values from -0.1875 to 0.1875
- presence: int32 [64, 64], P('node'), may hold values from 0 to 1, as said below
- tile_masks: int32 [64, 16, 128, 128], P('node'), may hold values 0 or 1
Outputs:
- mixed: bfloat16 [8192, 256], P('node')
Inputs may be any that keep to these rules, and one draw needn't show every extreme that they name: Each row holds exactly 16 ones; tile_masks[r, k] belongs to the k-th present tile of row r of presence, counted in ascending order of tile.
All inputs are finite; a program needn't handle non-finite values. No bound on the sum of `tile_masks` on one device may be relied on, other than what follows from the above.
Results may differ from a plain program's by a relative error of at most 0.015.
Values may be sent and summed in bfloat16 or wider, within the bound.
No kernel may reach another device: no remote copies, remote signals or barrier semaphores. Data moves between devices by JAX's collectives and lax.ppermute only.
A program may use at most 64 MiB of HBM per device.

v0:
```python
import math

import jax
import jax.numpy as jnp
from jax import lax
from jax.sharding import PartitionSpec as P


def leaky_relu(values):
    return jnp.where(values > 0, values, 0.2 * values)


def per_device(features, proj_weight, score_source, score_target, out_weight, presence, tile_masks):
    target_count = features.shape[0]
    heads_here = score_source.shape[0]
    head_width = score_source.shape[1]
    tile_width = tile_masks.shape[-1]
    row_tiles = presence.shape[0]

    def project(rows):
        return jnp.dot(rows, proj_weight, preferred_element_type=jnp.float32).astype(jnp.bfloat16)

    def head_terms(projected, vectors):
        widened = lax.optimization_barrier(projected).astype(jnp.float32)
        widened = widened.reshape(projected.shape[0], heads_here, head_width)
        return jnp.sum(widened * vectors[None], axis=-1).T

    local_proj = project(features)
    target_terms = head_terms(local_proj, score_target)
    first_row = lax.axis_index("node") * target_count
    target_ids = first_row + jnp.arange(target_count, dtype=jnp.int32)
    slots = jnp.maximum(jnp.cumsum(presence, axis=1) - 1, 0)
    tile_rows = jnp.arange(row_tiles, dtype=jnp.int32)

    def absorb(carry, block):
        running, denominator, accum = carry
        block_values, block_source, block_start = block
        span_rows = block_values.shape[0]
        column_ids = block_start + jnp.arange(span_rows, dtype=jnp.int32)
        column_tiles = column_ids // tile_width
        column_lanes = column_ids % tile_width
        present_here = jnp.take(presence, column_tiles, axis=1)
        slot_here = jnp.take(slots, column_tiles, axis=1)
        gathered = tile_masks[tile_rows[:, None], slot_here, :, column_lanes[None, :]]
        tile_bits = (
            (gathered * present_here[:, :, None])
            .transpose(0, 2, 1)
            .reshape(target_count, span_rows)
        )
        itself = column_ids[None, :] == target_ids[:, None]
        linked = (tile_bits == 1) & jnp.logical_not(itself) | itself
        edge_scores = leaky_relu(target_terms[:, :, None] + block_source[:, None, :])
        edge_scores = jnp.where(linked[None], edge_scores, -1e30)
        new_peak = jnp.maximum(running, jnp.max(edge_scores, axis=-1))
        edge_weights = jnp.where(linked[None], jnp.exp(edge_scores - new_peak[:, :, None]), 0.0)
        factor = jnp.exp(running - new_peak)
        denominator = denominator * factor + jnp.sum(edge_weights, axis=-1)
        update = jnp.einsum(
            "htb,bhd->htd",
            edge_weights.astype(jnp.bfloat16),
            block_values.reshape(span_rows, heads_here, head_width),
            preferred_element_type=jnp.float32,
        )
        accum = accum * factor[:, :, None] + update
        return ((new_peak, denominator, accum), None)

    initial = (
        jnp.full((heads_here, target_count), -1e30, jnp.float32),
        jnp.zeros((heads_here, target_count), jnp.float32),
        jnp.zeros((heads_here, target_count, head_width), jnp.float32),
    )
    carry = initial
    block_values = project(lax.all_gather(features, "node", axis=0, tiled=True))
    total_rows = block_values.shape[0]
    stride = math.gcd(total_rows, 1024)
    blocks = total_rows // stride
    block_source = head_terms(block_values, score_source)
    stacked = (
        block_values.reshape(blocks, stride, heads_here * head_width),
        block_source.reshape(heads_here, blocks, stride).transpose(1, 0, 2),
        stride * jnp.arange(blocks, dtype=jnp.int32),
    )
    carry, unused = lax.scan(absorb, carry, stacked)
    running, denominator, accum = carry
    heads_out = jax.nn.elu(accum / denominator[:, :, None]).astype(jnp.bfloat16)
    heads_out = heads_out.transpose(1, 0, 2).reshape(target_count, heads_here * head_width)
    partial_sum = jnp.dot(heads_out, out_weight, preferred_element_type=jnp.float32)
    result = lax.psum(partial_sum.astype(jnp.bfloat16), "head")
    return result


def solution(mesh):
    return jax.shard_map(
        per_device,
        mesh=mesh,
        in_specs=(
            P("node", None),
            P(None, "head"),
            P("head", None),
            P("head", None),
            P("head", None),
            P("node", None),
            P("node", None, None, None),
        ),
        out_specs=P("node", None),
        check_vma=False,
    )
```

profile of v0, /device:TPU:1, one launch (start us, length us, event | category | flops | bytes accessed | tf_op | source)
XLA Modules:
  0.0 1014.7 jit_solution(6120727612200111464)
XLA Ops:
  9.5 137.3 %all-gather.2.cloned.1.call-done = bf16[8192,128]{1,0:T(8,128)(2,1)} async-done(((bf16[128,128]{1,0:T(8,128)(2,1)}), bf16[8192,128]{1,0:T(8,128)(2,1)}) %all-gather.2.cloned.1.call-update) | async-done | bytes 2097168 | tf_op jit(solution)/shard_map/all_gather | solution.py:73
  150.4 781.3 %while.17 = (s32[]{:T(128)}, f32[1,128]{1,0:T(1,128)S(1)}, f32[1,128]{1,0:T(1,128)S(1)}, f32[1,128,128]{2,1,0:T(8,128)S(1)}, s32[8]{0:T(128)S(1)}, /*index=5*/s3...) while((s32[]{:T(128)}, f32[1,128]{1,0:T(1,128)S(1)}, ...), condition=%wide.region_6.8_spmd.clone, body=%wide.region_3.7_spmd.clone.sunk | while | flops 37613440 | bytes 2482873 | solution.py:83
  154.0 40.4 %select_select_fusion.5 = s32[1024]{0:T(1024)S(1)} fusion(s32[]{:T(128)} %bitcast.403, s32[]{:T(128)} %bitcast.404, s32[]{:T(128)} %bitcast.405, s32[]{:T(128)} %bitcast.406, s32[]{:T(128)} %bitcast.407, s32[]{:T(128)} %bitcast.408, s32[]{:T(128)} %bitcast.409, s32[]{:T(128)} %bitcast.410, s32[]{:T(128)} %bitcast.411, s32[]{:T(128)} %bitcast.412, ...), kind=kLoop, calls=%fused_computation.49.clone.1 | loop fusion | flops 152576 | bytes 4356 | tf_op jit(solution)/shard_map/while/body/eval_jaxpr/jit(_take)/select_n | solution.py:43
  195.2 6.8 gather_fusion
  204.2 40.6 %select_select_fusion.4 = s32[1024]{0:T(1024)S(1)} fusion(s32[]{:T(128)} %bitcast.339, s32[]{:T(128)} %bitcast.340, s32[]{:T(128)} %bitcast.341, s32[]{:T(128)} %bitcast.342, s32[]{:T(128)} %bitcast.343, s32[]{:T(128)} %bitcast.344, s32[]{:T(128)} %bitcast.345, s32[]{:T(128)} %bitcast.346, s32[]{:T(128)} %bitcast.347, s32[]{:T(128)} %bitcast.348, ...), kind=kLoop, calls=%fused_computation.48.clone.1 | loop fusion | flops 152576 | bytes 4356 | tf_op jit(solution)/shard_map/while/body/eval_jaxpr/jit(_take)/select_n | solution.py:42
  251.6 40.4 %select_select_fusion.5 = s32[1024]{0:T(1024)S(1)} fusion(s32[]{:T(128)} %bitcast.403, s32[]{:T(128)} %bitcast.404, s32[]{:T(128)} %bitcast.405, s32[]{:T(128)} %bitcast.406, s32[]{:T(128)} %bitcast.407, s32[]{:T(128)} %bitcast.408, s32[]{:T(128)} %bitcast.409, s32[]{:T(128)} %bitcast.410, s32[]{:T(128)} %bitcast.411, s32[]{:T(128)} %bitcast.412, ...), kind=kLoop, calls=%fused_computation.49.clone.1 | loop fusion | flops 152576 | bytes 4356 | tf_op jit(solution)/shard_map/while/body/eval_jaxpr/jit(_take)/select_n | solution.py:43
  292.9 6.8 gather_fusion
  301.9 40.6 %select_select_fusion.4 = s32[1024]{0:T(1024)S(1)} fusion(s32[]{:T(128)} %bitcast.339, s32[]{:T(128)} %bitcast.340, s32[]{:T(128)} %bitcast.341, s32[]{:T(128)} %bitcast.342, s32[]{:T(128)} %bitcast.343, s32[]{:T(128)} %bitcast.344, s32[]{:T(128)} %bitcast.345, s32[]{:T(128)} %bitcast.346, s32[]{:T(128)} %bitcast.347, s32[]{:T(128)} %bitcast.348, ...), kind=kLoop, calls=%fused_computation.48.clone.1 | loop fusion | flops 152576 | bytes 4356 | tf_op jit(solution)/shard_map/while/body/eval_jaxpr/jit(_take)/select_n | solution.py:42
  349.3 40.4 %select_select_fusion.5 = s32[1024]{0:T(1024)S(1)} fusion(s32[]{:T(128)} %bitcast.403, s32[]{:T(128)} %bitcast.404, s32[]{:T(128)} %bitcast.405, s32[]{:T(128)} %bitcast.406, s32[]{:T(128)} %bitcast.407, s32[]{:T(128)} %bitcast.408, s32[]{:T(128)} %bitcast.409, s32[]{:T(128)} %bitcast.410, s32[]{:T(128)} %bitcast.411, s32[]{:T(128)} %bitcast.412, ...), kind=kLoop, calls=%fused_computation.49.clone.1 | loop fusion | flops 152576 | bytes 4356 | tf_op jit(solution)/shard_map/while/body/eval_jaxpr/jit(_take)/select_n | solution.py:43
  390.5 6.8 gather_fusion
  399.5 40.6 %select_select_fusion.4 = s32[1024]{0:T(1024)S(1)} fusion(s32[]{:T(128)} %bitcast.339, s32[]{:T(128)} %bitcast.340, s32[]{:T(128)} %bitcast.341, s32[]{:T(128)} %bitcast.342, s32[]{:T(128)} %bitcast.343, s32[]{:T(128)} %bitcast.344, s32[]{:T(128)} %bitcast.345, s32[]{:T(128)} %bitcast.346, s32[]{:T(128)} %bitcast.347, s32[]{:T(128)} %bitcast.348, ...), kind=kLoop, calls=%fused_computation.48.clone.1 | loop fusion | flops 152576 | bytes 4356 | tf_op jit(solution)/shard_map/while/body/eval_jaxpr/jit(_take)/select_n | solution.py:42
  447.0 40.4 %select_select_fusion.5 = s32[1024]{0:T(1024)S(1)} fusion(s32[]{:T(128)} %bitcast.403, s32[]{:T(128)} %bitcast.404, s32[]{:T(128)} %bitcast.405, s32[]{:T(128)} %bitcast.406, s32[]{:T(128)} %bitcast.407, s32[]{:T(128)} %bitcast.408, s32[]{:T(128)} %bitcast.409, s32[]{:T(128)} %bitcast.410, s32[]{:T(128)} %bitcast.411, s32[]{:T(128)} %bitcast.412, ...), kind=kLoop, calls=%fused_computation.49.clone.1 | loop fusion | flops 152576 | bytes 4356 | tf_op jit(solution)/shard_map/while/body/eval_jaxpr/jit(_take)/select_n | solution.py:43
  488.2 6.8 gather_fusion
  497.2 40.6 %select_select_fusion.4 = s32[1024]{0:T(1024)S(1)} fusion(s32[]{:T(128)} %bitcast.339, s32[]{:T(128)} %bitcast.340, s32[]{:T(128)} %bitcast.341, s32[]{:T(128)} %bitcast.342, s32[]{:T(128)} %bitcast.343, s32[]{:T(128)} %bitcast.344, s32[]{:T(128)} %bitcast.345, s32[]{:T(128)} %bitcast.346, s32[]{:T(128)} %bitcast.347, s32[]{:T(128)} %bitcast.348, ...), kind=kLoop, calls=%fused_computation.48.clone.1 | loop fusion | flops 152576 | bytes 4356 | tf_op jit(solution)/shard_map/while/body/eval_jaxpr/jit(_take)/select_n | solution.py:42
  544.6 40.4 %select_select_fusion.5 = s32[1024]{0:T(1024)S(1)} fusion(s32[]{:T(128)} %bitcast.403, s32[]{:T(128)} %bitcast.404, s32[]{:T(128)} %bitcast.405, s32[]{:T(128)} %bitcast.406, s32[]{:T(128)} %bitcast.407, s32[]{:T(128)} %bitcast.408, s32[]{:T(128)} %bitcast.409, s32[]{:T(128)} %bitcast.410, s32[]{:T(128)} %bitcast.411, s32[]{:T(128)} %bitcast.412, ...), kind=kLoop, calls=%fused_computation.49.clone.1 | loop fusion | flops 152576 | bytes 4356 | tf_op jit(solution)/shard_map/while/body/eval_jaxpr/jit(_take)/select_n | solution.py:43
  585.9 6.8 gather_fusion
  594.9 40.6 %select_select_fusion.4 = s32[1024]{0:T(1024)S(1)} fusion(s32[]{:T(128)} %bitcast.339, s32[]{:T(128)} %bitcast.340, s32[]{:T(128)} %bitcast.341, s32[]{:T(128)} %bitcast.342, s32[]{:T(128)} %bitcast.343, s32[]{:T(128)} %bitcast.344, s32[]{:T(128)} %bitcast.345, s32[]{:T(128)} %bitcast.346, s32[]{:T(128)} %bitcast.347, s32[]{:T(128)} %bitcast.348, ...), kind=kLoop, calls=%fused_computation.48.clone.1 | loop fusion | flops 152576 | bytes 4356 | tf_op jit(solution)/shard_map/while/body/eval_jaxpr/jit(_take)/select_n | solution.py:42
  642.3 40.4 %select_select_fusion.5 = s32[1024]{0:T(1024)S(1)} fusion(s32[]{:T(128)} %bitcast.403, s32[]{:T(128)} %bitcast.404, s32[]{:T(128)} %bitcast.405, s32[]{:T(128)} %bitcast.406, s32[]{:T(128)} %bitcast.407, s32[]{:T(128)} %bitcast.408, s32[]{:T(128)} %bitcast.409, s32[]{:T(128)} %bitcast.410, s32[]{:T(128)} %bitcast.411, s32[]{:T(128)} %bitcast.412, ...), kind=kLoop, calls=%fused_computation.49.clone.1 | loop fusion | flops 152576 | bytes 4356 | tf_op jit(solution)/shard_map/while/body/eval_jaxpr/jit(_take)/select_n | solution.py:43
  692.5 40.6 %select_select_fusion.4 = s32[1024]{0:T(1024)S(1)} fusion(s32[]{:T(128)} %bitcast.339, s32[]{:T(128)} %bitcast.340, s32[]{:T(128)} %bitcast.341, s32[]{:T(128)} %bitcast.342, s32[]{:T(128)} %bitcast.343, s32[]{:T(128)} %bitcast.344, s32[]{:T(128)} %bitcast.345, s32[]{:T(128)} %bitcast.346, s32[]{:T(128)} %bitcast.347, s32[]{:T(128)} %bitcast.348, ...), kind=kLoop, calls=%fused_computation.48.clone.1 | loop fusion | flops 152576 | bytes 4356 | tf_op jit(solution)/shard_map/while/body/eval_jaxpr/jit(_take)/select_n | solution.py:42
  740.0 40.4 %select_select_fusion.5 = s32[1024]{0:T(1024)S(1)} fusion(s32[]{:T(128)} %bitcast.403, s32[]{:T(128)} %bitcast.404, s32[]{:T(128)} %bitcast.405, s32[]{:T(128)} %bitcast.406, s32[]{:T(128)} %bitcast.407, s32[]{:T(128)} %bitcast.408, s32[]{:T(128)} %bitcast.409, s32[]{:T(128)} %bitcast.410, s32[]{:T(128)} %bitcast.411, s32[]{:T(128)} %bitcast.412, ...), kind=kLoop, calls=%fused_computation.49.clone.1 | loop fusion | flops 152576 | bytes 4356 | tf_op jit(solution)/shard_map/while/body/eval_jaxpr/jit(_take)/select_n | solution.py:43
  790.2 40.6 %select_select_fusion.4 = s32[1024]{0:T(1024)S(1)} fusion(s32[]{:T(128)} %bitcast.339, s32[]{:T(128)} %bitcast.340, s32[]{:T(128)} %bitcast.341, s32[]{:T(128)} %bitcast.342, s32[]{:T(128)} %bitcast.343, s32[]{:T(128)} %bitcast.344, s32[]{:T(128)} %bitcast.345, s32[]{:T(128)} %bitcast.346, s32[]{:T(128)} %bitcast.347, s32[]{:T(128)} %bitcast.348, ...), kind=kLoop, calls=%fused_computation.48.clone.1 | loop fusion | flops 152576 | bytes 4356 | tf_op jit(solution)/shard_map/while/body/eval_jaxpr/jit(_take)/select_n | solution.py:42
  837.6 40.4 %select_select_fusion.5 = s32[1024]{0:T(1024)S(1)} fusion(s32[]{:T(128)} %bitcast.403, s32[]{:T(128)} %bitcast.404, s32[]{:T(128)} %bitcast.405, s32[]{:T(128)} %bitcast.406, s32[]{:T(128)} %bitcast.407, s32[]{:T(128)} %bitcast.408, s32[]{:T(128)} %bitcast.409, s32[]{:T(128)} %bitcast.410, s32[]{:T(128)} %bitcast.411, s32[]{:T(128)} %bitcast.412, ...), kind=kLoop, calls=%fused_computation.49.clone.1 | loop fusion | flops 152576 | bytes 4356 | tf_op jit(solution)/shard_map/while/body/eval_jaxpr/jit(_take)/select_n | solution.py:43
  887.9 40.6 %select_select_fusion.4 = s32[1024]{0:T(1024)S(1)} fusion(s32[]{:T(128)} %bitcast.339, s32[]{:T(128)} %bitcast.340, s32[]{:T(128)} %bitcast.341, s32[]{:T(128)} %bitcast.342, s32[]{:T(128)} %bitcast.343, s32[]{:T(128)} %bitcast.344, s32[]{:T(128)} %bitcast.345, s32[]{:T(128)} %bitcast.346, s32[]{:T(128)} %bitcast.347, s32[]{:T(128)} %bitcast.348, ...), kind=kLoop, calls=%fused_computation.48.clone.1 | loop fusion | flops 152576 | bytes 4356 | tf_op jit(solution)/shard_map/while/body/eval_jaxpr/jit(_take)/select_n | solution.py:42
  932.7 73.7 %all-reduce.2.cloned.1.call-done = bf16[128,256]{1,0:T(8,128)(2,1)} async-done(((bf16[128,256]{1,0:T(8,128)(2,1)}), bf16[128,256]{1,0:T(8,128)(2,1)}) %all-reduce.2.cloned.1.call-update) | async-done | bytes 65552 | tf_op jit(solution)/shard_map/psum | solution.py:88
  (210 shorter events, 106.7 us)
Async XLA Ops:
  6.5 925.2 %copy-start = (bf16[128,256]{1,0:T(8,128)(2,1)S(1)}, bf16[128,256]{1,0:T(8,128)(2,1)}, u32[]{:S(2)}) copy-start(bf16[128,256]{1,0:T(8,128)(2,1)} %param.15) | copy-start | bytes 196612
  6.5 2.4 copy-start.4
  6.5 2.4 copy-start.3
  6.5 2.5 copy-start.1
  6.5 2.8 copy-start.5
  6.5 140.2 %all-gather.2.cloned.1.call-start = ((), (), s32[]{:S(2)}) async-start(), calls=%async_computation | async-start | bytes 2129920 | tf_op jit(solution)/shard_map/all_gather | solution.py:73
  7.3 999.1 %all-reduce.2.cloned.1.call-start = ((), (), s32[]{:S(2)}) async-start(), calls=%async_computation.1 | async-start | bytes 131072 | tf_op jit(solution)/shard_map/psum | solution.py:88
  9.5 139.6 %copy-start.6 = (f32[1,128]{1,0:T(1,128)S(1)}, f32[1,128]{1,0:T(1,128)}, u32[]{:S(2)}) copy-start(f32[1,128]{1,0:T(1,128)} %param.13) | copy-start | bytes 1540
  149.1 1.3 copy-start.2
Sparse Core Ops, SparseCore 0:
  11.7 135.0 all-gather.1
  932.8 73.5 all-reduce.1
where the time goes:
time: 1030 us; the launch traced here: 1010 us
  other arithmetic  670 us (65%)
  waiting for transfers between devices  212 us (21%)
  local copies, waits for them, and re-layouts  104 us (10%)
  matrix products  14.9 us (1%)
  between operations  13.5 us (1%)
    select_n x8, other arithmetic, absorb(): present_here = jnp.take(presence, column_tiles, axis=1)  325 us
    select_n x8, other arithmetic, absorb(): slot_here = jnp.take(slots, column_tiles, axis=1)  323 us
    all_gather x1, waiting for transfers between devices, per_device(): block_values = project(lax.all_gather(features, 'node', axis=0, tiled=True))  137 us
    psum x1, waiting for transfers between devices, per_device(): result = lax.psum(partial_sum.astype(jnp.bfloat16), 'head')  73.7 us
    gather x8, local copies, waits for them, and re-layouts, absorb(): tile_masks[tile_rows[:, None], slot_here, :, column_lanes[None, :]]  54.3 us
    gather x32, local copies, waits for them, and re-layouts, absorb(): slot_here = jnp.take(slots, column_tiles, axis=1)  23.1 us
  transfers between devices with their start and end apart: 2, of which 2 were waited for; matrix products, arithmetic and copies ran while one was open for 0% of the time, Pallas kernels for 0%

commit v1 on v0

v1 whole, which is shorter than its diff:
```python
import functools

import jax
import jax.numpy as jnp
import numpy as np
from jax import lax
from jax.experimental import pallas as pl
from jax.experimental.pallas import tpu as pltpu
from jax.sharding import Mesh
from jax.sharding import PartitionSpec as P

NODE = ("yh", "z", "x")
HEAD = ("yl", "c")
LOW = -3.0e38


def leaky_relu(values):
    return jnp.maximum(values, 0.2 * values)


def pick_kernel(presence_ref, gathered_ref, out_ref):
    copies = out_ref.shape[0]
    slots = out_ref.shape[1]

    def visit(tile, slot):
        here = presence_ref[0, tile]

        @pl.when((here == 1) & (slot < slots))
        def _():
            rows = gathered_ref[tile]
            for i in range(copies):
                out_ref[i, slot] = rows

        return slot + here

    lax.fori_loop(0, gathered_ref.shape[0], visit, jnp.int32(0))


def attend_kernel(
    where_ref,
    presence_ref,
    own_ref,
    other_ref,
    features_ref,
    proj_ref,
    source_ref,
    target_ref,
    weight_ref,
    masks_hbm,
    out_ref,
    masks,
    values,
    weights,
    sem,
):
    slots, tile, _ = masks.shape
    groups = own_ref.shape[0]
    part = own_ref.shape[2]
    copy = pltpu.make_async_copy(masks_hbm.at[0], masks, sem)
    copy.start()
    node = where_ref[0]
    core = where_ref[1]

    def project(rows):
        return jnp.dot(rows, proj_ref[...], preferred_element_type=jnp.float32).astype(jnp.bfloat16)

    for ref, side in ((own_ref, core), (other_ref, 1 - core)):
        for group in range(groups):
            rows = project(ref[group].reshape(slots * part, tile))
            values[:, group, side] = rows.reshape(slots, part, tile)

    local = project(features_ref[...])
    local_wide = local.astype(jnp.float32)
    target_terms = jnp.sum(local_wide * target_ref[...], axis=1, keepdims=True)
    self_source = jnp.sum(local_wide * source_ref[...], axis=1, keepdims=True)

    source = source_ref[...]
    high = source.astype(jnp.bfloat16).astype(jnp.float32)
    rest = source - high
    middle = rest.astype(jnp.bfloat16).astype(jnp.float32)
    low = rest - middle
    row = lax.broadcasted_iota(jnp.int32, (16, tile), 0)
    split = jnp.where(row == 0, high, jnp.where(row == 1, middle, jnp.where(row == 2, low, 0.0)))
    projected = values[...].reshape(slots * tile, tile)
    terms = lax.dot_general(
        split.astype(jnp.bfloat16),
        projected,
        (((1,), (1,)), ((), ())),
        preferred_element_type=jnp.float32,
    )
    source_terms = terms[0:1] + terms[1:2] + terms[2:3]

    def count(i, rank):
        return rank + presence_ref[0, i]

    rank = lax.fori_loop(0, node, count, jnp.int32(0))
    copy.wait()

    @pl.when(presence_ref[0, node] == 1)
    def _():
        down = lax.broadcasted_iota(jnp.int32, (tile, tile), 0)
        across = lax.broadcasted_iota(jnp.int32, (tile, tile), 1)
        masks[rank] = jnp.where(down == across, 0, masks[rank])

    best = jnp.full((tile, tile), LOW, jnp.float32)
    for k in range(slots):
        terms_here = source_terms[:, k * tile : (k + 1) * tile]
        best = jnp.maximum(best, jnp.where(masks[k] == 1, terms_here, LOW))
    top = jnp.maximum(jnp.max(best, axis=1, keepdims=True), self_source)
    peak = leaky_relu(target_terms + top)
    self_weight = jnp.exp(leaky_relu(target_terms + self_source) - peak)

    total = jnp.zeros((tile, tile), jnp.float32)
    for k in range(slots):
        scores = leaky_relu(target_terms + source_terms[:, k * tile : (k + 1) * tile])
        edge = jnp.where(masks[k] == 1, jnp.exp(scores - peak), 0.0)
        total = total + edge
        weights[:, k * tile : (k + 1) * tile] = edge.astype(jnp.bfloat16)
    denominator = jnp.sum(total, axis=1, keepdims=True) + self_weight
    summed = jnp.dot(weights[...], projected, preferred_element_type=jnp.float32)
    summed = summed + self_weight.astype(jnp.bfloat16).astype(jnp.float32) * local_wide
    attended = summed / denominator
    below = jnp.minimum(attended, 0.0)
    half = jnp.tanh(0.5 * below)
    heads_out = jnp.where(attended > 0, attended, 2.0 * half / (1.0 - half)).astype(jnp.bfloat16)
    out_ref[...] = jnp.dot(
        heads_out, weight_ref[...], preferred_element_type=jnp.float32
    ).astype(jnp.bfloat16)


def per_device(sizes, features, proj_weight, score_source, score_target, out_weight, presence, tile_masks):
    nodes, lows, cores = sizes
    tile, width = features.shape
    slots = tile_masks.shape[1]
    part = tile // (lows * cores)
    vmem = pl.BlockSpec(memory_space=pltpu.VMEM)
    smem = pl.BlockSpec(memory_space=pltpu.SMEM)

    core = lax.axis_index("c")
    first = lax.axis_index(HEAD) * part
    mine = lax.dynamic_slice(features, (first, 0), (part, width))
    gathered = lax.all_to_all(
        jnp.broadcast_to(mine[None], (nodes, part, width)), NODE, 0, 0, tiled=True
    )
    picked = pl.pallas_call(
        pick_kernel,
        out_shape=jax.ShapeDtypeStruct((lows, slots, part, width), jnp.bfloat16),
        in_specs=[smem, vmem],
        out_specs=vmem,
        compiler_params=pltpu.CompilerParams(vmem_limit_bytes=4 << 20),
        name="pick",
    )(presence, gathered)
    own = lax.all_to_all(picked, "yl", 0, 0, tiled=True)
    swap = [(0, 1), (1, 0)]
    other = lax.ppermute(own, "c", swap)
    place = jnp.stack([lax.axis_index(NODE), core]).astype(jnp.int32)
    partial = pl.pallas_call(
        attend_kernel,
        out_shape=jax.ShapeDtypeStruct((tile, out_weight.shape[1]), jnp.bfloat16),
        in_specs=[smem, smem] + [vmem] * 7 + [pl.BlockSpec(memory_space=pl.ANY)],
        out_specs=vmem,
        scratch_shapes=[
            pltpu.VMEM((slots, tile, tile), jnp.int32),
            pltpu.VMEM((slots, lows, cores, part, width), jnp.bfloat16),
            pltpu.VMEM((tile, slots * tile), jnp.bfloat16),
            pltpu.SemaphoreType.DMA,
        ],
        compiler_params=pltpu.CompilerParams(vmem_limit_bytes=16 << 20),
        name="attend",
    )(place, presence, own, other, features, proj_weight, score_source, score_target, out_weight, tile_masks)
    paired = partial.astype(jnp.float32) + lax.ppermute(partial, "c", swap).astype(jnp.float32)
    paired = jnp.broadcast_to(paired.astype(jnp.bfloat16)[None], (lows,) + partial.shape)
    pieces = lax.all_to_all(paired, "yl", 0, 0, tiled=True)
    return jnp.sum(pieces.astype(jnp.float32), axis=0).astype(jnp.bfloat16)


def solution(mesh):
    fine = Mesh(np.asarray(mesh.devices).reshape(2, 8, 4, 4, 2), NODE + HEAD)
    return jax.shard_map(
        functools.partial(per_device, (64, 4, 2)),
        mesh=fine,
        in_specs=(
            P(NODE, None),
            P(None, HEAD),
            P(HEAD, None),
            P(HEAD, None),
            P(HEAD, None),
            P(NODE, None),
            P(NODE, None, None, None),
        ),
        out_specs=P(NODE, None),
        check_vma=False,
    )
```

time: 1030 us -> 70.4 us (0.07); the launches traced: 1010 us -> 69.7 us
  other arithmetic: 670 us -> 0.76 us
  waiting for transfers between devices: 212 us -> 1.9 us
  local copies, waits for them, and re-layouts: 104 us -> 1.53 us
  blocking collectives: 0 us -> 53.8 us
  matrix products: 14.9 us -> 0 us
  between operations: 13.5 us -> 0.14 us
    select_n x24 -> x0, other arithmetic: 654 us -> none  [the longest x8 325 us: absorb(): present_here = jnp.take(presence, column_tiles, axis=1)]
    all_gather x1 -> x0, waiting for transfers between devices: 137 us -> none  [per_device(): block_values = project(lax.all_gather(features, 'node', axis=0, tiled=True))]
    gather x64 -> x0, local copies, waits for them, and re-layouts: 95 us -> none  [the longest x8 54.3 us: absorb(): tile_masks[tile_rows[:, None], slot_here, :, column_lanes[None, :]]]
    psum x1 -> x0, waiting for transfers between devices: 73.7 us -> none  [per_device(): result = lax.psum(partial_sum.astype(jnp.bfloat16), 'head')]
    all_to_all x0 -> x3, blocking collectives: none -> 53.8 us  [the longest x1 33.4 us: per_device(): lax.all_to_all(jnp.broadcast_to(mine[None], (nodes, part, width)), NODE,...]
    dot_general x11 -> x0, matrix products: 14.9 us -> none  [the longest x8 11.6 us: absorb(): jnp.einsum('htb,bhd->htd', edge_weights.astype(jnp.bfloat16), block_value...]
where the time goes in v1:
time: 70.4 us; the launch traced here: 69.7 us
  blocking collectives  53.8 us (76%)
  starting transfers between devices  8.04 us (11%)
  Pallas kernels  3.5 us (5%)
  waiting for transfers between devices  1.9 us (3%)
  local copies, waits for them, and re-layouts  1.53 us (2%)
  other arithmetic  0.76 us (1%)
    all_to_all x1, blocking collectives, per_device(): lax.all_to_all(jnp.broadcast_to(mine[None], (nodes, part, width)), NODE,...  33.4 us
    all_to_all x1, blocking collectives, per_device(): own = lax.all_to_all(picked, 'yl', 0, 0, tiled=True)  10.7 us
    all_to_all x1, blocking collectives, per_device(): pieces = lax.all_to_all(paired, 'yl', 0, 0, tiled=True)  9.75 us
    ppermute x1, starting transfers between devices, per_device(): other = lax.ppermute(own, 'c', swap)  5.75 us
    ppermute x1, starting transfers between devices, per_device(): lax.ppermute(partial, 'c', swap).astype(jnp.float32)  2.29 us
    pallas_call x1, Pallas kernels, per_device(): pl.pallas_call(attend_kernel, out_shape=jax.ShapeDtypeStruct((tile, out_w...  2.05 us
    pallas_call x1, Pallas kernels, per_device(): pl.pallas_call(pick_kernel, out_shape=jax.ShapeDtypeStruct((lows, slots,...  1.45 us
  transfers between devices with their start and end apart: 2, of which 2 were waited for; matrix products, arithmetic and copies ran while one was open for 0% of the time, Pallas kernels for 0%

profile of v1, /device:TPU:1, one launch (start us, length us, event | category | flops | bytes accessed | tf_op | source)
XLA Modules:
  0.0 69.7 jit_solution(6099183637208276724)
XLA Ops:
  0.0 0.8 %constant_dynamic-slice_fusion = bf16[16,128]{1,0:T(8,128)(2,1)S(1)} fusion(bf16[128,128]{1,0:T(8,128)(2,1)} %features_ref.1, s32[]{:T(128)S(6)} %select_n.3), kind=kLoop, calls=%fused_computation.2 | loop fusion | bytes 8196 | tf_op jit(solution)/shard_map/dynamic_slice | solution.py:141
  0.8 33.4 %all_to_all.15.gathered_ref = bf16[64,16,128]{2,1,0:T(8,128)(2,1)S(1)} all-to-all(bf16[64,16,128]{2,1,0:T(8,128)(2,1)S(1)} %broadcast_in_dim.4), channel_id=1, replica_groups=mesh['yh'=2,'z'=8,'x'=4,'yl'=4,'c'=2] {'yh','z','x'}, dimensions={0} | all-to-all | bytes 524288 | tf_op jit(solution)/shard_map/all_to_all | solution.py:142
  34.2 0.7 copy-done.4
  34.9 1.4 %pick.1 = bf16[4,16,16,128]{3,2,1,0:T(8,128)(2,1)S(1)} custom-call(s32[1,64]{1,0:T(1,128)S(1)} %copy-done.4, bf16[64,16,128]{2,1,0:T(8,128)(2,1)S(1)} %all_to_all.15.gathered_ref), custom_call_target="tpu_custom_call" | custom-call | tf_op jit(solution)/shard_map/pick/pallas_call | solution.py:145
  36.3 0.0 copy-start.1
  36.3 0.0 copy-start.2
  36.3 0.0 copy-start.3
  36.3 10.7 %all_to_all.16.own_ref = bf16[4,16,16,128]{3,2,1,0:T(8,128)(2,1)S(1)} all-to-all(bf16[4,16,16,128]{3,2,1,0:T(8,128)(2,1)S(1)} %pick.1), channel_id=1, replica_groups=mesh['yh'=2,'z'=8,'x'=4,'yl'=4,'c'=2] {'yl'}, dimensions={0} | all-to-all | bytes 524288 | tf_op jit(solution)/shard_map/all_to_all | solution.py:153
  47.1 5.8 %collective-permute-start = (bf16[4,16,16,128]{3,2,1,0:T(8,128)(2,1)S(1)}, bf16[4,16,16,128]{3,2,1,0:T(8,128)(2,1)S(1)}, u32[]{:S(2)}, u32[]{:S(2)}) collective-permute-start(bf16[4,16,16,128]{3,2,1,0:T(8,128)(2,1)S(1)} %all_to_all.16.own_ref), channel_id=1, source_target_pairs={{0,1},{1,0},{2,3},{3,2},{4,5},{5,4},{6,7},{7,6},{8,9},{9,8},{10,11... | collective-permute-start | bytes 786440 | tf_op jit(solution)/shard_map/ppermute | solution.py:155
  52.8 0.0 copy-start.5
  52.8 0.0 copy-start.6
  52.9 0.0 copy-start.7
  52.9 0.1 pad_add_fusion.where_ref
  52.9 1.0 %collective-permute-done.other_ref = bf16[4,16,16,128]{3,2,1,0:T(8,128)(2,1)S(1)} collective-permute-done((bf16[4,16,16,128]{3,2,1,0:T(8,128)(2,1)S(1)}, bf16[4,16,16,128]{3,2,1,0:T(8,128)(2,1)S(1)}, u32[]{:S(2)}, u32[]{:S(2)}) %collective-permute-start) | collective-permute-done | bytes 262176 | tf_op jit(solution)/shard_map/ppermute | solution.py:155
  54.0 0.0 copy-done
  54.0 0.0 copy-done.1
  54.0 0.0 copy-done.2
  54.0 0.0 copy-done.3
  54.0 0.0 copy-done.5
  54.0 2.0 %attend.1 = bf16[128,256]{1,0:T(8,128)(2,1)S(1)} custom-call(s32[2]{0:T(128)S(1)} %pad_add_fusion.where_ref, s32[1,64]{1,0:T(1,128)S(1)} %copy-done.5, bf16[4,16,16,128]{3,2,1,0:T(8,128)(2,1)S(1)} %all_to_all.16.own_ref, bf16[4,16,16,128]{3,2,1,0:T(8,128)(2,1)S(1)} %collective-permute-done.other_ref, bf16[128,128]{1,0:T(8,128)(2,1)S(1)} %copy-done.2, ...), custom_call_target="tpu_custom_call" | custom-call | tf_op jit(solution)/shard_map/attend/pallas_call | solution.py:157
  56.1 2.3 %collective-permute-start.1 = (bf16[128,256]{1,0:T(8,128)(2,1)S(1)}, bf16[128,256]{1,0:T(8,128)(2,1)S(1)}, u32[]{:S(2)}, u32[]{:S(2)}) collective-permute-start(bf16[128,256]{1,0:T(8,128)(2,1)S(1)} %attend.1), channel_id=1, source_target_pairs={{0,1},{1,0},{2,3},{3,2},{4,5},{5,4},{6,7},{7,6},{8,9},{9,8},{10,11... | collective-permute-start | bytes 196616 | tf_op jit(solution)/shard_map/ppermute | solution.py:171
  58.4 0.9 %collective-permute-done.1 = bf16[128,256]{1,0:T(8,128)(2,1)S(1)} collective-permute-done((bf16[128,256]{1,0:T(8,128)(2,1)S(1)}, bf16[128,256]{1,0:T(8,128)(2,1)S(1)}, u32[]{:S(2)}, u32[]{:S(2)}) %collective-permute-start.1) | collective-permute-done | bytes 65568 | tf_op jit(solution)/shard_map/ppermute | solution.py:171
  59.3 9.8 %all_to_all.17 = bf16[4,128,256]{2,1,0:T(8,128)(2,1)S(1)} all-to-all(bf16[4,128,256]{2,1,0:T(8,128)(2,1)S(1)} %broadcast_in_dim.5), channel_id=1, replica_groups=mesh['yh'=2,'z'=8,'x'=4,'yl'=4,'c'=2] {'yl'}, dimensions={0} | all-to-all | bytes 524288 | tf_op jit(solution)/shard_map/all_to_all | solution.py:173
  69.0 0.7 reduce_sum.12
  (7 shorter events, 0.1 us)
Async XLA Ops:
  0.0 54.0 %copy-start = (s32[1,16,128,128]{3,2,1,0:T(8,128)S(1)}, s32[1,16,128,128]{3,2,1,0:T(8,128)}, u32[]{:S(2)}) copy-start(s32[1,16,128,128]{3,2,1,0:T(8,128)} %masks_hbm.1) | copy-start | bytes 3145732
  34.2 0.7 copy-start.4
  36.3 17.7 %copy-start.1 = (bf16[128,256]{1,0:T(8,128)(2,1)S(1)}, bf16[128,256]{1,0:T(8,128)(2,1)}, u32[]{:S(2)}) copy-start(bf16[128,256]{1,0:T(8,128)(2,1)} %weight_ref.1) | copy-start | bytes 196612
  36.3 17.6 %copy-start.2 = (bf16[128,128]{1,0:T(8,128)(2,1)S(1)}, bf16[128,128]{1,0:T(8,128)(2,1)}, u32[]{:S(2)}) copy-start(bf16[128,128]{1,0:T(8,128)(2,1)} %features_ref.1) | copy-start | bytes 98308
  36.3 17.6 %copy-start.3 = (bf16[128,128]{1,0:T(8,128)(2,1)S(1)}, bf16[128,128]{1,0:T(8,128)(2,1)}, u32[]{:S(2)}) copy-start(bf16[128,128]{1,0:T(8,128)(2,1)} %proj_ref.1) | copy-start | bytes 98308
  47.1 6.9 %collective-permute-start = (bf16[4,16,16,128]{3,2,1,0:T(8,128)(2,1)S(1)}, bf16[4,16,16,128]{3,2,1,0:T(8,128)(2,1)S(1)}, u32[]{:S(2)}, u32[]{:S(2)}) collective-permute-start(bf16[4,16,16,128]{3,2,1,0:T(8,128)(2,1)S(1)} %all_to_all.16.own_ref), channel_id=1, source_target_pairs={{0,1},{1,0},{2,3},{3,2},{4,5},{5,4},{6,7},{7,6},{8,9},{9,8},{10,11... | collective-permute-start | bytes 786440 | tf_op jit(solution)/shard_map/ppermute | solution.py:155
  52.8 1.1 %copy-start.5 = (s32[1,64]{1,0:T(1,128)S(1)}, s32[1,64]{1,0:T(1,128)}, u32[]{:S(2)}) copy-start(s32[1,64]{1,0:T(1,128)} %presence_ref.3) | copy-start | bytes 772
  52.8 1.1 %copy-start.6 = (f32[1,128]{1,0:T(1,128)S(1)}, f32[1,128]{1,0:T(1,128)}, u32[]{:S(2)}) copy-start(f32[1,128]{1,0:T(1,128)} %source_ref.1) | copy-start | bytes 1540
  52.9 1.1 %copy-start.7 = (f32[1,128]{1,0:T(1,128)S(1)}, f32[1,128]{1,0:T(1,128)}, u32[]{:S(2)}) copy-start(f32[1,128]{1,0:T(1,128)} %target_ref.1) | copy-start | bytes 1540
  56.1 3.2 %collective-permute-start.1 = (bf16[128,256]{1,0:T(8,128)(2,1)S(1)}, bf16[128,256]{1,0:T(8,128)(2,1)S(1)}, u32[]{:S(2)}, u32[]{:S(2)}) collective-permute-start(bf16[128,256]{1,0:T(8,128)(2,1)S(1)} %attend.1), channel_id=1, source_target_pairs={{0,1},{1,0},{2,3},{3,2},{4,5},{5,4},{6,7},{7,6},{8,9},{9,8},{10,11... | collective-permute-start | bytes 196616 | tf_op jit(solution)/shard_map/ppermute | solution.py:171

commit v2 on v1

v2 whole, which is shorter than its diff:
```python
import functools

import jax
import jax.numpy as jnp
import numpy as np
from jax import lax
from jax.experimental import pallas as pl
from jax.experimental.pallas import tpu as pltpu
from jax.sharding import Mesh
from jax.sharding import PartitionSpec as P

NODE = ("yh", "z", "x")
HEAD = ("yl", "c")
EVERY = NODE + ("yl",)
SIZES = {"yh": 2, "z": 8, "x": 4, "yl": 4, "c": 2}
NODES = 64
QUARTERS = 4
LOW = -1.0e38


def node_groups():
    groups = []
    for pair in range(SIZES["yl"]):
        group = []
        for yh in range(SIZES["yh"]):
            for z in range(SIZES["z"]):
                for x in range(SIZES["x"]):
                    place = (yh * SIZES["z"] + z) * SIZES["x"] + x
                    group.append(place * SIZES["yl"] + (pair ^ (2 * yh)))
        groups.append(group)
    return groups


def leaky_relu(values):
    return jnp.maximum(values, 0.2 * values)


def prepare_kernel(features_hbm, presence_hbm, send_ref, presence_ref, rows_ref, sems):
    part = rows_ref.shape[0]
    start = (lax.rem(lax.axis_index("yl"), 2) * 2 + lax.axis_index("c")) * part
    rows_copy = pltpu.make_async_copy(
        features_hbm.at[pl.ds(pl.multiple_of(start, part), part)], rows_ref, sems.at[0]
    )
    presence_copy = pltpu.make_async_copy(presence_hbm, presence_ref, sems.at[1])
    rows_copy.start()
    presence_copy.start()
    rows_copy.wait()
    rows = rows_ref[...]
    for i in range(send_ref.shape[0]):
        send_ref[i] = rows
    presence_copy.wait()


def pick_kernel(presence_ref, gathered_ref, out_ref, slots_ref):
    slot = jnp.int32(0)
    for tile in range(gathered_ref.shape[0]):
        slots_ref[slot] = gathered_ref[tile]
        slot = jnp.minimum(slot + presence_ref[0, tile], out_ref.shape[0])
    for i in range(out_ref.shape[0]):
        out_ref[i] = slots_ref[i]


def attend_kernel(
    presence_ref,
    own_ref,
    beside_ref,
    twin_ref,
    across_ref,
    features_ref,
    proj_ref,
    source_ref,
    target_ref,
    weight_ref,
    masks_ref,
    out_ref,
    values,
    masked,
    weights,
):
    slots, tile, _ = masked.shape
    part = own_ref.shape[1]
    node = (lax.axis_index("yh") * SIZES["z"] + lax.axis_index("z")) * SIZES["x"] + lax.axis_index("x")
    half = lax.rem(lax.axis_index("yl"), 2)
    core = lax.axis_index("c")

    def project(rows):
        return jnp.dot(rows, proj_ref[...], preferred_element_type=jnp.float32).astype(jnp.bfloat16)

    for ref, place, side in (
        (own_ref, half, core),
        (beside_ref, 1 - half, core),
        (twin_ref, half, 1 - core),
        (across_ref, 1 - half, 1 - core),
    ):
        rows = project(ref[...].reshape(slots * part, tile))
        values[:, place, side] = rows.reshape(slots, part, tile)

    local = project(features_ref[...])
    local_wide = local.astype(jnp.float32)
    target_terms = jnp.sum(local_wide * target_ref[...], axis=1, keepdims=True)
    self_source = jnp.sum(local_wide * source_ref[...], axis=1, keepdims=True)

    source = source_ref[...]
    high = source.astype(jnp.bfloat16).astype(jnp.float32)
    rest = source - high
    middle = rest.astype(jnp.bfloat16).astype(jnp.float32)
    low = rest - middle
    row = lax.broadcasted_iota(jnp.int32, (16, tile), 0)
    split = jnp.where(row == 0, high, jnp.where(row == 1, middle, jnp.where(row == 2, low, 0.0)))
    projected = values[...].reshape(slots * tile, tile)
    terms = lax.dot_general(
        split.astype(jnp.bfloat16),
        projected,
        (((1,), (1,)), ((), ())),
        preferred_element_type=jnp.float32,
    )
    source_terms = terms[0:1] + terms[1:2] + terms[2:3]

    best = jnp.full((tile, tile), LOW, jnp.float32)
    for k in range(slots):
        terms_here = source_terms[:, k * tile : (k + 1) * tile]
        linked = jnp.where(masks_ref[0, k] == 1, terms_here, LOW)
        masked[k] = linked
        best = jnp.maximum(best, linked)
    top = jnp.maximum(jnp.max(best, axis=1, keepdims=True), self_source)
    peak = leaky_relu(target_terms + top)
    self_weight = jnp.exp(leaky_relu(target_terms + self_source) - peak)

    def count(i, rank):
        return rank + presence_ref[0, i]

    rank = lax.fori_loop(0, node, count, jnp.int32(0))

    @pl.when(presence_ref[0, node] == 1)
    def _():
        down = lax.broadcasted_iota(jnp.int32, (tile, tile), 0)
        over = lax.broadcasted_iota(jnp.int32, (tile, tile), 1)
        masked[rank] = jnp.where(down == over, LOW, masked[rank])

    total = jnp.zeros((tile, tile), jnp.float32)
    for k in range(slots):
        edge = jnp.exp(leaky_relu(target_terms + masked[k]) - peak)
        total = total + edge
        weights[:, k * tile : (k + 1) * tile] = edge.astype(jnp.bfloat16)
    denominator = jnp.sum(total, axis=1, keepdims=True) + self_weight
    summed = jnp.dot(weights[...], projected, preferred_element_type=jnp.float32)
    summed = summed + self_weight.astype(jnp.bfloat16).astype(jnp.float32) * local_wide
    attended = summed / denominator
    below = jnp.minimum(attended, 0.0)
    bent = jnp.tanh(0.5 * below)
    heads_out = jnp.where(attended > 0, attended, 2.0 * bent / (1.0 - bent)).astype(jnp.bfloat16)
    out_ref[...] = jnp.dot(
        heads_out, weight_ref[...], preferred_element_type=jnp.float32
    ).astype(jnp.bfloat16)


def per_device(features, proj_weight, score_source, score_target, out_weight, presence, tile_masks):
    tile, width = features.shape
    slots = tile_masks.shape[1]
    part = tile // QUARTERS
    vmem = pl.BlockSpec(memory_space=pltpu.VMEM)
    smem = pl.BlockSpec(memory_space=pltpu.SMEM)
    raw = pl.BlockSpec(memory_space=pltpu.HBM)

    send, presence = pl.pallas_call(
        prepare_kernel,
        out_shape=(
            jax.ShapeDtypeStruct((NODES, part, width), jnp.bfloat16),
            jax.ShapeDtypeStruct(presence.shape, jnp.int32),
        ),
        in_specs=[raw, raw],
        out_specs=(vmem, vmem),
        scratch_shapes=[pltpu.VMEM((part, width), jnp.bfloat16), pltpu.SemaphoreType.DMA((2,))],
        compiler_params=pltpu.CompilerParams(vmem_limit_bytes=4 << 20),
        name="prepare",
    )(features, presence)
    gathered = lax.all_to_all(
        send, EVERY, 0, 0, tiled=True, axis_index_groups=node_groups()
    )
    own = pl.pallas_call(
        pick_kernel,
        out_shape=jax.ShapeDtypeStruct((slots, part, width), jnp.bfloat16),
        in_specs=[smem, vmem],
        out_specs=vmem,
        scratch_shapes=[pltpu.VMEM((slots + 1, part, width), jnp.bfloat16)],
        compiler_params=pltpu.CompilerParams(vmem_limit_bytes=4 << 20),
        name="pick",
    )(presence, gathered)
    swap = [(0, 1), (1, 0)]
    beside = lax.ppermute(own, "yl", [(i, i ^ 1) for i in range(SIZES["yl"])])
    twin = lax.ppermute(own, "c", swap)
    across = lax.ppermute(beside, "c", swap)
    partial = pl.pallas_call(
        attend_kernel,
        out_shape=jax.ShapeDtypeStruct((tile, out_weight.shape[1]), jnp.bfloat16),
        in_specs=[smem] + [vmem] * 10,
        out_specs=vmem,
        scratch_shapes=[
            pltpu.VMEM((slots, 2, 2, part, width), jnp.bfloat16),
            pltpu.VMEM((slots, tile, tile), jnp.float32),
            pltpu.VMEM((tile, slots * tile), jnp.bfloat16),
        ],
        compiler_params=pltpu.CompilerParams(vmem_limit_bytes=16 << 20),
        name="attend",
    )(
        presence, own, beside, twin, across, features,
        proj_weight, score_source, score_target, out_weight, tile_masks,
    )
    paired = partial.astype(jnp.float32) + lax.ppermute(partial, "c", swap).astype(jnp.float32)
    lows = SIZES["yl"]
    paired = jnp.broadcast_to(paired.astype(jnp.bfloat16)[None], (lows,) + partial.shape)
    pieces = lax.all_to_all(paired, "yl", 0, 0, tiled=True)
    return jnp.sum(pieces.astype(jnp.float32), axis=0).astype(jnp.bfloat16)


def solution(mesh):
    shape = tuple(SIZES[name] for name in NODE + HEAD)
    fine = Mesh(np.asarray(mesh.devices).reshape(shape), NODE + HEAD)
    return jax.shard_map(
        per_device,
        mesh=fine,
        in_specs=(
            P(NODE, None),
            P(None, HEAD),
            P(HEAD, None),
            P(HEAD, None),
            P(HEAD, None),
            P(NODE, None),
            P(NODE, None, None, None),
        ),
        out_specs=P(NODE, None),
        check_vma=False,
    )
```

time: 70.4 us -> 68.9 us (0.979)
  the two profiles are of different devices: /device:TPU:1 before, /device:TPU:6 now
where the time goes in v2:
time: 68.9 us; the launch traced here: 68.6 us
  blocking collectives  47 us (68%)
  starting transfers between devices  13.2 us (19%)
  waiting for transfers between devices  3.4 us (5%)
  Pallas kernels  2.66 us (4%)
  local copies, waits for them, and re-layouts  1.54 us (2%)
  other arithmetic  0.69 us (1%)
    all_to_all x1, blocking collectives, per_device(): lax.all_to_all(send, EVERY, 0, 0, tiled=True, axis_index_groups=node_grou...  33.2 us
    all_to_all x1, blocking collectives, per_device(): pieces = lax.all_to_all(paired, 'yl', 0, 0, tiled=True)  13.8 us
    ppermute x1, starting transfers between devices, per_device(): beside = lax.ppermute(own, 'yl', [(i, i ^ 1) for i in range(SIZES['yl'])])  7.29 us
    ppermute x1, starting transfers between devices, per_device(): lax.ppermute(partial, 'c', swap).astype(jnp.float32)  2.05 us
    ppermute x1, starting transfers between devices, per_device(): twin = lax.ppermute(own, 'c', swap)  1.92 us
    ppermute x1, starting transfers between devices, per_device(): across = lax.ppermute(beside, 'c', swap)  1.91 us
    pallas_call x1, Pallas kernels, per_device(): pl.pallas_call(attend_kernel, out_shape=jax.ShapeDtypeStruct((tile, out_w...  1.88 us
    unnamed x16, local copies, waits for them, and re-layouts  1.53 us
  transfers between devices with their start and end apart: 4, of which 3 were waited for; matrix products, arithmetic and copies ran while one was open for 0% of the time, Pallas kernels for 0%

profile of v2, /device:TPU:6, one launch (start us, length us, event | category | flops | bytes accessed | tf_op | source)
XLA Modules:
  0.0 68.6 jit_solution(694341101609896104)
XLA Ops:
  0.0 0.0 copy-start
  0.0 0.8 %copy-done.1 = bf16[128,128]{1,0:T(8,128)(2,1)S(1)} copy-done((bf16[128,128]{1,0:T(8,128)(2,1)S(1)}, bf16[128,128]{1,0:T(8,128)(2,1)}, u32[]{:S(2)}) %copy-start.1) | copy-done | bytes 32792
  0.9 0.7 copy-done.5
  1.5 0.1 prepare.1
  1.6 33.2 %all_to_all.10.gathered_ref = bf16[64,32,128]{2,1,0:T(8,128)(2,1)S(1)} all-to-all(bf16[64,32,128]{2,1,0:T(8,128)(2,1)S(1)} %get-tuple-element.8), channel_id=1, replica_groups={{0,8,16,24,32,40,48,56,64,72,80,88,96,104,112,120,128,136,144,152,160,1..., dimensions={0} | all-to-all | bytes 1048576 | tf_op jit(solution)/shard_map/all_to_all | solution.py:177
  34.8 0.0 copy-start.7
  34.8 0.7 %pick.1.own_ref = bf16[16,32,128]{2,1,0:T(8,128)(2,1)S(1)} custom-call(s32[1,64]{1,0:T(1,128)S(1)} %get-tuple-element.7.presence_ref, bf16[64,32,128]{2,1,0:T(8,128)(2,1)S(1)} %all_to_all.10.gathered_ref), custom_call_target="tpu_custom_call" | custom-call | tf_op jit(solution)/shard_map/pick/pallas_call | solution.py:180
  35.5 7.3 %collective-permute-start = (bf16[16,32,128]{2,1,0:T(8,128)(2,1)S(1)}, bf16[16,32,128]{2,1,0:T(8,128)(2,1)S(1)}, u32[]{:S(2)}, u32[]{:S(2)}) collective-permute-start(bf16[16,32,128]{2,1,0:T(8,128)(2,1)S(1)} %pick.1.own_ref), channel_id=1, source_target_pairs={{0,2},{2,0},{4,6},{6,4},{1,3},{3,1},{5,7},{7,5},{8,10},{10,8},{12,... | collective-permute-start | bytes 393224 | tf_op jit(solution)/shard_map/ppermute | solution.py:190
  42.8 1.9 %collective-permute-start.1 = (bf16[16,32,128]{2,1,0:T(8,128)(2,1)S(1)}, bf16[16,32,128]{2,1,0:T(8,128)(2,1)S(1)}, u32[]{:S(2)}, u32[]{:S(2)}) collective-permute-start(bf16[16,32,128]{2,1,0:T(8,128)(2,1)S(1)} %pick.1.own_ref), channel_id=1, source_target_pairs={{0,1},{1,0},{2,3},{3,2},{4,5},{5,4},{6,7},{7,6},{8,9},{9,8},{10,11... | collective-permute-start | bytes 393224 | tf_op jit(solution)/shard_map/ppermute | solution.py:191
  44.7 1.0 %collective-permute-done.beside_ref = bf16[16,32,128]{2,1,0:T(8,128)(2,1)S(1)} collective-permute-done((bf16[16,32,128]{2,1,0:T(8,128)(2,1)S(1)}, bf16[16,32,128]{2,1,0:T(8,128)(2,1)S(1)}, u32[]{:S(2)}, u32[]{:S(2)}) %collective-permute-start) | collective-permute-done | bytes 131104 | tf_op jit(solution)/shard_map/ppermute | solution.py:190
  45.7 1.9 %collective-permute-start.2 = (bf16[16,32,128]{2,1,0:T(8,128)(2,1)S(1)}, bf16[16,32,128]{2,1,0:T(8,128)(2,1)S(1)}, u32[]{:S(2)}, u32[]{:S(2)}) collective-permute-start(bf16[16,32,128]{2,1,0:T(8,128)(2,1)S(1)} %collective-permute-done.beside_ref), channel_id=1, source_target_pairs={{0,1},{1,0},{2,3},{3,2},{4,5},{5,4},{6,7},{7,6},{8,9},{9,8},{10,11... | collective-permute-start | bytes 393224 | tf_op jit(solution)/shard_map/ppermute | solution.py:192
  47.6 0.0 collective-permute-done.1.twin_ref
  47.7 1.3 %collective-permute-done.2.across_ref = bf16[16,32,128]{2,1,0:T(8,128)(2,1)S(1)} collective-permute-done((bf16[16,32,128]{2,1,0:T(8,128)(2,1)S(1)}, bf16[16,32,128]{2,1,0:T(8,128)(2,1)S(1)}, u32[]{:S(2)}, u32[]{:S(2)}) %collective-permute-start.2) | collective-permute-done | bytes 131104 | tf_op jit(solution)/shard_map/ppermute | solution.py:192
  49.0 0.0 copy-done
  49.0 0.0 copy-done.2
  49.0 0.0 copy-done.3
  49.0 0.0 copy-done.4
  49.0 0.0 copy-done.6
  49.0 0.0 copy-done.7
  49.0 1.9 %attend.1 = bf16[128,256]{1,0:T(8,128)(2,1)S(1)} custom-call(s32[1,64]{1,0:T(1,128)S(1)} %get-tuple-element.7.presence_ref, bf16[16,32,128]{2,1,0:T(8,128)(2,1)S(1)} %pick.1.own_ref, bf16[16,32,128]{2,1,0:T(8,128)(2,1)S(1)} %collective-permute-done.beside_ref, bf16[16,32,128]{2,1,0:T(8,128)(2,1)S(1)} %collective-permute-done.1.twin_ref, ...), custom_call_target="tpu_custom_call" | custom-call | tf_op jit(solution)/shard_map/attend/pallas_call | solution.py:193
  50.9 2.0 %collective-permute-start.3 = (bf16[128,256]{1,0:T(8,128)(2,1)S(1)}, bf16[128,256]{1,0:T(8,128)(2,1)S(1)}, u32[]{:S(2)}, u32[]{:S(2)}) collective-permute-start(bf16[128,256]{1,0:T(8,128)(2,1)S(1)} %attend.1), channel_id=1, source_target_pairs={{0,1},{1,0},{2,3},{3,2},{4,5},{5,4},{6,7},{7,6},{8,9},{9,8},{10,11... | collective-permute-start | bytes 196616 | tf_op jit(solution)/shard_map/ppermute | solution.py:209
  52.9 1.1 %collective-permute-done.3 = bf16[128,256]{1,0:T(8,128)(2,1)S(1)} collective-permute-done((bf16[128,256]{1,0:T(8,128)(2,1)S(1)}, bf16[128,256]{1,0:T(8,128)(2,1)S(1)}, u32[]{:S(2)}, u32[]{:S(2)}) %collective-permute-start.3) | collective-permute-done | bytes 65568 | tf_op jit(solution)/shard_map/ppermute | solution.py:209
  54.1 13.8 %all_to_all.11 = bf16[4,128,256]{2,1,0:T(8,128)(2,1)S(1)} all-to-all(bf16[4,128,256]{2,1,0:T(8,128)(2,1)S(1)} %broadcast_in_dim.2), channel_id=1, replica_groups=mesh['yh'=2,'z'=8,'x'=4,'yl'=4,'c'=2] {'yl'}, dimensions={0} | all-to-all | bytes 524288 | tf_op jit(solution)/shard_map/all_to_all | solution.py:212
  67.9 0.7 reduce_sum.12
  (8 shorter events, 0.0 us)
Async XLA Ops:
  0.0 49.0 %copy-start = (s32[1,16,128,128]{3,2,1,0:T(8,128)S(1)}, s32[1,16,128,128]{3,2,1,0:T(8,128)}, u32[]{:S(2)}) copy-start(s32[1,16,128,128]{3,2,1,0:T(8,128)} %masks_ref.1) | copy-start | bytes 3145732
  0.0 0.8 %copy-start.1 = (bf16[128,128]{1,0:T(8,128)(2,1)S(1)}, bf16[128,128]{1,0:T(8,128)(2,1)}, u32[]{:S(2)}) copy-start(bf16[128,128]{1,0:T(8,128)(2,1)} %features_ref.1) | copy-start | bytes 98308
  0.8 0.7 copy-start.5
  34.8 14.2 %copy-start.2 = (bf16[128,128]{1,0:T(8,128)(2,1)S(1)}, bf16[128,128]{1,0:T(8,128)(2,1)}, u32[]{:S(2)}) copy-start(bf16[128,128]{1,0:T(8,128)(2,1)} %features_ref.1) | copy-start | bytes 98308
  34.8 14.2 %copy-start.3 = (bf16[128,256]{1,0:T(8,128)(2,1)S(1)}, bf16[128,256]{1,0:T(8,128)(2,1)}, u32[]{:S(2)}) copy-start(bf16[128,256]{1,0:T(8,128)(2,1)} %weight_ref.1) | copy-start | bytes 196612
  34.8 14.2 %copy-start.4 = (bf16[128,128]{1,0:T(8,128)(2,1)S(1)}, bf16[128,128]{1,0:T(8,128)(2,1)}, u32[]{:S(2)}) copy-start(bf16[128,128]{1,0:T(8,128)(2,1)} %proj_ref.1) | copy-start | bytes 98308
  34.8 14.2 %copy-start.6 = (f32[1,128]{1,0:T(1,128)S(1)}, f32[1,128]{1,0:T(1,128)}, u32[]{:S(2)}) copy-start(f32[1,128]{1,0:T(1,128)} %source_ref.1) | copy-start | bytes 1540
  34.8 14.2 %copy-start.7 = (f32[1,128]{1,0:T(1,128)S(1)}, f32[1,128]{1,0:T(1,128)}, u32[]{:S(2)}) copy-start(f32[1,128]{1,0:T(1,128)} %target_ref.1) | copy-start | bytes 1540
  35.5 10.2 %collective-permute-start = (bf16[16,32,128]{2,1,0:T(8,128)(2,1)S(1)}, bf16[16,32,128]{2,1,0:T(8,128)(2,1)S(1)}, u32[]{:S(2)}, u32[]{:S(2)}) collective-permute-start(bf16[16,32,128]{2,1,0:T(8,128)(2,1)S(1)} %pick.1.own_ref), channel_id=1, source_target_pairs={{0,2},{2,0},{4,6},{6,4},{1,3},{3,1},{5,7},{7,5},{8,10},{10,8},{12,... | collective-permute-start | bytes 393224 | tf_op jit(solution)/shard_map/ppermute | solution.py:190
  42.8 4.9 %collective-permute-start.1 = (bf16[16,32,128]{2,1,0:T(8,128)(2,1)S(1)}, bf16[16,32,128]{2,1,0:T(8,128)(2,1)S(1)}, u32[]{:S(2)}, u32[]{:S(2)}) collective-permute-start(bf16[16,32,128]{2,1,0:T(8,128)(2,1)S(1)} %pick.1.own_ref), channel_id=1, source_target_pairs={{0,1},{1,0},{2,3},{3,2},{4,5},{5,4},{6,7},{7,6},{8,9},{9,8},{10,11... | collective-permute-start | bytes 393224 | tf_op jit(solution)/shard_map/ppermute | solution.py:191
  45.7 3.2 %collective-permute-start.2 = (bf16[16,32,128]{2,1,0:T(8,128)(2,1)S(1)}, bf16[16,32,128]{2,1,0:T(8,128)(2,1)S(1)}, u32[]{:S(2)}, u32[]{:S(2)}) collective-permute-start(bf16[16,32,128]{2,1,0:T(8,128)(2,1)S(1)} %collective-permute-done.beside_ref), channel_id=1, source_target_pairs={{0,1},{1,0},{2,3},{3,2},{4,5},{5,4},{6,7},{7,6},{8,9},{9,8},{10,11... | collective-permute-start | bytes 393224 | tf_op jit(solution)/shard_map/ppermute | solution.py:192
  50.9 3.1 %collective-permute-start.3 = (bf16[128,256]{1,0:T(8,128)(2,1)S(1)}, bf16[128,256]{1,0:T(8,128)(2,1)S(1)}, u32[]{:S(2)}, u32[]{:S(2)}) collective-permute-start(bf16[128,256]{1,0:T(8,128)(2,1)S(1)} %attend.1), channel_id=1, source_target_pairs={{0,1},{1,0},{2,3},{3,2},{4,5},{5,4},{6,7},{7,6},{8,9},{9,8},{10,11... | collective-permute-start | bytes 196616 | tf_op jit(solution)/shard_map/ppermute | solution.py:209

commit v3 on v2

--- a/solution.py
+++ b/solution.py
@@ -14,7 +14,7 @@
 EVERY = NODE + ("yl",)
 SIZES = {"yh": 2, "z": 8, "x": 4, "yl": 4, "c": 2}
 NODES = 64
-QUARTERS = 4
+EIGHTHS = 8
 LOW = -1.0e38
 
 
@@ -31,13 +31,21 @@
     return groups
 
 
+def pair_of_device():
+    return lax.axis_index("yl") ^ (2 * lax.axis_index("yh"))
+
+
+def toward(flip):
+    return [(i, i ^ flip) for i in range(SIZES["yl"])]
+
+
 def leaky_relu(values):
     return jnp.maximum(values, 0.2 * values)
 
 
 def prepare_kernel(features_hbm, presence_hbm, send_ref, presence_ref, rows_ref, sems):
     part = rows_ref.shape[0]
-    start = (lax.rem(lax.axis_index("yl"), 2) * 2 + lax.axis_index("c")) * part
+    start = (pair_of_device() * SIZES["c"] + lax.axis_index("c")) * part
     rows_copy = pltpu.make_async_copy(
         features_hbm.at[pl.ds(pl.multiple_of(start, part), part)], rows_ref, sems.at[0]
     )
@@ -62,10 +70,9 @@
 
 def attend_kernel(
     presence_ref,
-    own_ref,
-    beside_ref,
-    twin_ref,
-    across_ref,
+    first_ref,
+    second_ref,
+    other_ref,
     features_ref,
     proj_ref,
     source_ref,
@@ -78,22 +85,19 @@
     weights,
 ):
     slots, tile, _ = masked.shape
-    part = own_ref.shape[1]
+    part = first_ref.shape[2]
     node = (lax.axis_index("yh") * SIZES["z"] + lax.axis_index("z")) * SIZES["x"] + lax.axis_index("x")
-    half = lax.rem(lax.axis_index("yl"), 2)
+    pair = pair_of_device()
     core = lax.axis_index("c")
 
     def project(rows):
         return jnp.dot(rows, proj_ref[...], preferred_element_type=jnp.float32).astype(jnp.bfloat16)
 
-    for ref, place, side in (
-        (own_ref, half, core),
-        (beside_ref, 1 - half, core),
-        (twin_ref, half, 1 - core),
-        (across_ref, 1 - half, 1 - core),
-    ):
-        rows = project(ref[...].reshape(slots * part, tile))
-        values[:, place, side] = rows.reshape(slots, part, tile)
+    for i, flip in enumerate((0, 2, 1, 3)):
+        mine = (first_ref if i < 2 else second_ref)[i % 2]
+        for rows, side in ((mine, core), (other_ref[i], 1 - core)):
+            rows = project(rows.reshape(slots * part, tile))
+            values[:, pair ^ flip, side] = rows.reshape(slots, part, tile)
 
     local = project(features_ref[...])
     local_wide = local.astype(jnp.float32)
@@ -157,11 +161,13 @@
 def per_device(features, proj_weight, score_source, score_target, out_weight, presence, tile_masks):
     tile, width = features.shape
     slots = tile_masks.shape[1]
-    part = tile // QUARTERS
+    part = tile // EIGHTHS
     vmem = pl.BlockSpec(memory_space=pltpu.VMEM)
     smem = pl.BlockSpec(memory_space=pltpu.SMEM)
     raw = pl.BlockSpec(memory_space=pltpu.HBM)
 
+    features_far = pltpu.with_memory_space_constraint(features, pltpu.HBM)
+    presence_far = pltpu.with_memory_space_constraint(presence, pltpu.HBM)
     send, presence = pl.pallas_call(
         prepare_kernel,
         out_shape=(
@@ -173,7 +179,7 @@
         scratch_shapes=[pltpu.VMEM((part, width), jnp.bfloat16), pltpu.SemaphoreType.DMA((2,))],
         compiler_params=pltpu.CompilerParams(vmem_limit_bytes=4 << 20),
         name="prepare",
-    )(features, presence)
+    )(features_far, presence_far)
     gathered = lax.all_to_all(
         send, EVERY, 0, 0, tiled=True, axis_index_groups=node_groups()
     )
@@ -187,30 +193,29 @@
         name="pick",
     )(presence, gathered)
     swap = [(0, 1), (1, 0)]
-    beside = lax.ppermute(own, "yl", [(i, i ^ 1) for i in range(SIZES["yl"])])
-    twin = lax.ppermute(own, "c", swap)
-    across = lax.ppermute(beside, "c", swap)
+    first = jnp.stack([own, lax.ppermute(own, "yl", toward(2))])
+    second = lax.ppermute(first, "yl", toward(1))
+    other = lax.ppermute(jnp.concatenate([first, second]), "c", swap)
     partial = pl.pallas_call(
         attend_kernel,
         out_shape=jax.ShapeDtypeStruct((tile, out_weight.shape[1]), jnp.bfloat16),
-        in_specs=[smem] + [vmem] * 10,
+        in_specs=[smem] + [vmem] * 9,
         out_specs=vmem,
         scratch_shapes=[
-            pltpu.VMEM((slots, 2, 2, part, width), jnp.bfloat16),
+            pltpu.VMEM((slots, SIZES["yl"], SIZES["c"], part, width), jnp.bfloat16),
             pltpu.VMEM((slots, tile, tile), jnp.float32),
             pltpu.VMEM((tile, slots * tile), jnp.bfloat16),
         ],
         compiler_params=pltpu.CompilerParams(vmem_limit_bytes=16 << 20),
         name="attend",
     )(
-        presence, own, beside, twin, across, features,
+        presence, first, second, other, features,
         proj_weight, score_source, score_target, out_weight, tile_masks,
     )
-    paired = partial.astype(jnp.float32) + lax.ppermute(partial, "c", swap).astype(jnp.float32)
-    lows = SIZES["yl"]
-    paired = jnp.broadcast_to(paired.astype(jnp.bfloat16)[None], (lows,) + partial.shape)
-    pieces = lax.all_to_all(paired, "yl", 0, 0, tiled=True)
-    return jnp.sum(pieces.astype(jnp.float32), axis=0).astype(jnp.bfloat16)
+    for axis, perm in (("c", swap), ("yl", toward(1)), ("yl", toward(2))):
+        moved = lax.ppermute(partial, axis, perm)
+        partial = (partial.astype(jnp.float32) + moved.astype(jnp.float32)).astype(jnp.bfloat16)
+    return partial
 
 
 def solution(mesh):

time: 68.9 us -> 70.8 us (1.028)
  the two profiles are of different devices: /device:TPU:6 before, /device:TPU:1 now
where the time goes in v3:
time: 70.8 us; the launch traced here: 69.5 us
  blocking collectives  30 us (42%)
  starting transfers between devices  23.8 us (34%)
  waiting for transfers between devices  11.5 us (16%)
  Pallas kernels  3.39 us (5%)
  other arithmetic  0.73 us (1%)
    all_to_all x1, blocking collectives, per_device(): lax.all_to_all(send, EVERY, 0, 0, tiled=True, axis_index_groups=node_grou...  30 us
    ppermute x3, starting transfers between devices, per_device(): moved = lax.ppermute(partial, axis, perm)  9.81 us
    ppermute x1, starting transfers between devices, per_device(): first = jnp.stack([own, lax.ppermute(own, 'yl', toward(2))])  6.98 us
    ppermute x1, starting transfers between devices, per_device(): other = lax.ppermute(jnp.concatenate([first, second]), 'c', swap)  4.91 us
    ppermute x3, waiting for transfers between devices, per_device(): moved = lax.ppermute(partial, axis, perm)  4.82 us
    ppermute x1, waiting for transfers between devices, per_device(): second = lax.ppermute(first, 'yl', toward(1))  3.78 us
    ppermute x1, starting transfers between devices, per_device(): second = lax.ppermute(first, 'yl', toward(1))  2.05 us
    pallas_call x1, Pallas kernels, per_device(): pl.pallas_call(attend_kernel, out_shape=jax.ShapeDtypeStruct((tile, out_w...  1.88 us
  transfers between devices with their start and end apart: 6, of which 6 were waited for; matrix products, arithmetic and copies ran while one was open for 0% of the time, Pallas kernels for 0%

profile of v3, /device:TPU:1, one launch (start us, length us, event | category | flops | bytes accessed | tf_op | source)
XLA Modules:
  0.0 69.5 jit_solution(13171177617156197419)
XLA Ops:
  0.0 0.8 %prepare.1 = (bf16[64,16,128]{2,1,0:T(8,128)(2,1)S(1)}, s32[1,64]{1,0:T(1,128)S(1)}) custom-call(bf16[128,128]{1,0:T(8,128)(2,1)} %features_ref.1, s32[1,64]{1,0:T(1,128)} %presence_hbm.1), custom_call_target="tpu_custom_call" | custom-call | tf_op jit(solution)/shard_map/prepare/pallas_call | solution.py:171
  0.8 30.0 %all_to_all.5.gathered_ref = bf16[64,16,128]{2,1,0:T(8,128)(2,1)S(1)} all-to-all(bf16[64,16,128]{2,1,0:T(8,128)(2,1)S(1)} %get-tuple-element.8), channel_id=1, replica_groups={{0,8,16,24,32,40,48,56,64,72,80,88,96,104,112,120,128,136,144,152,160,1..., dimensions={0} | all-to-all | bytes 524288 | tf_op jit(solution)/shard_map/all_to_all | solution.py:183
  30.8 0.7 pick.1
  31.5 7.0 %collective-permute-start = (bf16[16,16,128]{2,1,0:T(8,128)(2,1)S(1)}, bf16[16,16,128]{2,1,0:T(8,128)(2,1)S(1)}, u32[]{:S(2)}, u32[]{:S(2)}) collective-permute-start(bf16[16,16,128]{2,1,0:T(8,128)(2,1)S(1)} %pick.1), channel_id=1, source_target_pairs={{0,4},{2,6},{4,0},{6,2},{1,5},{3,7},{5,1},{7,3},{8,12},{10,14},{12... | collective-permute-start | bytes 196616 | tf_op jit(solution)/shard_map/ppermute | solution.py:196
  38.5 1.8 %collective-permute-done = bf16[16,16,128]{2,1,0:T(8,128)(2,1)S(1)} collective-permute-done((bf16[16,16,128]{2,1,0:T(8,128)(2,1)S(1)}, bf16[16,16,128]{2,1,0:T(8,128)(2,1)S(1)}, u32[]{:S(2)}, u32[]{:S(2)}) %collective-permute-start) | collective-permute-done | bytes 65568 | tf_op jit(solution)/shard_map/ppermute | solution.py:196
  40.3 0.0 copy-start.1
  40.3 0.0 copy-start.2
  40.3 0.0 copy-start.3
  40.3 0.0 copy-start.4
  40.3 0.0 copy-start.5
  40.3 2.1 %collective-permute-start.1 = (bf16[2,16,16,128]{3,2,1,0:T(8,128)(2,1)S(1)}, bf16[2,16,16,128]{3,2,1,0:T(8,128)(2,1)S(1)}, u32[]{:S(2)}, u32[]{:S(2)}) collective-permute-start(bf16[2,16,16,128]{3,2,1,0:T(8,128)(2,1)S(1)} %pad_maximum_fusion.1.first_ref), channel_id=1, source_target_pairs={{0,2},{2,0},{4,6},{6,4},{1,3},{3,1},{5,7},{7,5},{8,10},{10,8},{12,... | collective-permute-start | bytes 393224 | tf_op jit(solution)/shard_map/ppermute | solution.py:197
  42.4 3.8 %collective-permute-done.1.second_ref = bf16[2,16,16,128]{3,2,1,0:T(8,128)(2,1)S(1)} collective-permute-done((bf16[2,16,16,128]{3,2,1,0:T(8,128)(2,1)S(1)}, bf16[2,16,16,128]{3,2,1,0:T(8,128)(2,1)S(1)}, u32[]{:S(2)}, u32[]{:S(2)}) %collective-permute-start.1) | collective-permute-done | bytes 131104 | tf_op jit(solution)/shard_map/ppermute | solution.py:197
  46.2 4.9 %collective-permute-start.2 = (bf16[4,16,16,128]{3,2,1,0:T(8,128)(2,1)S(1)}, bf16[4,16,16,128]{3,2,1,0:T(8,128)(2,1)S(1)}, u32[]{:S(2)}, u32[]{:S(2)}) collective-permute-start(bf16[4,16,16,128]{3,2,1,0:T(8,128)(2,1)S(1)} %pad_maximum_fusion), channel_id=1, source_target_pairs={{0,1},{1,0},{2,3},{3,2},{4,5},{5,4},{6,7},{7,6},{8,9},{9,8},{10,11... | collective-permute-start | bytes 786440 | tf_op jit(solution)/shard_map/ppermute | solution.py:198
  51.1 1.1 %collective-permute-done.2.other_ref = bf16[4,16,16,128]{3,2,1,0:T(8,128)(2,1)S(1)} collective-permute-done((bf16[4,16,16,128]{3,2,1,0:T(8,128)(2,1)S(1)}, bf16[4,16,16,128]{3,2,1,0:T(8,128)(2,1)S(1)}, u32[]{:S(2)}, u32[]{:S(2)}) %collective-permute-start.2) | collective-permute-done | bytes 262176 | tf_op jit(solution)/shard_map/ppermute | solution.py:198
  52.3 0.0 copy-done
  52.3 0.0 copy-done.1
  52.3 1.9 %attend.1 = bf16[128,256]{1,0:T(8,128)(2,1)S(1)} custom-call(s32[1,64]{1,0:T(1,128)S(1)} %get-tuple-element.7.presence_ref, bf16[2,16,16,128]{3,2,1,0:T(8,128)(2,1)S(1)} %pad_maximum_fusion.1.first_ref, bf16[2,16,16,128]{3,2,1,0:T(8,128)(2,1)S(1)} %collective-permute-done.1.second_ref, bf16[4,16,16,128]{3,2,1,0:T(8,128)(2,1)S(1)} %collective-permute-done.2.other_ref, ...), custom_call_target="tpu_custom_call" | custom-call | tf_op jit(solution)/shard_map/attend/pallas_call | solution.py:199
  54.2 2.3 %collective-permute-start.3 = (bf16[128,256]{1,0:T(8,128)(2,1)S(1)}, bf16[128,256]{1,0:T(8,128)(2,1)S(1)}, u32[]{:S(2)}, u32[]{:S(2)}) collective-permute-start(bf16[128,256]{1,0:T(8,128)(2,1)S(1)} %attend.1), channel_id=1, source_target_pairs={{0,1},{1,0},{2,3},{3,2},{4,5},{5,4},{6,7},{7,6},{8,9},{9,8},{10,11... | collective-permute-start | bytes 196616 | tf_op jit(solution)/shard_map/ppermute | solution.py:216
  56.5 0.9 %collective-permute-done.3 = bf16[128,256]{1,0:T(8,128)(2,1)S(1)} collective-permute-done((bf16[128,256]{1,0:T(8,128)(2,1)S(1)}, bf16[128,256]{1,0:T(8,128)(2,1)S(1)}, u32[]{:S(2)}, u32[]{:S(2)}) %collective-permute-start.3) | collective-permute-done | bytes 65568 | tf_op jit(solution)/shard_map/ppermute | solution.py:216
  57.4 3.6 %collective-permute-start.4 = (bf16[128,256]{1,0:T(8,128)(2,1)S(1)}, bf16[128,256]{1,0:T(8,128)(2,1)S(1)}, u32[]{:S(2)}, u32[]{:S(2)}) collective-permute-start(bf16[128,256]{1,0:T(8,128)(2,1)S(1)} %add_convert_fusion.2), channel_id=1, source_target_pairs={{0,2},{2,0},{4,6},{6,4},{1,3},{3,1},{5,7},{7,5},{8,10},{10,8},{12,... | collective-permute-start | bytes 196616 | tf_op jit(solution)/shard_map/ppermute | solution.py:216
  61.0 2.0 %collective-permute-done.4 = bf16[128,256]{1,0:T(8,128)(2,1)S(1)} collective-permute-done((bf16[128,256]{1,0:T(8,128)(2,1)S(1)}, bf16[128,256]{1,0:T(8,128)(2,1)S(1)}, u32[]{:S(2)}, u32[]{:S(2)}) %collective-permute-start.4) | collective-permute-done | bytes 65568 | tf_op jit(solution)/shard_map/ppermute | solution.py:216
  63.0 4.0 %collective-permute-start.5 = (bf16[128,256]{1,0:T(8,128)(2,1)S(1)}, bf16[128,256]{1,0:T(8,128)(2,1)S(1)}, u32[]{:S(2)}, u32[]{:S(2)}) collective-permute-start(bf16[128,256]{1,0:T(8,128)(2,1)S(1)} %add_convert_fusion.1), channel_id=1, source_target_pairs={{0,4},{2,6},{4,0},{6,2},{1,5},{3,7},{5,1},{7,3},{8,12},{10,14},{12... | collective-permute-start | bytes 196616 | tf_op jit(solution)/shard_map/ppermute | solution.py:216
  67.0 1.9 %collective-permute-done.5 = bf16[128,256]{1,0:T(8,128)(2,1)S(1)} collective-permute-done((bf16[128,256]{1,0:T(8,128)(2,1)S(1)}, bf16[128,256]{1,0:T(8,128)(2,1)S(1)}, u32[]{:S(2)}, u32[]{:S(2)}) %collective-permute-start.5) | collective-permute-done | bytes 65568 | tf_op jit(solution)/shard_map/ppermute | solution.py:216
  68.9 0.6 add_convert_fusion
  (9 shorter events, 0.1 us)
Async XLA Ops:
  0.0 52.3 %copy-start = (s32[1,16,128,128]{3,2,1,0:T(8,128)S(1)}, s32[1,16,128,128]{3,2,1,0:T(8,128)}, u32[]{:S(2)}) copy-start(s32[1,16,128,128]{3,2,1,0:T(8,128)} %masks_ref.1) | copy-start | bytes 3145732
  31.5 8.8 %collective-permute-start = (bf16[16,16,128]{2,1,0:T(8,128)(2,1)S(1)}, bf16[16,16,128]{2,1,0:T(8,128)(2,1)S(1)}, u32[]{:S(2)}, u32[]{:S(2)}) collective-permute-start(bf16[16,16,128]{2,1,0:T(8,128)(2,1)S(1)} %pick.1), channel_id=1, source_target_pairs={{0,4},{2,6},{4,0},{6,2},{1,5},{3,7},{5,1},{7,3},{8,12},{10,14},{12... | collective-permute-start | bytes 196616 | tf_op jit(solution)/shard_map/ppermute | solution.py:196
  40.3 12.0 %copy-start.1 = (bf16[128,128]{1,0:T(8,128)(2,1)S(1)}, bf16[128,128]{1,0:T(8,128)(2,1)}, u32[]{:S(2)}) copy-start(bf16[128,128]{1,0:T(8,128)(2,1)} %features_ref.1) | copy-start | bytes 98308
  40.3 12.0 %copy-start.2 = (bf16[128,256]{1,0:T(8,128)(2,1)S(1)}, bf16[128,256]{1,0:T(8,128)(2,1)}, u32[]{:S(2)}) copy-start(bf16[128,256]{1,0:T(8,128)(2,1)} %weight_ref.1) | copy-start | bytes 196612
  40.3 12.0 %copy-start.3 = (bf16[128,128]{1,0:T(8,128)(2,1)S(1)}, bf16[128,128]{1,0:T(8,128)(2,1)}, u32[]{:S(2)}) copy-start(bf16[128,128]{1,0:T(8,128)(2,1)} %proj_ref.1) | copy-start | bytes 98308
  40.3 12.0 %copy-start.4 = (f32[1,128]{1,0:T(1,128)S(1)}, f32[1,128]{1,0:T(1,128)}, u32[]{:S(2)}) copy-start(f32[1,128]{1,0:T(1,128)} %source_ref.1) | copy-start | bytes 1540
  40.3 12.0 %copy-start.5 = (f32[1,128]{1,0:T(1,128)S(1)}, f32[1,128]{1,0:T(1,128)}, u32[]{:S(2)}) copy-start(f32[1,128]{1,0:T(1,128)} %target_ref.1) | copy-start | bytes 1540
  40.3 5.8 %collective-permute-start.1 = (bf16[2,16,16,128]{3,2,1,0:T(8,128)(2,1)S(1)}, bf16[2,16,16,128]{3,2,1,0:T(8,128)(2,1)S(1)}, u32[]{:S(2)}, u32[]{:S(2)}) collective-permute-start(bf16[2,16,16,128]{3,2,1,0:T(8,128)(2,1)S(1)} %pad_maximum_fusion.1.first_ref), channel_id=1, source_target_pairs={{0,2},{2,0},{4,6},{6,4},{1,3},{3,1},{5,7},{7,5},{8,10},{10,8},{12,... | collective-permute-start | bytes 393224 | tf_op jit(solution)/shard_map/ppermute | solution.py:197
  46.2 6.1 %collective-permute-start.2 = (bf16[4,16,16,128]{3,2,1,0:T(8,128)(2,1)S(1)}, bf16[4,16,16,128]{3,2,1,0:T(8,128)(2,1)S(1)}, u32[]{:S(2)}, u32[]{:S(2)}) collective-permute-start(bf16[4,16,16,128]{3,2,1,0:T(8,128)(2,1)S(1)} %pad_maximum_fusion), channel_id=1, source_target_pairs={{0,1},{1,0},{2,3},{3,2},{4,5},{5,4},{6,7},{7,6},{8,9},{9,8},{10,11... | collective-permute-start | bytes 786440 | tf_op jit(solution)/shard_map/ppermute | solution.py:198
  54.2 3.2 %collective-permute-start.3 = (bf16[128,256]{1,0:T(8,128)(2,1)S(1)}, bf16[128,256]{1,0:T(8,128)(2,1)S(1)}, u32[]{:S(2)}, u32[]{:S(2)}) collective-permute-start(bf16[128,256]{1,0:T(8,128)(2,1)S(1)} %attend.1), channel_id=1, source_target_pairs={{0,1},{1,0},{2,3},{3,2},{4,5},{5,4},{6,7},{7,6},{8,9},{9,8},{10,11... | collective-permute-start | bytes 196616 | tf_op jit(solution)/shard_map/ppermute | solution.py:216
  57.4 5.6 %collective-permute-start.4 = (bf16[128,256]{1,0:T(8,128)(2,1)S(1)}, bf16[128,256]{1,0:T(8,128)(2,1)S(1)}, u32[]{:S(2)}, u32[]{:S(2)}) collective-permute-start(bf16[128,256]{1,0:T(8,128)(2,1)S(1)} %add_convert_fusion.2), channel_id=1, source_target_pairs={{0,2},{2,0},{4,6},{6,4},{1,3},{3,1},{5,7},{7,5},{8,10},{10,8},{12,... | collective-permute-start | bytes 196616 | tf_op jit(solution)/shard_map/ppermute | solution.py:216
  63.0 5.9 %collective-permute-start.5 = (bf16[128,256]{1,0:T(8,128)(2,1)S(1)}, bf16[128,256]{1,0:T(8,128)(2,1)S(1)}, u32[]{:S(2)}, u32[]{:S(2)}) collective-permute-start(bf16[128,256]{1,0:T(8,128)(2,1)S(1)} %add_convert_fusion.1), channel_id=1, source_target_pairs={{0,4},{2,6},{4,0},{6,2},{1,5},{3,7},{5,1},{7,3},{8,12},{10,14},{12... | collective-permute-start | bytes 196616 | tf_op jit(solution)/shard_map/ppermute | solution.py:216

commit v4 on v3

v4 whole, which is shorter than its diff:
```python
import functools

import jax
import jax.numpy as jnp
import numpy as np
from jax import lax
from jax.experimental import pallas as pl
from jax.experimental.pallas import tpu as pltpu
from jax.sharding import Mesh
from jax.sharding import PartitionSpec as P

NODE = ("yh", "z", "x")
HEAD = ("yl", "c")
EVERY = NODE + ("yl",)
SIZES = {"yh": 2, "z": 8, "x": 4, "yl": 4, "c": 2}
NODES = 64
EIGHTHS = 8
LOW = -1.0e38


def node_groups():
    groups = []
    for pair in range(SIZES["yl"]):
        group = []
        for yh in range(SIZES["yh"]):
            for z in range(SIZES["z"]):
                for x in range(SIZES["x"]):
                    place = (yh * SIZES["z"] + z) * SIZES["x"] + x
                    group.append(place * SIZES["yl"] + (pair ^ (2 * yh)))
        groups.append(group)
    return groups


def pair_of_device():
    return lax.axis_index("yl") ^ (2 * lax.axis_index("yh"))


def leaky_relu(values):
    return jnp.maximum(values, 0.2 * values)


def prepare_kernel(features_hbm, presence_hbm, send_ref, presence_ref, rows_ref, sems):
    part = rows_ref.shape[0]
    start = (pair_of_device() * SIZES["c"] + lax.axis_index("c")) * part
    rows_copy = pltpu.make_async_copy(
        features_hbm.at[pl.ds(pl.multiple_of(start, part), part)], rows_ref, sems.at[0]
    )
    presence_copy = pltpu.make_async_copy(presence_hbm, presence_ref, sems.at[1])
    rows_copy.start()
    presence_copy.start()
    rows_copy.wait()
    rows = rows_ref[...]
    for i in range(send_ref.shape[0]):
        send_ref[i] = rows
    presence_copy.wait()


def pick_kernel(presence_ref, gathered_ref, out_ref, slots_ref):
    slot = jnp.int32(0)
    for tile in range(gathered_ref.shape[0]):
        slots_ref[slot] = gathered_ref[tile]
        slot = jnp.minimum(slot + presence_ref[0, tile], out_ref.shape[1])
    for i in range(out_ref.shape[1]):
        rows = slots_ref[i]
        for copy in range(out_ref.shape[0]):
            out_ref[copy, i] = rows


def split_rows(vector):
    high = vector.astype(jnp.bfloat16).astype(jnp.float32)
    rest = vector - high
    middle = rest.astype(jnp.bfloat16).astype(jnp.float32)
    return high, middle, rest - middle


def pack_kernel(own_ref, proj_ref, weight_ref, source_ref, target_ref, out_ref):
    lows, slots, part, width = own_ref.shape
    rows = lows * slots * part
    out_ref[:rows] = own_ref[...].reshape(rows, width)
    out_ref[rows : rows + width] = proj_ref[...]
    for i in range(weight_ref.shape[1] // width):
        start = rows + (i + 1) * width
        out_ref[start : start + width] = weight_ref[:, i * width : (i + 1) * width]
    row = lax.broadcasted_iota(jnp.int32, (16, width), 0)
    block = jnp.zeros((16, width), jnp.float32)
    for i, vector in enumerate(split_rows(source_ref[...]) + split_rows(target_ref[...])):
        block = jnp.where(row == i, vector, block)
    out_ref[rows + 3 * width :] = block.astype(jnp.bfloat16)


def attend_kernel(
    presence_ref,
    own_ref,
    other_ref,
    features_ref,
    masks_ref,
    out_ref,
    sources,
    tables,
    masked,
    weights,
):
    slots, lows, cores, part, width = sources.shape
    heads = cores
    tile = masks_ref.shape[2]
    rows = lows * slots * part
    node = (lax.axis_index("yh") * SIZES["z"] + lax.axis_index("z")) * SIZES["x"] + lax.axis_index("x")
    core = lax.axis_index("c")
    for ref, side in ((own_ref, core), (other_ref, 1 - core)):
        tables[side] = ref[rows:]
        for low in range(lows):
            pair = low ^ (2 * lax.axis_index("yh"))
            start = low * slots * part
            sources[:, pair, side] = ref[start : start + slots * part].reshape(slots, part, width)

    both = jnp.concatenate([tables[h, :width] for h in range(heads)], axis=1)

    def project(values):
        return jnp.dot(values, both, preferred_element_type=jnp.float32).astype(jnp.bfloat16)

    projected = project(sources[...].reshape(slots * tile, width))
    local = project(features_ref[...]).astype(jnp.float32)
    vectors = [tables[h, 3 * width :] for h in range(heads)]
    row = lax.broadcasted_iota(jnp.int32, (16, width), 0)

    target_terms, self_source, source_terms = [], [], []
    for h in range(heads):
        wide = vectors[h].astype(jnp.float32)
        source = wide[0:1] + wide[1:2] + wide[2:3]
        target = wide[3:4] + wide[4:5] + wide[5:6]
        mine = local[:, h * width : (h + 1) * width]
        target_terms.append(jnp.sum(mine * target, axis=1, keepdims=True))
        self_source.append(jnp.sum(mine * source, axis=1, keepdims=True))
        terms = lax.dot_general(
            vectors[h],
            projected[:, h * width : (h + 1) * width],
            (((1,), (1,)), ((), ())),
            preferred_element_type=jnp.float32,
        )
        source_terms.append(terms[0:1] + terms[1:2] + terms[2:3])

    best = [jnp.full((tile, tile), LOW, jnp.float32) for h in range(heads)]
    for k in range(slots):
        linked = masks_ref[0, k] == 1
        for h in range(heads):
            value = jnp.where(linked, source_terms[h][:, k * tile : (k + 1) * tile], LOW)
            masked[h, k] = value
            best[h] = jnp.maximum(best[h], value)

    def count(i, rank):
        return rank + presence_ref[0, i]

    rank = lax.fori_loop(0, node, count, jnp.int32(0))

    @pl.when(presence_ref[0, node] == 1)
    def _():
        down = lax.broadcasted_iota(jnp.int32, (tile, tile), 0)
        over = lax.broadcasted_iota(jnp.int32, (tile, tile), 1)
        for h in range(heads):
            masked[h, rank] = jnp.where(down == over, LOW, masked[h, rank])

    outs = []
    for h in range(heads):
        mine = local[:, h * width : (h + 1) * width]
        top = jnp.maximum(jnp.max(best[h], axis=1, keepdims=True), self_source[h])
        peak = leaky_relu(target_terms[h] + top)
        self_weight = jnp.exp(leaky_relu(target_terms[h] + self_source[h]) - peak)
        total = jnp.zeros((tile, tile), jnp.float32)
        for k in range(slots):
            edge = jnp.exp(leaky_relu(target_terms[h] + masked[h, k]) - peak)
            total = total + edge
            weights[h, :, k * tile : (k + 1) * tile] = edge.astype(jnp.bfloat16)
        denominator = jnp.sum(total, axis=1, keepdims=True) + self_weight
        summed = jnp.dot(
            weights[h],
            projected[:, h * width : (h + 1) * width],
            preferred_element_type=jnp.float32,
        )
        summed = summed + self_weight.astype(jnp.bfloat16).astype(jnp.float32) * mine
        attended = summed / denominator
        below = jnp.minimum(attended, 0.0)
        bent = jnp.tanh(0.5 * below)
        outs.append(jnp.where(attended > 0, attended, 2.0 * bent / (1.0 - bent)).astype(jnp.bfloat16))
    joined = jnp.concatenate(outs, axis=1)
    columns = []
    for i in (1, 2):
        table = jnp.concatenate(
            [tables[h, i * width : (i + 1) * width] for h in range(heads)], axis=0
        )
        columns.append(jnp.dot(joined, table, preferred_element_type=jnp.float32))
    mixed = jnp.concatenate(columns, axis=1).astype(jnp.bfloat16)
    for copy in range(out_ref.shape[0]):
        out_ref[copy] = mixed


def per_device(features, proj_weight, score_source, score_target, out_weight, presence, tile_masks):
    tile, width = features.shape
    slots = tile_masks.shape[1]
    part = tile // EIGHTHS
    lows = SIZES["yl"]
    vmem = pl.BlockSpec(memory_space=pltpu.VMEM)
    smem = pl.BlockSpec(memory_space=pltpu.SMEM)
    raw = pl.BlockSpec(memory_space=pltpu.HBM)

    features_far = pltpu.with_memory_space_constraint(features, pltpu.HBM)
    presence_far = pltpu.with_memory_space_constraint(presence, pltpu.HBM)
    send, presence = pl.pallas_call(
        prepare_kernel,
        out_shape=(
            jax.ShapeDtypeStruct((NODES, part, width), jnp.bfloat16),
            jax.ShapeDtypeStruct(presence.shape, jnp.int32),
        ),
        in_specs=[raw, raw],
        out_specs=(vmem, vmem),
        scratch_shapes=[pltpu.VMEM((part, width), jnp.bfloat16), pltpu.SemaphoreType.DMA((2,))],
        compiler_params=pltpu.CompilerParams(vmem_limit_bytes=4 << 20),
        name="prepare",
    )(features_far, presence_far)
    gathered = lax.all_to_all(
        send, EVERY, 0, 0, tiled=True, axis_index_groups=node_groups()
    )
    picked = pl.pallas_call(
        pick_kernel,
        out_shape=jax.ShapeDtypeStruct((lows, slots, part, width), jnp.bfloat16),
        in_specs=[smem, vmem],
        out_specs=vmem,
        scratch_shapes=[pltpu.VMEM((slots + 1, part, width), jnp.bfloat16)],
        compiler_params=pltpu.CompilerParams(vmem_limit_bytes=4 << 20),
        name="pick",
    )(presence, gathered)
    swap = [(0, 1), (1, 0)]
    own = lax.all_to_all(picked, "yl", 0, 0, tiled=True)
    payload = lows * slots * part + 3 * width + 16
    packed = pl.pallas_call(
        pack_kernel,
        out_shape=jax.ShapeDtypeStruct((payload, width), jnp.bfloat16),
        in_specs=[vmem] * 5,
        out_specs=vmem,
        compiler_params=pltpu.CompilerParams(vmem_limit_bytes=4 << 20),
        name="pack",
    )(own, proj_weight, out_weight, score_source, score_target)
    other = lax.ppermute(packed, "c", swap)
    cores = SIZES["c"]
    paired = pl.pallas_call(
        attend_kernel,
        out_shape=jax.ShapeDtypeStruct((lows, tile, out_weight.shape[1]), jnp.bfloat16),
        in_specs=[smem] + [vmem] * 4,
        out_specs=vmem,
        scratch_shapes=[
            pltpu.VMEM((slots, lows, cores, part, width), jnp.bfloat16),
            pltpu.VMEM((cores, 3 * width + 16, width), jnp.bfloat16),
            pltpu.VMEM((cores, slots, tile, tile), jnp.float32),
            pltpu.VMEM((cores, tile, slots * tile), jnp.bfloat16),
        ],
        compiler_params=pltpu.CompilerParams(vmem_limit_bytes=16 << 20),
        name="attend",
    )(presence, packed, other, features, tile_masks)
    pieces = lax.all_to_all(paired, "yl", 0, 0, tiled=True)
    return jnp.sum(pieces.astype(jnp.float32), axis=0).astype(jnp.bfloat16)


def solution(mesh):
    shape = tuple(SIZES[name] for name in NODE + HEAD)
    fine = Mesh(np.asarray(mesh.devices).reshape(shape), NODE + HEAD)
    return jax.shard_map(
        per_device,
        mesh=fine,
        in_specs=(
            P(NODE, None),
            P(None, HEAD),
            P(HEAD, None),
            P(HEAD, None),
            P(HEAD, None),
            P(NODE, None),
            P(NODE, None, None, None),
        ),
        out_specs=P(NODE, None),
        check_vma=False,
    )
```

time: 70.8 us -> 65.1 us (0.919)
  blocking collectives: 30 us -> 52 us
  starting transfers between devices: 23.8 us -> 5.6 us
  waiting for transfers between devices: 11.5 us -> 1.29 us
  Pallas kernels: 3.39 us -> 4.34 us
    all_to_all x0 -> x2, blocking collectives: none -> 21.9 us  [the longest x1 12.4 us: per_device(): own = lax.all_to_all(picked, 'yl', 0, 0, tiled=True)]
    ppermute x6 -> x1, starting transfers between devices: 23.8 us -> 5.6 us  [per_device(): other = lax.ppermute(packed, 'c', swap)]
    ppermute x6 -> x1, waiting for transfers between devices: 11.5 us -> 1.29 us  [per_device(): other = lax.ppermute(packed, 'c', swap)]
    pallas_call x2 -> x3, Pallas kernels: 2.56 us -> 3.6 us  [the longest x1 2.85 us: per_device(): pl.pallas_call(attend_kernel, out_shape=jax.ShapeDtypeStruct((lows, tile,...]
  transfers between devices with their start and end apart: 6 -> 1, of which waited for: 6 -> 1; matrix products, arithmetic and copies ran while one was open for 0% -> 0% of each run, Pallas kernels for 0% -> 0%
where the time goes in v4:
time: 65.1 us; the launch traced here: 64 us
  blocking collectives  52 us (80%)
  starting transfers between devices  5.6 us (9%)
  Pallas kernels  4.34 us (7%)
  waiting for transfers between devices  1.29 us (2%)
  other arithmetic  0.67 us (1%)
    all_to_all x1, blocking collectives, per_device(): lax.all_to_all(send, EVERY, 0, 0, tiled=True, axis_index_groups=node_grou...  30.1 us
    all_to_all x1, blocking collectives, per_device(): own = lax.all_to_all(picked, 'yl', 0, 0, tiled=True)  12.4 us
    all_to_all x1, blocking collectives, per_device(): pieces = lax.all_to_all(paired, 'yl', 0, 0, tiled=True)  9.45 us
    ppermute x1, starting transfers between devices, per_device(): other = lax.ppermute(packed, 'c', swap)  5.6 us
    pallas_call x1, Pallas kernels, per_device(): pl.pallas_call(attend_kernel, out_shape=jax.ShapeDtypeStruct((lows, tile,...  2.85 us
  transfers between devices with their start and end apart: 1, of which 1 were waited for; matrix products, arithmetic and copies ran while one was open for 0% of the time, Pallas kernels for 0%

profile of v4, /device:TPU:1, one launch (start us, length us, event | category | flops | bytes accessed | tf_op | source)
XLA Modules:
  0.0 64.0 jit_solution(6297623833398635121)
XLA Ops:
  0.0 0.7 %prepare.1 = (bf16[64,16,128]{2,1,0:T(8,128)(2,1)S(1)}, s32[1,64]{1,0:T(1,128)S(1)}) custom-call(bf16[128,128]{1,0:T(8,128)(2,1)} %features_ref.1, s32[1,64]{1,0:T(1,128)} %presence_hbm.1), custom_call_target="tpu_custom_call" | custom-call | tf_op jit(solution)/shard_map/prepare/pallas_call | solution.py:207
  0.7 0.0 copy-start
  0.8 30.1 %all_to_all.15.gathered_ref = bf16[64,16,128]{2,1,0:T(8,128)(2,1)S(1)} all-to-all(bf16[64,16,128]{2,1,0:T(8,128)(2,1)S(1)} %get-tuple-element.8), channel_id=1, replica_groups={{0,8,16,24,32,40,48,56,64,72,80,88,96,104,112,120,128,136,144,152,160,1..., dimensions={0} | all-to-all | bytes 524288 | tf_op jit(solution)/shard_map/all_to_all | solution.py:219
  30.9 0.7 %pick.1 = bf16[4,16,16,128]{3,2,1,0:T(8,128)(2,1)S(1)} custom-call(s32[1,64]{1,0:T(1,128)S(1)} %get-tuple-element.7.presence_ref, bf16[64,16,128]{2,1,0:T(8,128)(2,1)S(1)} %all_to_all.15.gathered_ref), custom_call_target="tpu_custom_call" | custom-call | tf_op jit(solution)/shard_map/pick/pallas_call | solution.py:222
  31.6 0.0 copy-start.2
  31.6 0.0 copy-start.3
  31.6 0.0 copy-start.4
  31.6 0.0 copy-start.5
  31.6 12.4 %all_to_all.16.own_ref = bf16[4,16,16,128]{3,2,1,0:T(8,128)(2,1)S(1)} all-to-all(bf16[4,16,16,128]{3,2,1,0:T(8,128)(2,1)S(1)} %pick.1), channel_id=1, replica_groups=mesh['yh'=2,'z'=8,'x'=4,'yl'=4,'c'=2] {'yl'}, dimensions={0} | all-to-all | bytes 524288 | tf_op jit(solution)/shard_map/all_to_all | solution.py:232
  44.1 0.0 copy-done.2
  44.1 0.0 copy-done.3
  44.1 0.0 copy-done.4
  44.1 0.0 copy-done.5
  44.1 0.0 copy-start.1
  44.1 5.6 %collective-permute-start = (bf16[1424,128]{1,0:T(8,128)(2,1)S(1)}, bf16[1424,128]{1,0:T(8,128)(2,1)S(1)}, u32[]{:S(2)}, u32[]{:S(2)}) collective-permute-start(bf16[1424,128]{1,0:T(8,128)(2,1)S(1)} %pack.1.own_ref), channel_id=1, source_target_pairs={{0,1},{1,0},{2,3},{3,2},{4,5},{5,4},{6,7},{7,6},{8,9},{9,8},{10,11... | collective-permute-start | bytes 1093640 | tf_op jit(solution)/shard_map/ppermute | solution.py:242
  49.7 1.3 %collective-permute-done.other_ref = bf16[1424,128]{1,0:T(8,128)(2,1)S(1)} collective-permute-done((bf16[1424,128]{1,0:T(8,128)(2,1)S(1)}, bf16[1424,128]{1,0:T(8,128)(2,1)S(1)}, u32[]{:S(2)}, u32[]{:S(2)}) %collective-permute-start) | collective-permute-done | bytes 364576 | tf_op jit(solution)/shard_map/ppermute | solution.py:242
  51.0 0.0 copy-done
  51.0 0.0 copy-done.1
  51.0 2.8 %attend.1 = bf16[4,128,256]{2,1,0:T(8,128)(2,1)S(1)} custom-call(s32[1,64]{1,0:T(1,128)S(1)} %get-tuple-element.7.presence_ref, bf16[1424,128]{1,0:T(8,128)(2,1)S(1)} %pack.1.own_ref, bf16[1424,128]{1,0:T(8,128)(2,1)S(1)} %collective-permute-done.other_ref, bf16[128,128]{1,0:T(8,128)(2,1)S(1)} %copy-done.1, s32[1,16,128,128]{3,2,1,0:T(8,128)S(1)} %copy-done), custom_call_target="tpu_custom_call" | custom-call | tf_op jit(solution)/shard_map/attend/pallas_call | solution.py:244
  53.9 9.4 %all_to_all.17 = bf16[4,128,256]{2,1,0:T(8,128)(2,1)S(1)} all-to-all(bf16[4,128,256]{2,1,0:T(8,128)(2,1)S(1)} %attend.1), channel_id=1, replica_groups=mesh['yh'=2,'z'=8,'x'=4,'yl'=4,'c'=2] {'yl'}, dimensions={0} | all-to-all | bytes 524288 | tf_op jit(solution)/shard_map/all_to_all | solution.py:258
  63.3 0.7 %reduce_sum.12 = bf16[128,256]{1,0:T(8,128)(2,1)} reduce(bf16[4,128,256]{2,1,0:T(8,128)(2,1)S(1)} %all_to_all.17, bf16[]{:T(256)} %constant.2.clone.1), dimensions={0}, to_apply=%region_0.0 | reduce | flops 98304 | bytes 327682 | tf_op jit(solution)/shard_map/reduce_sum | solution.py:259
  (1 shorter events, 0.0 us)
Async XLA Ops:
  0.7 50.3 %copy-start = (s32[1,16,128,128]{3,2,1,0:T(8,128)S(1)}, s32[1,16,128,128]{3,2,1,0:T(8,128)}, u32[]{:S(2)}) copy-start(s32[1,16,128,128]{3,2,1,0:T(8,128)} %masks_ref.1) | copy-start | bytes 3145732
  31.6 12.5 %copy-start.2 = (bf16[128,256]{1,0:T(8,128)(2,1)S(1)}, bf16[128,256]{1,0:T(8,128)(2,1)}, u32[]{:S(2)}) copy-start(bf16[128,256]{1,0:T(8,128)(2,1)} %weight_ref.1) | copy-start | bytes 196612
  31.6 12.5 %copy-start.3 = (bf16[128,128]{1,0:T(8,128)(2,1)S(1)}, bf16[128,128]{1,0:T(8,128)(2,1)}, u32[]{:S(2)}) copy-start(bf16[128,128]{1,0:T(8,128)(2,1)} %proj_ref.1) | copy-start | bytes 98308
  31.6 12.4 %copy-start.4 = (f32[1,128]{1,0:T(1,128)S(1)}, f32[1,128]{1,0:T(1,128)}, u32[]{:S(2)}) copy-start(f32[1,128]{1,0:T(1,128)} %source_ref.1) | copy-start | bytes 1540
  31.6 12.4 %copy-start.5 = (f32[1,128]{1,0:T(1,128)S(1)}, f32[1,128]{1,0:T(1,128)}, u32[]{:S(2)}) copy-start(f32[1,128]{1,0:T(1,128)} %target_ref.1) | copy-start | bytes 1540
  44.1 7.0 %copy-start.1 = (bf16[128,128]{1,0:T(8,128)(2,1)S(1)}, bf16[128,128]{1,0:T(8,128)(2,1)}, u32[]{:S(2)}) copy-start(bf16[128,128]{1,0:T(8,128)(2,1)} %features_ref.1) | copy-start | bytes 98308
  44.1 6.9 %collective-permute-start = (bf16[1424,128]{1,0:T(8,128)(2,1)S(1)}, bf16[1424,128]{1,0:T(8,128)(2,1)S(1)}, u32[]{:S(2)}, u32[]{:S(2)}) collective-permute-start(bf16[1424,128]{1,0:T(8,128)(2,1)S(1)} %pack.1.own_ref), channel_id=1, source_target_pairs={{0,1},{1,0},{2,3},{3,2},{4,5},{5,4},{6,7},{7,6},{8,9},{9,8},{10,11... | collective-permute-start | bytes 1093640 | tf_op jit(solution)/shard_map/ppermute | solution.py:242

commit v5 on v4

--- a/solution.py
+++ b/solution.py
@@ -16,6 +16,7 @@
 NODES = 64
 EIGHTHS = 8
 LOW = -1.0e38
+LOG2E = 1.4426950408889634
 
 
 def node_groups():
@@ -88,64 +89,11 @@
     out_ref[rows + 3 * width :] = block.astype(jnp.bfloat16)
 
 
-def attend_kernel(
-    presence_ref,
-    own_ref,
-    other_ref,
-    features_ref,
-    masks_ref,
-    out_ref,
-    sources,
-    tables,
-    masked,
-    weights,
-):
-    slots, lows, cores, part, width = sources.shape
-    heads = cores
-    tile = masks_ref.shape[2]
-    rows = lows * slots * part
+def mask_kernel(presence_ref, masks_ref, out_ref):
+    _, slots, tile, _ = masks_ref.shape
     node = (lax.axis_index("yh") * SIZES["z"] + lax.axis_index("z")) * SIZES["x"] + lax.axis_index("x")
-    core = lax.axis_index("c")
-    for ref, side in ((own_ref, core), (other_ref, 1 - core)):
-        tables[side] = ref[rows:]
-        for low in range(lows):
-            pair = low ^ (2 * lax.axis_index("yh"))
-            start = low * slots * part
-            sources[:, pair, side] = ref[start : start + slots * part].reshape(slots, part, width)
-
-    both = jnp.concatenate([tables[h, :width] for h in range(heads)], axis=1)
-
-    def project(values):
-        return jnp.dot(values, both, preferred_element_type=jnp.float32).astype(jnp.bfloat16)
-
-    projected = project(sources[...].reshape(slots * tile, width))
-    local = project(features_ref[...]).astype(jnp.float32)
-    vectors = [tables[h, 3 * width :] for h in range(heads)]
-    row = lax.broadcasted_iota(jnp.int32, (16, width), 0)
-
-    target_terms, self_source, source_terms = [], [], []
-    for h in range(heads):
-        wide = vectors[h].astype(jnp.float32)
-        source = wide[0:1] + wide[1:2] + wide[2:3]
-        target = wide[3:4] + wide[4:5] + wide[5:6]
-        mine = local[:, h * width : (h + 1) * width]
-        target_terms.append(jnp.sum(mine * target, axis=1, keepdims=True))
-        self_source.append(jnp.sum(mine * source, axis=1, keepdims=True))
-        terms = lax.dot_general(
-            vectors[h],
-            projected[:, h * width : (h + 1) * width],
-            (((1,), (1,)), ((), ())),
-            preferred_element_type=jnp.float32,
-        )
-        source_terms.append(terms[0:1] + terms[1:2] + terms[2:3])
-
-    best = [jnp.full((tile, tile), LOW, jnp.float32) for h in range(heads)]
     for k in range(slots):
-        linked = masks_ref[0, k] == 1
-        for h in range(heads):
-            value = jnp.where(linked, source_terms[h][:, k * tile : (k + 1) * tile], LOW)
-            masked[h, k] = value
-            best[h] = jnp.maximum(best[h], value)
+        out_ref[k] = jnp.where(masks_ref[0, k] == 1, 0.0, LOW)
 
     def count(i, rank):
         return rank + presence_ref[0, i]
@@ -156,27 +104,89 @@
     def _():
         down = lax.broadcasted_iota(jnp.int32, (tile, tile), 0)
         over = lax.broadcasted_iota(jnp.int32, (tile, tile), 1)
+        out_ref[rank] = jnp.where(down == over, LOW, out_ref[rank])
+
+
+def attend_kernel(own_ref, other_ref, features_ref, added_ref, out_ref, values, tables):
+    slots, lows, cores, part, columns = values.shape
+    heads = cores
+    width = columns // heads
+    tile = added_ref.shape[1]
+    share = slots * part
+    rows = lows * share
+    core = lax.axis_index("c")
+    for ref, side in ((own_ref, core), (other_ref, 1 - core)):
+        tables[side] = ref[rows:]
+    both = jnp.concatenate([tables[h, :width] for h in range(heads)], axis=1)
+
+    def project(block):
+        return jnp.dot(block, both, preferred_element_type=jnp.float32).astype(jnp.bfloat16)
+
+    for ref, side in ((own_ref, core), (other_ref, 1 - core)):
+        for low in range(lows):
+            pair = low ^ (2 * lax.axis_index("yh"))
+            block = project(ref[low * share : (low + 1) * share])
+            values[:, pair, side] = block.reshape(slots, part, columns)
+
+    local = project(features_ref[...]).astype(jnp.float32)
+    row = lax.broadcasted_iota(jnp.int32, (16, width), 0)
+    target_terms, self_source, spread = [], [], []
+    for h in range(heads):
+        wide = tables[h, 3 * width :].astype(jnp.float32)
+        source = wide[0:1] + wide[1:2] + wide[2:3]
+        target = wide[3:4] + wide[4:5] + wide[5:6]
+        mine = local[:, h * width : (h + 1) * width]
+        target_terms.append(LOG2E * jnp.sum(mine * target, axis=1, keepdims=True))
+        self_source.append(LOG2E * jnp.sum(mine * source, axis=1, keepdims=True))
+        block = jnp.zeros((16, width), jnp.float32)
+        for i in range(3):
+            block = jnp.where(row == 8 * h + i, wide[i : i + 1], block)
+        spread.append(block)
+    terms = lax.dot_general(
+        jnp.concatenate(spread, axis=1).astype(jnp.bfloat16),
+        values[...].reshape(slots * tile, columns),
+        (((1,), (1,)), ((), ())),
+        preferred_element_type=jnp.float32,
+    )
+    source_terms = [
+        LOG2E * (terms[8 * h : 8 * h + 1] + terms[8 * h + 1 : 8 * h + 2] + terms[8 * h + 2 : 8 * h + 3])
+        for h in range(heads)
+    ]
+
+    best = [jnp.full((tile, tile), LOW, jnp.float32) for h in range(heads)]
+    for k in range(slots):
+        added = added_ref[k]
         for h in range(heads):
-            masked[h, rank] = jnp.where(down == over, LOW, masked[h, rank])
+            best[h] = jnp.maximum(best[h], source_terms[h][:, k * tile : (k + 1) * tile] + added)
+    peaks, self_weights = [], []
+    for h in range(heads):
+        top = jnp.maximum(jnp.max(best[h], axis=1, keepdims=True), self_source[h])
+        peaks.append(leaky_relu(target_terms[h] + top))
+        self_weights.append(jnp.exp2(leaky_relu(target_terms[h] + self_source[h]) - peaks[h]))
+
+    totals = [jnp.zeros((tile, tile), jnp.float32) for h in range(heads)]
+    sums = [jnp.zeros((tile, width), jnp.float32) for h in range(heads)]
+    group = 2
+    for first in range(0, slots, group):
+        for h in range(heads):
+            edges = []
+            for k in range(first, first + group):
+                scores = source_terms[h][:, k * tile : (k + 1) * tile] + added_ref[k]
+                edge = jnp.exp2(leaky_relu(target_terms[h] + scores) - peaks[h])
+                totals[h] = totals[h] + edge
+                edges.append(edge.astype(jnp.bfloat16))
+            near = values[first : first + group, :, :, :, h * width : (h + 1) * width]
+            sums[h] = sums[h] + jnp.dot(
+                jnp.concatenate(edges, axis=1),
+                near.reshape(group * tile, width),
+                preferred_element_type=jnp.float32,
+            )
 
     outs = []
     for h in range(heads):
         mine = local[:, h * width : (h + 1) * width]
-        top = jnp.maximum(jnp.max(best[h], axis=1, keepdims=True), self_source[h])
-        peak = leaky_relu(target_terms[h] + top)
-        self_weight = jnp.exp(leaky_relu(target_terms[h] + self_source[h]) - peak)
-        total = jnp.zeros((tile, tile), jnp.float32)
-        for k in range(slots):
-            edge = jnp.exp(leaky_relu(target_terms[h] + masked[h, k]) - peak)
-            total = total + edge
-            weights[h, :, k * tile : (k + 1) * tile] = edge.astype(jnp.bfloat16)
-        denominator = jnp.sum(total, axis=1, keepdims=True) + self_weight
-        summed = jnp.dot(
-            weights[h],
-            projected[:, h * width : (h + 1) * width],
-            preferred_element_type=jnp.float32,
-        )
-        summed = summed + self_weight.astype(jnp.bfloat16).astype(jnp.float32) * mine
+        denominator = jnp.sum(totals[h], axis=1, keepdims=True) + self_weights[h]
+        summed = sums[h] + self_weights[h].astype(jnp.bfloat16).astype(jnp.float32) * mine
         attended = summed / denominator
         below = jnp.minimum(attended, 0.0)
         bent = jnp.tanh(0.5 * below)
@@ -241,20 +251,27 @@
     )(own, proj_weight, out_weight, score_source, score_target)
     other = lax.ppermute(packed, "c", swap)
     cores = SIZES["c"]
+    added = pl.pallas_call(
+        mask_kernel,
+        out_shape=jax.ShapeDtypeStruct((slots, tile, tile), jnp.float32),
+        in_specs=[smem, vmem],
+        out_specs=vmem,
+        compiler_params=pltpu.CompilerParams(vmem_limit_bytes=4 << 20),
+        cost_estimate=pl.CostEstimate(flops=slots * tile * tile, bytes_accessed=8 * slots * tile * tile, transcendentals=0),
+        name="mask",
+    )(presence, tile_masks)
     paired = pl.pallas_call(
         attend_kernel,
         out_shape=jax.ShapeDtypeStruct((lows, tile, out_weight.shape[1]), jnp.bfloat16),
-        in_specs=[smem] + [vmem] * 4,
+        in_specs=[vmem] * 4,
         out_specs=vmem,
         scratch_shapes=[
-            pltpu.VMEM((slots, lows, cores, part, width), jnp.bfloat16),
+            pltpu.VMEM((slots, lows, cores, part, cores * width), jnp.bfloat16),
             pltpu.VMEM((cores, 3 * width + 16, width), jnp.bfloat16),
-            pltpu.VMEM((cores, slots, tile, tile), jnp.float32),
-            pltpu.VMEM((cores, tile, slots * tile), jnp.bfloat16),
         ],
         compiler_params=pltpu.CompilerParams(vmem_limit_bytes=16 << 20),
         name="attend",
-    )(presence, packed, other, features, tile_masks)
+    )(packed, other, features, added)
     pieces = lax.all_to_all(paired, "yl", 0, 0, tiled=True)
     return jnp.sum(pieces.astype(jnp.float32), axis=0).astype(jnp.bfloat16)
 

time: 65.1 us -> 64.3 us (0.988)
  waiting for transfers between devices: 1.29 us -> 0.62 us
    pallas_call x1, Pallas kernels: 2.85 us -> 1.97 us  [per_device(): pl.pallas_call(attend_kernel, out_shape=jax.ShapeDtypeStruct((lows, tile,...]
    ppermute x1, waiting for transfers between devices: 1.29 us -> 0.62 us  [per_device(): other = lax.ppermute(packed, 'c', swap)]
  transfers between devices with their start and end apart: 1 -> 1, of which waited for: 1 -> 1; matrix products, arithmetic and copies ran while one was open for 0% -> 0% of each run, Pallas kernels for 0% -> 1%
where the time goes in v5:
time: 64.3 us; the launch traced here: 63.1 us
  blocking collectives  52 us (81%)
  starting transfers between devices  5.6 us (9%)
  Pallas kernels  4.11 us (6%)
  other arithmetic  0.67 us (1%)
    all_to_all x1, blocking collectives, per_device(): lax.all_to_all(send, EVERY, 0, 0, tiled=True, axis_index_groups=node_grou...  30.1 us
    all_to_all x1, blocking collectives, per_device(): own = lax.all_to_all(picked, 'yl', 0, 0, tiled=True)  12.4 us
    all_to_all x1, blocking collectives, per_device(): pieces = lax.all_to_all(paired, 'yl', 0, 0, tiled=True)  9.44 us
    ppermute x1, starting transfers between devices, per_device(): other = lax.ppermute(packed, 'c', swap)  5.6 us
    pallas_call x1, Pallas kernels, per_device(): pl.pallas_call(attend_kernel, out_shape=jax.ShapeDtypeStruct((lows, tile,...  1.97 us
  transfers between devices with their start and end apart: 1, of which 1 were waited for; matrix products, arithmetic and copies ran while one was open for 0% of the time, Pallas kernels for 1%

profile of v5, /device:TPU:1, one launch (start us, length us, event | category | flops | bytes accessed | tf_op | source)
XLA Modules:
  0.0 63.1 jit_solution(10229604914123668095)
XLA Ops:
  0.0 0.7 %prepare.1 = (bf16[64,16,128]{2,1,0:T(8,128)(2,1)S(1)}, s32[1,64]{1,0:T(1,128)S(1)}) custom-call(bf16[128,128]{1,0:T(8,128)(2,1)} %features_ref.1, s32[1,64]{1,0:T(1,128)} %presence_hbm.1), custom_call_target="tpu_custom_call" | custom-call | tf_op jit(solution)/shard_map/prepare/pallas_call | solution.py:217
  0.7 0.0 copy-start
  0.8 30.1 %all_to_all.15.gathered_ref = bf16[64,16,128]{2,1,0:T(8,128)(2,1)S(1)} all-to-all(bf16[64,16,128]{2,1,0:T(8,128)(2,1)S(1)} %get-tuple-element.8), channel_id=1, replica_groups={{0,8,16,24,32,40,48,56,64,72,80,88,96,104,112,120,128,136,144,152,160,1..., dimensions={0} | all-to-all | bytes 524288 | tf_op jit(solution)/shard_map/all_to_all | solution.py:229
  30.9 0.7 %pick.1 = bf16[4,16,16,128]{3,2,1,0:T(8,128)(2,1)S(1)} custom-call(s32[1,64]{1,0:T(1,128)S(1)} %get-tuple-element.7.presence_ref, bf16[64,16,128]{2,1,0:T(8,128)(2,1)S(1)} %all_to_all.15.gathered_ref), custom_call_target="tpu_custom_call" | custom-call | tf_op jit(solution)/shard_map/pick/pallas_call | solution.py:232
  31.6 0.0 copy-start.2
  31.6 0.0 copy-start.3
  31.6 0.0 copy-start.4
  31.6 0.0 copy-start.5
  31.6 12.4 %all_to_all.16.own_ref = bf16[4,16,16,128]{3,2,1,0:T(8,128)(2,1)S(1)} all-to-all(bf16[4,16,16,128]{3,2,1,0:T(8,128)(2,1)S(1)} %pick.1), channel_id=1, replica_groups=mesh['yh'=2,'z'=8,'x'=4,'yl'=4,'c'=2] {'yl'}, dimensions={0} | all-to-all | bytes 524288 | tf_op jit(solution)/shard_map/all_to_all | solution.py:242
  44.1 0.0 copy-done.2
  44.1 0.0 copy-done.3
  44.1 0.0 copy-done.4
  44.1 0.0 copy-done.5
  44.1 0.0 copy-start.1
  44.1 5.6 %collective-permute-start = (bf16[1424,128]{1,0:T(8,128)(2,1)S(1)}, bf16[1424,128]{1,0:T(8,128)(2,1)S(1)}, u32[]{:S(2)}, u32[]{:S(2)}) collective-permute-start(bf16[1424,128]{1,0:T(8,128)(2,1)S(1)} %pack.1.own_ref), channel_id=1, source_target_pairs={{0,1},{1,0},{2,3},{3,2},{4,5},{5,4},{6,7},{7,6},{8,9},{9,8},{10,11... | collective-permute-start | bytes 1093640 | tf_op jit(solution)/shard_map/ppermute | solution.py:252
  49.7 0.0 copy-done
  49.8 0.6 %mask.1.added_ref = f32[16,128,128]{2,1,0:T(8,128)S(1)} custom-call(s32[1,64]{1,0:T(1,128)S(1)} %get-tuple-element.7.presence_ref, s32[1,16,128,128]{3,2,1,0:T(8,128)S(1)} %copy-done), custom_call_target="tpu_custom_call" | custom-call | flops 262144 | bytes 2097152 | tf_op jit(solution)/shard_map/mask/pallas_call | solution.py:254
  50.4 0.6 collective-permute-done.other_ref
  51.0 0.0 copy-done.1
  51.0 2.0 %attend.1 = bf16[4,128,256]{2,1,0:T(8,128)(2,1)S(1)} custom-call(bf16[1424,128]{1,0:T(8,128)(2,1)S(1)} %pack.1.own_ref, bf16[1424,128]{1,0:T(8,128)(2,1)S(1)} %collective-permute-done.other_ref, bf16[128,128]{1,0:T(8,128)(2,1)S(1)} %copy-done.1, f32[16,128,128]{2,1,0:T(8,128)S(1)} %mask.1.added_ref), custom_call_target="tpu_custom_call" | custom-call | tf_op jit(solution)/shard_map/attend/pallas_call | solution.py:263
  53.0 9.4 %all_to_all.17 = bf16[4,128,256]{2,1,0:T(8,128)(2,1)S(1)} all-to-all(bf16[4,128,256]{2,1,0:T(8,128)(2,1)S(1)} %attend.1), channel_id=1, replica_groups=mesh['yh'=2,'z'=8,'x'=4,'yl'=4,'c'=2] {'yl'}, dimensions={0} | all-to-all | bytes 524288 | tf_op jit(solution)/shard_map/all_to_all | solution.py:275
  62.5 0.7 %reduce_sum.12 = bf16[128,256]{1,0:T(8,128)(2,1)} reduce(bf16[4,128,256]{2,1,0:T(8,128)(2,1)S(1)} %all_to_all.17, bf16[]{:T(256)} %constant.2.clone.1), dimensions={0}, to_apply=%region_0.0 | reduce | flops 98304 | bytes 327682 | tf_op jit(solution)/shard_map/reduce_sum | solution.py:276
  (1 shorter events, 0.0 us)
Async XLA Ops:
  0.7 49.0 %copy-start = (s32[1,16,128,128]{3,2,1,0:T(8,128)S(1)}, s32[1,16,128,128]{3,2,1,0:T(8,128)}, u32[]{:S(2)}) copy-start(s32[1,16,128,128]{3,2,1,0:T(8,128)} %masks_ref.1) | copy-start | bytes 3145732
  31.6 12.5 %copy-start.2 = (bf16[128,256]{1,0:T(8,128)(2,1)S(1)}, bf16[128,256]{1,0:T(8,128)(2,1)}, u32[]{:S(2)}) copy-start(bf16[128,256]{1,0:T(8,128)(2,1)} %weight_ref.1) | copy-start | bytes 196612
  31.6 12.5 %copy-start.3 = (bf16[128,128]{1,0:T(8,128)(2,1)S(1)}, bf16[128,128]{1,0:T(8,128)(2,1)}, u32[]{:S(2)}) copy-start(bf16[128,128]{1,0:T(8,128)(2,1)} %proj_ref.1) | copy-start | bytes 98308
  31.6 12.4 %copy-start.4 = (f32[1,128]{1,0:T(1,128)S(1)}, f32[1,128]{1,0:T(1,128)}, u32[]{:S(2)}) copy-start(f32[1,128]{1,0:T(1,128)} %source_ref.1) | copy-start | bytes 1540
  31.6 12.4 %copy-start.5 = (f32[1,128]{1,0:T(1,128)S(1)}, f32[1,128]{1,0:T(1,128)}, u32[]{:S(2)}) copy-start(f32[1,128]{1,0:T(1,128)} %target_ref.1) | copy-start | bytes 1540
  44.1 6.9 %copy-start.1 = (bf16[128,128]{1,0:T(8,128)(2,1)S(1)}, bf16[128,128]{1,0:T(8,128)(2,1)}, u32[]{:S(2)}) copy-start(bf16[128,128]{1,0:T(8,128)(2,1)} %features_ref.1) | copy-start | bytes 98308
  44.1 6.9 %collective-permute-start = (bf16[1424,128]{1,0:T(8,128)(2,1)S(1)}, bf16[1424,128]{1,0:T(8,128)(2,1)S(1)}, u32[]{:S(2)}, u32[]{:S(2)}) collective-permute-start(bf16[1424,128]{1,0:T(8,128)(2,1)S(1)} %pack.1.own_ref), channel_id=1, source_target_pairs={{0,1},{1,0},{2,3},{3,2},{4,5},{5,4},{6,7},{7,6},{8,9},{9,8},{10,11... | collective-permute-start | bytes 1093640 | tf_op jit(solution)/shard_map/ppermute | solution.py:252

commit v6 on v5

--- a/solution.py
+++ b/solution.py
@@ -40,20 +40,58 @@
     return jnp.maximum(values, 0.2 * values)
 
 
-def prepare_kernel(features_hbm, presence_hbm, send_ref, presence_ref, rows_ref, sems):
-    part = rows_ref.shape[0]
+def split_rows(vector):
+    high = vector.astype(jnp.bfloat16).astype(jnp.float32)
+    rest = vector - high
+    middle = rest.astype(jnp.bfloat16).astype(jnp.float32)
+    return high, middle, rest - middle
+
+
+def prepare_kernel(
+    features_hbm,
+    presence_hbm,
+    proj_hbm,
+    weight_hbm,
+    source_hbm,
+    target_hbm,
+    send_ref,
+    presence_ref,
+    table_ref,
+    rows_ref,
+    source_ref,
+    target_ref,
+    sems,
+):
+    part, width = rows_ref.shape
     start = (pair_of_device() * SIZES["c"] + lax.axis_index("c")) * part
-    rows_copy = pltpu.make_async_copy(
-        features_hbm.at[pl.ds(pl.multiple_of(start, part), part)], rows_ref, sems.at[0]
-    )
-    presence_copy = pltpu.make_async_copy(presence_hbm, presence_ref, sems.at[1])
-    rows_copy.start()
-    presence_copy.start()
-    rows_copy.wait()
+    pairs = [
+        (features_hbm.at[pl.ds(pl.multiple_of(start, part), part)], rows_ref),
+        (presence_hbm, presence_ref),
+        (proj_hbm, table_ref.at[:width]),
+        (source_hbm, source_ref),
+        (target_hbm, target_ref),
+    ]
+    for i in range(weight_hbm.shape[1] // width):
+        pairs.append(
+            (
+                weight_hbm.at[:, i * width : (i + 1) * width],
+                table_ref.at[(i + 1) * width : (i + 2) * width],
+            )
+        )
+    copies = [pltpu.make_async_copy(*pair, sems.at[i]) for i, pair in enumerate(pairs)]
+    for copy in copies:
+        copy.start()
+    copies[0].wait()
     rows = rows_ref[...]
     for i in range(send_ref.shape[0]):
         send_ref[i] = rows
-    presence_copy.wait()
+    for copy in copies[1:]:
+        copy.wait()
+    row = lax.broadcasted_iota(jnp.int32, (16, width), 0)
+    block = jnp.zeros((16, width), jnp.float32)
+    for i, vector in enumerate(split_rows(source_ref[...]) + split_rows(target_ref[...])):
+        block = jnp.where(row == i, vector, block)
+    table_ref[3 * width :] = block.astype(jnp.bfloat16)
 
 
 def pick_kernel(presence_ref, gathered_ref, out_ref, slots_ref):
@@ -67,26 +105,13 @@
             out_ref[copy, i] = rows
 
 
-def split_rows(vector):
-    high = vector.astype(jnp.bfloat16).astype(jnp.float32)
-    rest = vector - high
-    middle = rest.astype(jnp.bfloat16).astype(jnp.float32)
-    return high, middle, rest - middle
-
-
-def pack_kernel(own_ref, proj_ref, weight_ref, source_ref, target_ref, out_ref):
+def pack_kernel(own_ref, table_ref, far_ref, out_ref):
     lows, slots, part, width = own_ref.shape
     rows = lows * slots * part
+    size = table_ref.shape[0]
     out_ref[:rows] = own_ref[...].reshape(rows, width)
-    out_ref[rows : rows + width] = proj_ref[...]
-    for i in range(weight_ref.shape[1] // width):
-        start = rows + (i + 1) * width
-        out_ref[start : start + width] = weight_ref[:, i * width : (i + 1) * width]
-    row = lax.broadcasted_iota(jnp.int32, (16, width), 0)
-    block = jnp.zeros((16, width), jnp.float32)
-    for i, vector in enumerate(split_rows(source_ref[...]) + split_rows(target_ref[...])):
-        block = jnp.where(row == i, vector, block)
-    out_ref[rows + 3 * width :] = block.astype(jnp.bfloat16)
+    out_ref[rows : rows + size] = table_ref[...]
+    out_ref[rows + size :] = far_ref[...]
 
 
 def mask_kernel(presence_ref, masks_ref, out_ref):
@@ -109,14 +134,15 @@
 
 def attend_kernel(own_ref, other_ref, features_ref, added_ref, out_ref, values, tables):
     slots, lows, cores, part, columns = values.shape
-    heads = cores
-    width = columns // heads
+    heads, size, width = tables.shape
     tile = added_ref.shape[1]
     share = slots * part
     rows = lows * share
     core = lax.axis_index("c")
+    upper = lax.axis_index("yl") // 2
     for ref, side in ((own_ref, core), (other_ref, 1 - core)):
-        tables[side] = ref[rows:]
+        tables[cores * upper + side] = ref[rows : rows + size]
+        tables[cores * (1 - upper) + side] = ref[rows + size :]
     both = jnp.concatenate([tables[h, :width] for h in range(heads)], axis=1)
 
     def project(block):
@@ -129,7 +155,7 @@
             values[:, pair, side] = block.reshape(slots, part, columns)
 
     local = project(features_ref[...]).astype(jnp.float32)
-    row = lax.broadcasted_iota(jnp.int32, (16, width), 0)
+    row = lax.broadcasted_iota(jnp.int32, (8 * heads, width), 0)
     target_terms, self_source, spread = [], [], []
     for h in range(heads):
         wide = tables[h, 3 * width :].astype(jnp.float32)
@@ -138,7 +164,7 @@
         mine = local[:, h * width : (h + 1) * width]
         target_terms.append(LOG2E * jnp.sum(mine * target, axis=1, keepdims=True))
         self_source.append(LOG2E * jnp.sum(mine * source, axis=1, keepdims=True))
-        block = jnp.zeros((16, width), jnp.float32)
+        block = jnp.zeros((8 * heads, width), jnp.float32)
         for i in range(3):
             block = jnp.where(row == 8 * h + i, wide[i : i + 1], block)
         spread.append(block)
@@ -199,8 +225,7 @@
         )
         columns.append(jnp.dot(joined, table, preferred_element_type=jnp.float32))
     mixed = jnp.concatenate(columns, axis=1).astype(jnp.bfloat16)
-    for copy in range(out_ref.shape[0]):
-        out_ref[copy] = mixed
+    out_ref[...] = mixed
 
 
 def per_device(features, proj_weight, score_source, score_target, out_weight, presence, tile_masks):
@@ -212,23 +237,34 @@
     smem = pl.BlockSpec(memory_space=pltpu.SMEM)
     raw = pl.BlockSpec(memory_space=pltpu.HBM)
 
-    features_far = pltpu.with_memory_space_constraint(features, pltpu.HBM)
-    presence_far = pltpu.with_memory_space_constraint(presence, pltpu.HBM)
-    send, presence = pl.pallas_call(
+    far = [
+        pltpu.with_memory_space_constraint(value, pltpu.HBM)
+        for value in (features, presence, proj_weight, out_weight, score_source, score_target)
+    ]
+    size = width + out_weight.shape[1] + 16
+    send, presence, table = pl.pallas_call(
         prepare_kernel,
         out_shape=(
             jax.ShapeDtypeStruct((NODES, part, width), jnp.bfloat16),
             jax.ShapeDtypeStruct(presence.shape, jnp.int32),
+            jax.ShapeDtypeStruct((size, width), jnp.bfloat16),
         ),
-        in_specs=[raw, raw],
-        out_specs=(vmem, vmem),
-        scratch_shapes=[pltpu.VMEM((part, width), jnp.bfloat16), pltpu.SemaphoreType.DMA((2,))],
+        in_specs=[raw] * 6,
+        out_specs=(vmem,) * 3,
+        scratch_shapes=[
+            pltpu.VMEM((part, width), jnp.bfloat16),
+            pltpu.VMEM(score_source.shape, jnp.float32),
+            pltpu.VMEM(score_target.shape, jnp.float32),
+            pltpu.SemaphoreType.DMA((7,)),
+        ],
         compiler_params=pltpu.CompilerParams(vmem_limit_bytes=4 << 20),
         name="prepare",
-    )(features_far, presence_far)
+    )(*far)
+    far_table = lax.ppermute(table, "yl", [(i, i ^ 2) for i in range(lows)])
     gathered = lax.all_to_all(
         send, EVERY, 0, 0, tiled=True, axis_index_groups=node_groups()
     )
+    gathered, far_table = lax.optimization_barrier((gathered, far_table))
     picked = pl.pallas_call(
         pick_kernel,
         out_shape=jax.ShapeDtypeStruct((lows, slots, part, width), jnp.bfloat16),
@@ -240,15 +276,14 @@
     )(presence, gathered)
     swap = [(0, 1), (1, 0)]
     own = lax.all_to_all(picked, "yl", 0, 0, tiled=True)
-    payload = lows * slots * part + 3 * width + 16
     packed = pl.pallas_call(
         pack_kernel,
-        out_shape=jax.ShapeDtypeStruct((payload, width), jnp.bfloat16),
-        in_specs=[vmem] * 5,
+        out_shape=jax.ShapeDtypeStruct((lows * slots * part + 2 * size, width), jnp.bfloat16),
+        in_specs=[vmem] * 3,
         out_specs=vmem,
         compiler_params=pltpu.CompilerParams(vmem_limit_bytes=4 << 20),
         name="pack",
-    )(own, proj_weight, out_weight, score_source, score_target)
+    )(own, table, far_table)
     other = lax.ppermute(packed, "c", swap)
     cores = SIZES["c"]
     added = pl.pallas_call(
@@ -260,20 +295,20 @@
         cost_estimate=pl.CostEstimate(flops=slots * tile * tile, bytes_accessed=8 * slots * tile * tile, transcendentals=0),
         name="mask",
     )(presence, tile_masks)
-    paired = pl.pallas_call(
+    partial = pl.pallas_call(
         attend_kernel,
-        out_shape=jax.ShapeDtypeStruct((lows, tile, out_weight.shape[1]), jnp.bfloat16),
+        out_shape=jax.ShapeDtypeStruct((tile, out_weight.shape[1]), jnp.bfloat16),
         in_specs=[vmem] * 4,
         out_specs=vmem,
         scratch_shapes=[
-            pltpu.VMEM((slots, lows, cores, part, cores * width), jnp.bfloat16),
-            pltpu.VMEM((cores, 3 * width + 16, width), jnp.bfloat16),
+            pltpu.VMEM((slots, lows, cores, part, 2 * cores * width), jnp.bfloat16),
+            pltpu.VMEM((2 * cores, size, width), jnp.bfloat16),
         ],
         compiler_params=pltpu.CompilerParams(vmem_limit_bytes=16 << 20),
         name="attend",
     )(packed, other, features, added)
-    pieces = lax.all_to_all(paired, "yl", 0, 0, tiled=True)
-    return jnp.sum(pieces.astype(jnp.float32), axis=0).astype(jnp.bfloat16)
+    beside = lax.ppermute(partial, "yl", [(i, i ^ 1) for i in range(lows)])
+    return (partial.astype(jnp.float32) + beside.astype(jnp.float32)).astype(jnp.bfloat16)
 
 
 def solution(mesh):

time: 64.3 us -> 61.5 us (0.956); the launches traced: 63.1 us -> 61.1 us
  blocking collectives: 52 us -> 12.3 us
  starting transfers between devices: 5.6 us -> 29.4 us
  waiting for transfers between devices: 0.62 us -> 12.1 us
  Pallas kernels: 4.11 us -> 6.54 us
    all_to_all x2 -> x0, blocking collectives: 39.6 us -> none  [the longest x1 30.1 us: per_device(): lax.all_to_all(send, EVERY, 0, 0, tiled=True, axis_index_groups=node_grou...]
    all_to_all x0 -> x1, starting transfers between devices: none -> 18 us  [per_device(): lax.all_to_all(send, EVERY, 0, 0, tiled=True, axis_index_groups=node_grou...]
    ppermute x0 -> x2, waiting for transfers between devices: none -> 8.87 us  [the longest x1 5.79 us: per_device(): far_table = lax.ppermute(table, 'yl', [(i, i ^ 2) for i in range(lows)])]
    ppermute x0 -> x2, starting transfers between devices: none -> 5.81 us  [the longest x1 3.89 us: per_device(): far_table = lax.ppermute(table, 'yl', [(i, i ^ 2) for i in range(lows)])]
    all_to_all x0 -> x1, waiting for transfers between devices: none -> 2.46 us  [per_device(): lax.all_to_all(send, EVERY, 0, 0, tiled=True, axis_index_groups=node_grou...]
    pallas_call x2, Pallas kernels: 2.01 us -> 3.57 us  [the longest x1 3.54 us: per_device(): pl.pallas_call(attend_kernel, out_shape=jax.ShapeDtypeStruct((tile, out_w...]
    pallas_call x1, Pallas kernels: 0.74 us -> 1.61 us  [per_device(): pl.pallas_call(prepare_kernel, out_shape=(jax.ShapeDtypeStruct((NODES, pa...]
    reduce_sum x1 -> x0, other arithmetic: 0.67 us -> none  [per_device(): return jnp.sum(pieces.astype(jnp.float32), axis=0).astype(jnp.bfloat16)]
  transfers between devices with their start and end apart: 1 -> 4, of which waited for: 1 -> 4; matrix products, arithmetic and copies ran while one was open for 0% -> 0% of each run, Pallas kernels for 1% -> 1%
where the time goes in v6:
time: 61.5 us; the launch traced here: 61.1 us
  starting transfers between devices  29.4 us (48%)
  blocking collectives  12.3 us (20%)
  waiting for transfers between devices  12.1 us (20%)
  Pallas kernels  6.54 us (11%)
  other arithmetic  0.65 us (1%)
    all_to_all x1, starting transfers between devices, per_device(): lax.all_to_all(send, EVERY, 0, 0, tiled=True, axis_index_groups=node_grou...  18 us
    all_to_all x1, blocking collectives, per_device(): own = lax.all_to_all(picked, 'yl', 0, 0, tiled=True)  12.3 us
    ppermute x1, waiting for transfers between devices, per_device(): far_table = lax.ppermute(table, 'yl', [(i, i ^ 2) for i in range(lows)])  5.79 us
    ppermute x1, starting transfers between devices, per_device(): other = lax.ppermute(packed, 'c', swap)  5.6 us
    ppermute x1, starting transfers between devices, per_device(): far_table = lax.ppermute(table, 'yl', [(i, i ^ 2) for i in range(lows)])  3.89 us
    pallas_call x1, Pallas kernels, per_device(): pl.pallas_call(attend_kernel, out_shape=jax.ShapeDtypeStruct((tile, out_w...  3.54 us
    ppermute x1, waiting for transfers between devices, per_device(): beside = lax.ppermute(partial, 'yl', [(i, i ^ 1) for i in range(lows)])  3.08 us
    all_to_all x1, waiting for transfers between devices, per_device(): lax.all_to_all(send, EVERY, 0, 0, tiled=True, axis_index_groups=node_grou...  2.46 us
  transfers between devices with their start and end apart: 4, of which 4 were waited for; matrix products, arithmetic and copies ran while one was open for 0% of the time, Pallas kernels for 1%

profile of v6, /device:TPU:1, one launch (start us, length us, event | category | flops | bytes accessed | tf_op | source)
XLA Modules:
  0.0 61.1 jit_solution(2351754728874672277)
XLA Ops:
  0.0 1.6 %prepare.1 = (bf16[64,16,128]{2,1,0:T(8,128)(2,1)}, s32[1,64]{1,0:T(1,128)S(1)}, bf16[400,128]{1,0:T(8,128)(2,1)S(1)}) custom-call(bf16[128,128]{1,0:T(8,128)(2,1)} %features_ref.1, s32[1,64]{1,0:T(1,128)} %presence_hbm.1, bf16[128,128]{1,0:T(8,128)(2,1)} %proj_hbm.1, bf16[128,256]{1,0:T(8,128)(2,1)} %weight_hbm.1, f32[1,128]{1,0:T(1,128)} %source_hbm.1, ...), custom_call_target="tpu_custom_call" | custom-call | tf_op jit(solution)/shard_map/prepare/pallas_call | solution.py:245
  1.6 18.0 %all-to-all-start = ((bf16[64,16,128]{2,1,0:T(8,128)(2,1)}), bf16[64,16,128]{2,1,0:T(8,128)(2,1)S(1)}, u32[]{:S(2)}, u32[]{:S(2)}) async-start(bf16[64,16,128]{2,1,0:T(8,128)(2,1)} %get-tuple-element.11), calls=%async_computation | async-start | bytes 524288 | tf_op jit(solution)/shard_map/all_to_all | solution.py:264
  19.7 0.0 copy-start
  19.7 3.9 %collective-permute-start = (bf16[400,128]{1,0:T(8,128)(2,1)S(1)}, bf16[400,128]{1,0:T(8,128)(2,1)S(1)}, u32[]{:S(2)}, u32[]{:S(2)}) collective-permute-start(bf16[400,128]{1,0:T(8,128)(2,1)S(1)} %get-tuple-element.12.table_ref), channel_id=1, source_target_pairs={{0,4},{2,6},{4,0},{6,2},{1,5},{3,7},{5,1},{7,3},{8,12},{10,14},{12... | collective-permute-start | bytes 307208 | tf_op jit(solution)/shard_map/ppermute | solution.py:263
  23.6 5.8 %collective-permute-done.far_ref = bf16[400,128]{1,0:T(8,128)(2,1)S(1)} collective-permute-done((bf16[400,128]{1,0:T(8,128)(2,1)S(1)}, bf16[400,128]{1,0:T(8,128)(2,1)S(1)}, u32[]{:S(2)}, u32[]{:S(2)}) %collective-permute-start) | collective-permute-done | bytes 102432 | tf_op jit(solution)/shard_map/ppermute | solution.py:263
  29.4 2.5 %all-to-all-done.gathered_ref = bf16[64,16,128]{2,1,0:T(8,128)(2,1)S(1)} async-done(((bf16[64,16,128]{2,1,0:T(8,128)(2,1)}), bf16[64,16,128]{2,1,0:T(8,128)(2,1)S(1)}, u32[]{:S(2)}, u32[]{:S(2)}) %all-to-all-start) | async-done | bytes 262176 | tf_op jit(solution)/shard_map/all_to_all | solution.py:264
  31.8 0.7 %pick.1 = bf16[4,16,16,128]{3,2,1,0:T(8,128)(2,1)S(1)} custom-call(s32[1,64]{1,0:T(1,128)S(1)} %get-tuple-element.10.presence_ref, bf16[64,16,128]{2,1,0:T(8,128)(2,1)S(1)} %all-to-all-done.gathered_ref), custom_call_target="tpu_custom_call" | custom-call | tf_op jit(solution)/shard_map/pick/pallas_call | solution.py:268
  32.5 12.3 %all_to_all.10.own_ref = bf16[4,16,16,128]{3,2,1,0:T(8,128)(2,1)S(1)} all-to-all(bf16[4,16,16,128]{3,2,1,0:T(8,128)(2,1)S(1)} %pick.1), channel_id=1, replica_groups=mesh['yh'=2,'z'=8,'x'=4,'yl'=4,'c'=2] {'yl'}, dimensions={0} | all-to-all | bytes 524288 | tf_op jit(solution)/shard_map/all_to_all | solution.py:278
  44.9 0.0 copy-start.1
  44.9 5.6 %collective-permute-start.1 = (bf16[1824,128]{1,0:T(8,128)(2,1)S(1)}, bf16[1824,128]{1,0:T(8,128)(2,1)S(1)}, u32[]{:S(2)}, u32[]{:S(2)}) collective-permute-start(bf16[1824,128]{1,0:T(8,128)(2,1)S(1)} %pack.1.own_ref), channel_id=1, source_target_pairs={{0,1},{1,0},{2,3},{3,2},{4,5},{5,4},{6,7},{7,6},{8,9},{9,8},{10,11... | collective-permute-start | bytes 1400840 | tf_op jit(solution)/shard_map/ppermute | solution.py:287
  50.5 0.0 copy-done
  50.5 0.6 %mask.1.added_ref = f32[16,128,128]{2,1,0:T(8,128)S(1)} custom-call(s32[1,64]{1,0:T(1,128)S(1)} %get-tuple-element.10.presence_ref, s32[1,16,128,128]{3,2,1,0:T(8,128)S(1)} %copy-done), custom_call_target="tpu_custom_call" | custom-call | flops 262144 | bytes 2097152 | tf_op jit(solution)/shard_map/mask/pallas_call | solution.py:289
  51.1 0.8 %collective-permute-done.1.other_ref = bf16[1824,128]{1,0:T(8,128)(2,1)S(1)} collective-permute-done((bf16[1824,128]{1,0:T(8,128)(2,1)S(1)}, bf16[1824,128]{1,0:T(8,128)(2,1)S(1)}, u32[]{:S(2)}, u32[]{:S(2)}) %collective-permute-start.1) | collective-permute-done | bytes 466976 | tf_op jit(solution)/shard_map/ppermute | solution.py:287
  51.9 0.0 copy-done.1
  51.9 3.5 %attend.1 = bf16[128,256]{1,0:T(8,128)(2,1)S(1)} custom-call(bf16[1824,128]{1,0:T(8,128)(2,1)S(1)} %pack.1.own_ref, bf16[1824,128]{1,0:T(8,128)(2,1)S(1)} %collective-permute-done.1.other_ref, bf16[128,128]{1,0:T(8,128)(2,1)S(1)} %copy-done.1, f32[16,128,128]{2,1,0:T(8,128)S(1)} %mask.1.added_ref), custom_call_target="tpu_custom_call" | custom-call | tf_op jit(solution)/shard_map/attend/pallas_call | solution.py:298
  55.5 1.9 %collective-permute-start.2 = (bf16[128,256]{1,0:T(8,128)(2,1)S(1)}, bf16[128,256]{1,0:T(8,128)(2,1)S(1)}, u32[]{:S(2)}, u32[]{:S(2)}) collective-permute-start(bf16[128,256]{1,0:T(8,128)(2,1)S(1)} %attend.1), channel_id=1, source_target_pairs={{0,2},{2,0},{4,6},{6,4},{1,3},{3,1},{5,7},{7,5},{8,10},{10,8},{12,... | collective-permute-start | bytes 196616 | tf_op jit(solution)/shard_map/ppermute | solution.py:310
  57.4 3.1 %collective-permute-done.2 = bf16[128,256]{1,0:T(8,128)(2,1)S(1)} collective-permute-done((bf16[128,256]{1,0:T(8,128)(2,1)S(1)}, bf16[128,256]{1,0:T(8,128)(2,1)S(1)}, u32[]{:S(2)}, u32[]{:S(2)}) %collective-permute-start.2) | collective-permute-done | bytes 65568 | tf_op jit(solution)/shard_map/ppermute | solution.py:310
  60.5 0.6 %add_convert_fusion = bf16[128,256]{1,0:T(8,128)(2,1)} fusion(bf16[128,256]{1,0:T(8,128)(2,1)S(1)} %collective-permute-done.2, bf16[128,256]{1,0:T(8,128)(2,1)S(1)} %attend.1), kind=kLoop, calls=%fused_computation | loop fusion | flops 131072 | bytes 196608 | tf_op jit(solution)/shard_map/convert_element_type | solution.py:311
  (1 shorter events, 0.0 us)
Async XLA Ops:
  1.6 30.2 %all-to-all-start = ((bf16[64,16,128]{2,1,0:T(8,128)(2,1)}), bf16[64,16,128]{2,1,0:T(8,128)(2,1)S(1)}, u32[]{:S(2)}, u32[]{:S(2)}) async-start(bf16[64,16,128]{2,1,0:T(8,128)(2,1)} %get-tuple-element.11), calls=%async_computation | async-start | bytes 524288 | tf_op jit(solution)/shard_map/all_to_all | solution.py:264
  19.7 30.8 %copy-start = (s32[1,16,128,128]{3,2,1,0:T(8,128)S(1)}, s32[1,16,128,128]{3,2,1,0:T(8,128)}, u32[]{:S(2)}) copy-start(s32[1,16,128,128]{3,2,1,0:T(8,128)} %masks_ref.1) | copy-start | bytes 3145732
  19.7 9.7 %collective-permute-start = (bf16[400,128]{1,0:T(8,128)(2,1)S(1)}, bf16[400,128]{1,0:T(8,128)(2,1)S(1)}, u32[]{:S(2)}, u32[]{:S(2)}) collective-permute-start(bf16[400,128]{1,0:T(8,128)(2,1)S(1)} %get-tuple-element.12.table_ref), channel_id=1, source_target_pairs={{0,4},{2,6},{4,0},{6,2},{1,5},{3,7},{5,1},{7,3},{8,12},{10,14},{12... | collective-permute-start | bytes 307208 | tf_op jit(solution)/shard_map/ppermute | solution.py:263
  44.9 7.1 %copy-start.1 = (bf16[128,128]{1,0:T(8,128)(2,1)S(1)}, bf16[128,128]{1,0:T(8,128)(2,1)}, u32[]{:S(2)}) copy-start(bf16[128,128]{1,0:T(8,128)(2,1)} %features_ref.1) | copy-start | bytes 98308
  44.9 7.0 %collective-permute-start.1 = (bf16[1824,128]{1,0:T(8,128)(2,1)S(1)}, bf16[1824,128]{1,0:T(8,128)(2,1)S(1)}, u32[]{:S(2)}, u32[]{:S(2)}) collective-permute-start(bf16[1824,128]{1,0:T(8,128)(2,1)S(1)} %pack.1.own_ref), channel_id=1, source_target_pairs={{0,1},{1,0},{2,3},{3,2},{4,5},{5,4},{6,7},{7,6},{8,9},{9,8},{10,11... | collective-permute-start | bytes 1400840 | tf_op jit(solution)/shard_map/ppermute | solution.py:287
  55.5 5.0 %collective-permute-start.2 = (bf16[128,256]{1,0:T(8,128)(2,1)S(1)}, bf16[128,256]{1,0:T(8,128)(2,1)S(1)}, u32[]{:S(2)}, u32[]{:S(2)}) collective-permute-start(bf16[128,256]{1,0:T(8,128)(2,1)S(1)} %attend.1), channel_id=1, source_target_pairs={{0,2},{2,0},{4,6},{6,4},{1,3},{3,1},{5,7},{7,5},{8,10},{10,8},{12,... | collective-permute-start | bytes 196616 | tf_op jit(solution)/shard_map/ppermute | solution.py:310

commit v7 on v6

--- a/solution.py
+++ b/solution.py
@@ -32,8 +32,19 @@
     return groups
 
 
-def pair_of_device():
-    return lax.axis_index("yl") ^ (2 * lax.axis_index("yh"))
+def square_groups():
+    groups = []
+    for plane in range(SIZES["yh"] * SIZES["z"]):
+        for x in range(0, SIZES["x"], 2):
+            for yl in range(0, SIZES["yl"], 2):
+                groups.append(
+                    [
+                        (plane * SIZES["x"] + x + i) * SIZES["yl"] + yl + j
+                        for i in range(2)
+                        for j in range(2)
+                    ]
+                )
+    return groups
 
 
 def leaky_relu(values):
@@ -47,30 +58,29 @@
     return high, middle, rest - middle
 
 
-def prepare_kernel(
-    features_hbm,
-    presence_hbm,
-    proj_hbm,
-    weight_hbm,
-    source_hbm,
-    target_hbm,
-    send_ref,
-    presence_ref,
-    table_ref,
-    rows_ref,
-    source_ref,
-    target_ref,
-    sems,
+def send_kernel(features_hbm, send_ref, rows_ref, sems):
+    sides, part, width = rows_ref.shape
+    first = (lax.rem(lax.axis_index("yl"), 2) * SIZES["c"] + lax.axis_index("c")) * part
+    copies = []
+    for side in range(sides):
+        start = pl.multiple_of(first + side * (features_hbm.shape[0] // sides), part)
+        copies.append(
+            pltpu.make_async_copy(
+                features_hbm.at[pl.ds(start, part)], rows_ref.at[side], sems.at[side]
+            )
+        )
+        copies[-1].start()
+    for copy in copies:
+        copy.wait()
+    for i in range(send_ref.shape[0]):
+        send_ref[i] = rows_ref[i % sides]
+
+
+def table_kernel(
+    proj_hbm, weight_hbm, source_hbm, target_hbm, table_ref, source_ref, target_ref, sems
 ):
-    part, width = rows_ref.shape
-    start = (pair_of_device() * SIZES["c"] + lax.axis_index("c")) * part
-    pairs = [
-        (features_hbm.at[pl.ds(pl.multiple_of(start, part), part)], rows_ref),
-        (presence_hbm, presence_ref),
-        (proj_hbm, table_ref.at[:width]),
-        (source_hbm, source_ref),
-        (target_hbm, target_ref),
-    ]
+    width = table_ref.shape[1]
+    pairs = [(proj_hbm, table_ref.at[:width]), (source_hbm, source_ref), (target_hbm, target_ref)]
     for i in range(weight_hbm.shape[1] // width):
         pairs.append(
             (
@@ -81,11 +91,7 @@
     copies = [pltpu.make_async_copy(*pair, sems.at[i]) for i, pair in enumerate(pairs)]
     for copy in copies:
         copy.start()
-    copies[0].wait()
-    rows = rows_ref[...]
-    for i in range(send_ref.shape[0]):
-        send_ref[i] = rows
-    for copy in copies[1:]:
+    for copy in copies:
         copy.wait()
     row = lax.broadcasted_iota(jnp.int32, (16, width), 0)
     block = jnp.zeros((16, width), jnp.float32)
@@ -94,15 +100,19 @@
     table_ref[3 * width :] = block.astype(jnp.bfloat16)
 
 
-def pick_kernel(presence_ref, gathered_ref, out_ref, slots_ref):
-    slot = jnp.int32(0)
+def pick_kernel(presence_ref, near_ref, gathered_ref, out_ref, slots_ref):
+    members, slots = out_ref.shape[:2]
+    ends = [jnp.int32(0), jnp.int32(0)]
     for tile in range(gathered_ref.shape[0]):
-        slots_ref[slot] = gathered_ref[tile]
-        slot = jnp.minimum(slot + presence_ref[0, tile], out_ref.shape[1])
-    for i in range(out_ref.shape[1]):
-        rows = slots_ref[i]
-        for copy in range(out_ref.shape[0]):
-            out_ref[copy, i] = rows
+        rows = gathered_ref[tile]
+        for i, ref in enumerate((presence_ref, near_ref)):
+            slots_ref[i, ends[i]] = rows
+            ends[i] = jnp.minimum(ends[i] + ref[0, tile], slots)
+    odd = lax.rem(lax.axis_index("x"), 2)
+    for member in range(members):
+        row = odd ^ (member // 2)
+        for k in range(slots):
+            out_ref[member, k] = slots_ref[row, k]
 
 
 def pack_kernel(own_ref, table_ref, far_ref, out_ref):
@@ -150,9 +160,8 @@
 
     for ref, side in ((own_ref, core), (other_ref, 1 - core)):
         for low in range(lows):
-            pair = low ^ (2 * lax.axis_index("yh"))
             block = project(ref[low * share : (low + 1) * share])
-            values[:, pair, side] = block.reshape(slots, part, columns)
+            values[:, low, side] = block.reshape(slots, part, columns)
 
     local = project(features_ref[...]).astype(jnp.float32)
     row = lax.broadcasted_iota(jnp.int32, (8 * heads, width), 0)
@@ -239,43 +248,51 @@
 
     far = [
         pltpu.with_memory_space_constraint(value, pltpu.HBM)
-        for value in (features, presence, proj_weight, out_weight, score_source, score_target)
+        for value in (features, proj_weight, out_weight, score_source, score_target)
     ]
     size = width + out_weight.shape[1] + 16
-    send, presence, table = pl.pallas_call(
-        prepare_kernel,
-        out_shape=(
-            jax.ShapeDtypeStruct((NODES, part, width), jnp.bfloat16),
-            jax.ShapeDtypeStruct(presence.shape, jnp.int32),
-            jax.ShapeDtypeStruct((size, width), jnp.bfloat16),
-        ),
-        in_specs=[raw] * 6,
-        out_specs=(vmem,) * 3,
+    send = pl.pallas_call(
+        send_kernel,
+        out_shape=jax.ShapeDtypeStruct((NODES, part, width), jnp.bfloat16),
+        in_specs=[raw],
+        out_specs=vmem,
+        scratch_shapes=[pltpu.VMEM((2, part, width), jnp.bfloat16), pltpu.SemaphoreType.DMA((2,))],
+        compiler_params=pltpu.CompilerParams(vmem_limit_bytes=4 << 20),
+        name="send",
+    )(far[0])
+    table = pl.pallas_call(
+        table_kernel,
+        out_shape=jax.ShapeDtypeStruct((size, width), jnp.bfloat16),
+        in_specs=[raw] * 4,
+        out_specs=vmem,
         scratch_shapes=[
-            pltpu.VMEM((part, width), jnp.bfloat16),
             pltpu.VMEM(score_source.shape, jnp.float32),
             pltpu.VMEM(score_target.shape, jnp.float32),
-            pltpu.SemaphoreType.DMA((7,)),
+            pltpu.SemaphoreType.DMA((5,)),
         ],
         compiler_params=pltpu.CompilerParams(vmem_limit_bytes=4 << 20),
-        name="prepare",
-    )(*far)
+        cost_estimate=pl.CostEstimate(flops=0, bytes_accessed=4 * size * width, transcendentals=0),
+        name="table",
+    )(*far[1:])
     far_table = lax.ppermute(table, "yl", [(i, i ^ 2) for i in range(lows)])
+    near = lax.ppermute(presence, "x", [(i, i ^ 1) for i in range(SIZES["x"])])
     gathered = lax.all_to_all(
         send, EVERY, 0, 0, tiled=True, axis_index_groups=node_groups()
     )
-    gathered, far_table = lax.optimization_barrier((gathered, far_table))
+    gathered, far_table, near = lax.optimization_barrier((gathered, far_table, near))
     picked = pl.pallas_call(
         pick_kernel,
         out_shape=jax.ShapeDtypeStruct((lows, slots, part, width), jnp.bfloat16),
-        in_specs=[smem, vmem],
-        out_specs=vmem,
-        scratch_shapes=[pltpu.VMEM((slots + 1, part, width), jnp.bfloat16)],
+        in_specs=[smem, smem, vmem],
+        out_specs=vmem,
+        scratch_shapes=[pltpu.VMEM((2, slots + 1, part, width), jnp.bfloat16)],
         compiler_params=pltpu.CompilerParams(vmem_limit_bytes=4 << 20),
         name="pick",
-    )(presence, gathered)
+    )(presence, near, gathered)
     swap = [(0, 1), (1, 0)]
-    own = lax.all_to_all(picked, "yl", 0, 0, tiled=True)
+    own = lax.all_to_all(
+        picked, EVERY, 0, 0, tiled=True, axis_index_groups=square_groups()
+    )
     packed = pl.pallas_call(
         pack_kernel,
         out_shape=jax.ShapeDtypeStruct((lows * slots * part + 2 * size, width), jnp.bfloat16),

time: 61.5 us -> 57.7 us (0.938)
  waiting for transfers between devices: 12.1 us -> 7.7 us
  blocking collectives: 12.3 us -> 8.13 us
  starting transfers between devices: 29.4 us -> 33.4 us
  Pallas kernels: 6.54 us -> 7.23 us
    ppermute x1, waiting for transfers between devices: 5.79 us -> 1.07 us  [per_device(): far_table = lax.ppermute(table, 'yl', [(i, i ^ 2) for i in range(lows)])]
    all_to_all x1, blocking collectives: 12.3 us -> 8.13 us  [per_device(): lax.all_to_all(picked, EVERY, 0, 0, tiled=True, axis_index_groups=square_...]
    ppermute x0 -> x1, starting transfers between devices: none -> 2.92 us  [per_device(): near = lax.ppermute(presence, 'x', [(i, i ^ 1) for i in range(SIZES['x'])])]
    ppermute x0 -> x1, waiting for transfers between devices: none -> 1.68 us  [per_device(): near = lax.ppermute(presence, 'x', [(i, i ^ 1) for i in range(SIZES['x'])])]
    pallas_call x1 -> x2, Pallas kernels: 1.61 us -> 2.41 us  [the longest x1 1.45 us: per_device(): pl.pallas_call(send_kernel, out_shape=jax.ShapeDtypeStruct((NODES, part,...]
    all_to_all x1, waiting for transfers between devices: 2.46 us -> 1.72 us  [per_device(): lax.all_to_all(send, EVERY, 0, 0, tiled=True, axis_index_groups=node_grou...]
    ppermute x1, waiting for transfers between devices: 3.08 us -> 2.46 us  [per_device(): beside = lax.ppermute(partial, 'yl', [(i, i ^ 1) for i in range(lows)])]
    ppermute x1, starting transfers between devices: 1.92 us -> 2.54 us  [per_device(): beside = lax.ppermute(partial, 'yl', [(i, i ^ 1) for i in range(lows)])]
  transfers between devices with their start and end apart: 4 -> 5, of which waited for: 4 -> 5; matrix products, arithmetic and copies ran while one was open for 0% -> 0% of each run, Pallas kernels for 1% -> 3%
where the time goes in v7:
time: 57.7 us; the launch traced here: 57.3 us
  starting transfers between devices  33.4 us (58%)
  blocking collectives  8.13 us (14%)
  waiting for transfers between devices  7.7 us (13%)
  Pallas kernels  7.23 us (13%)
  other arithmetic  0.65 us (1%)
    all_to_all x1, starting transfers between devices, per_device(): lax.all_to_all(send, EVERY, 0, 0, tiled=True, axis_index_groups=node_grou...  18 us
    all_to_all x1, blocking collectives, per_device(): lax.all_to_all(picked, EVERY, 0, 0, tiled=True, axis_index_groups=square_...  8.13 us
    ppermute x1, starting transfers between devices, per_device(): other = lax.ppermute(packed, 'c', swap)  6.16 us
    ppermute x1, starting transfers between devices, per_device(): far_table = lax.ppermute(table, 'yl', [(i, i ^ 2) for i in range(lows)])  3.76 us
    pallas_call x1, Pallas kernels, per_device(): pl.pallas_call(attend_kernel, out_shape=jax.ShapeDtypeStruct((tile, out_w...  3.35 us
    ppermute x1, starting transfers between devices, per_device(): near = lax.ppermute(presence, 'x', [(i, i ^ 1) for i in range(SIZES['x'])])  2.92 us
    ppermute x1, starting transfers between devices, per_device(): beside = lax.ppermute(partial, 'yl', [(i, i ^ 1) for i in range(lows)])  2.54 us
    ppermute x1, waiting for transfers between devices, per_device(): beside = lax.ppermute(partial, 'yl', [(i, i ^ 1) for i in range(lows)])  2.46 us
  transfers between devices with their start and end apart: 5, of which 5 were waited for; matrix products, arithmetic and copies ran while one was open for 0% of the time, Pallas kernels for 3%

profile of v7, /device:TPU:1, one launch (start us, length us, event | category | flops | bytes accessed | tf_op | source)
XLA Modules:
  0.0 57.3 jit_solution(17595159535156127088)
XLA Ops:
  0.0 1.4 %send.1 = bf16[64,16,128]{2,1,0:T(8,128)(2,1)} custom-call(bf16[128,128]{1,0:T(8,128)(2,1)} %features_ref.1), custom_call_target="tpu_custom_call" | custom-call | tf_op jit(solution)/shard_map/send/pallas_call | solution.py:254
  1.5 0.0 copy-start.2
  1.5 18.0 %all-to-all-start = ((bf16[64,16,128]{2,1,0:T(8,128)(2,1)}), bf16[64,16,128]{2,1,0:T(8,128)(2,1)S(1)}, u32[]{:S(2)}, u32[]{:S(2)}) async-start(bf16[64,16,128]{2,1,0:T(8,128)(2,1)} %send.1), calls=%async_computation | async-start | bytes 524288 | tf_op jit(solution)/shard_map/all_to_all | solution.py:279
  19.5 0.0 copy-start
  19.5 1.0 %table.1.table_ref = bf16[400,128]{1,0:T(8,128)(2,1)S(1)} custom-call(bf16[128,128]{1,0:T(8,128)(2,1)} %proj_hbm.1, bf16[128,256]{1,0:T(8,128)(2,1)} %weight_hbm.1, f32[1,128]{1,0:T(1,128)} %source_hbm.1, f32[1,128]{1,0:T(1,128)} %target_hbm.1), custom_call_target="tpu_custom_call" | custom-call | bytes 204800 | tf_op jit(solution)/shard_map/table/pallas_call | solution.py:263
  20.5 3.8 %collective-permute-start = (bf16[400,128]{1,0:T(8,128)(2,1)S(1)}, bf16[400,128]{1,0:T(8,128)(2,1)S(1)}, u32[]{:S(2)}, u32[]{:S(2)}) collective-permute-start(bf16[400,128]{1,0:T(8,128)(2,1)S(1)} %table.1.table_ref), channel_id=1, source_target_pairs={{0,4},{2,6},{4,0},{6,2},{1,5},{3,7},{5,1},{7,3},{8,12},{10,14},{12... | collective-permute-start | bytes 307208 | tf_op jit(solution)/shard_map/ppermute | solution.py:277
  24.3 0.0 copy-done.2
  24.3 2.9 %collective-permute-start.1 = (s32[1,64]{1,0:T(1,128)S(1)}, s32[1,64]{1,0:T(1,128)S(1)}, u32[]{:S(2)}, u32[]{:S(2)}) collective-permute-start(s32[1,64]{1,0:T(1,128)S(1)} %copy-done.2), channel_id=1, source_target_pairs={{0,8},{8,0},{16,24},{24,16},{1,9},{9,1},{17,25},{25,17},{2,10},{10... | collective-permute-start | bytes 776 | tf_op jit(solution)/shard_map/ppermute | solution.py:278
  27.2 1.7 %collective-permute-done.1.near_ref = s32[1,64]{1,0:T(1,128)S(1)} collective-permute-done((s32[1,64]{1,0:T(1,128)S(1)}, s32[1,64]{1,0:T(1,128)S(1)}, u32[]{:S(2)}, u32[]{:S(2)}) %collective-permute-start.1) | collective-permute-done | bytes 288 | tf_op jit(solution)/shard_map/ppermute | solution.py:278
  28.9 1.1 %collective-permute-done.far_ref = bf16[400,128]{1,0:T(8,128)(2,1)S(1)} collective-permute-done((bf16[400,128]{1,0:T(8,128)(2,1)S(1)}, bf16[400,128]{1,0:T(8,128)(2,1)S(1)}, u32[]{:S(2)}, u32[]{:S(2)}) %collective-permute-start) | collective-permute-done | bytes 102432 | tf_op jit(solution)/shard_map/ppermute | solution.py:277
  29.9 1.7 %all-to-all-done.gathered_ref = bf16[64,16,128]{2,1,0:T(8,128)(2,1)S(1)} async-done(((bf16[64,16,128]{2,1,0:T(8,128)(2,1)}), bf16[64,16,128]{2,1,0:T(8,128)(2,1)S(1)}, u32[]{:S(2)}, u32[]{:S(2)}) %all-to-all-start) | async-done | bytes 262176 | tf_op jit(solution)/shard_map/all_to_all | solution.py:279
  31.7 0.8 %pick.1 = bf16[4,16,16,128]{3,2,1,0:T(8,128)(2,1)S(1)} custom-call(s32[1,64]{1,0:T(1,128)S(1)} %copy-done.2, s32[1,64]{1,0:T(1,128)S(1)} %collective-permute-done.1.near_ref, bf16[64,16,128]{2,1,0:T(8,128)(2,1)S(1)} %all-to-all-done.gathered_ref), custom_call_target="tpu_custom_call" | custom-call | tf_op jit(solution)/shard_map/pick/pallas_call | solution.py:283
  32.5 8.1 %all_to_all.10.own_ref = bf16[4,16,16,128]{3,2,1,0:T(8,128)(2,1)S(1)} all-to-all(bf16[4,16,16,128]{3,2,1,0:T(8,128)(2,1)S(1)} %pick.1), channel_id=1, replica_groups={{0,2,8,10},{4,6,12,14},{16,18,24,26},{20,22,28,30},{32,34,40,42},{36,38..., dimensions={0} | all-to-all | bytes 524288 | tf_op jit(solution)/shard_map/all_to_all | solution.py:293
  40.6 0.0 copy-start.1
  40.6 6.2 %collective-permute-start.2 = (bf16[1824,128]{1,0:T(8,128)(2,1)S(1)}, bf16[1824,128]{1,0:T(8,128)(2,1)S(1)}, u32[]{:S(2)}, u32[]{:S(2)}) collective-permute-start(bf16[1824,128]{1,0:T(8,128)(2,1)S(1)} %pack.1.own_ref), channel_id=1, source_target_pairs={{0,1},{1,0},{2,3},{3,2},{4,5},{5,4},{6,7},{7,6},{8,9},{9,8},{10,11... | collective-permute-start | bytes 1400840 | tf_op jit(solution)/shard_map/ppermute | solution.py:304
  46.8 0.0 copy-done
  46.8 0.6 %mask.1.added_ref = f32[16,128,128]{2,1,0:T(8,128)S(1)} custom-call(s32[1,64]{1,0:T(1,128)S(1)} %copy-done.2, s32[1,16,128,128]{3,2,1,0:T(8,128)S(1)} %copy-done), custom_call_target="tpu_custom_call" | custom-call | flops 262144 | bytes 2097152 | tf_op jit(solution)/shard_map/mask/pallas_call | solution.py:306
  47.5 0.8 %collective-permute-done.2.other_ref = bf16[1824,128]{1,0:T(8,128)(2,1)S(1)} collective-permute-done((bf16[1824,128]{1,0:T(8,128)(2,1)S(1)}, bf16[1824,128]{1,0:T(8,128)(2,1)S(1)}, u32[]{:S(2)}, u32[]{:S(2)}) %collective-permute-start.2) | collective-permute-done | bytes 466976 | tf_op jit(solution)/shard_map/ppermute | solution.py:304
  48.2 0.0 copy-done.1
  48.2 3.4 %attend.1 = bf16[128,256]{1,0:T(8,128)(2,1)S(1)} custom-call(bf16[1824,128]{1,0:T(8,128)(2,1)S(1)} %pack.1.own_ref, bf16[1824,128]{1,0:T(8,128)(2,1)S(1)} %collective-permute-done.2.other_ref, bf16[128,128]{1,0:T(8,128)(2,1)S(1)} %copy-done.1, f32[16,128,128]{2,1,0:T(8,128)S(1)} %mask.1.added_ref), custom_call_target="tpu_custom_call" | custom-call | tf_op jit(solution)/shard_map/attend/pallas_call | solution.py:315
  51.6 2.5 %collective-permute-start.3 = (bf16[128,256]{1,0:T(8,128)(2,1)S(1)}, bf16[128,256]{1,0:T(8,128)(2,1)S(1)}, u32[]{:S(2)}, u32[]{:S(2)}) collective-permute-start(bf16[128,256]{1,0:T(8,128)(2,1)S(1)} %attend.1), channel_id=1, source_target_pairs={{0,2},{2,0},{4,6},{6,4},{1,3},{3,1},{5,7},{7,5},{8,10},{10,8},{12,... | collective-permute-start | bytes 196616 | tf_op jit(solution)/shard_map/ppermute | solution.py:327
  54.2 2.5 %collective-permute-done.3 = bf16[128,256]{1,0:T(8,128)(2,1)S(1)} collective-permute-done((bf16[128,256]{1,0:T(8,128)(2,1)S(1)}, bf16[128,256]{1,0:T(8,128)(2,1)S(1)}, u32[]{:S(2)}, u32[]{:S(2)}) %collective-permute-start.3) | collective-permute-done | bytes 65568 | tf_op jit(solution)/shard_map/ppermute | solution.py:327
  56.6 0.6 %add_convert_fusion = bf16[128,256]{1,0:T(8,128)(2,1)} fusion(bf16[128,256]{1,0:T(8,128)(2,1)S(1)} %collective-permute-done.3, bf16[128,256]{1,0:T(8,128)(2,1)S(1)} %attend.1), kind=kLoop, calls=%fused_computation | loop fusion | flops 131072 | bytes 196608 | tf_op jit(solution)/shard_map/convert_element_type | solution.py:328
  (1 shorter events, 0.0 us)
Async XLA Ops:
  1.5 22.8 %copy-start.2 = (s32[1,64]{1,0:T(1,128)S(1)}, s32[1,64]{1,0:T(1,128)}, u32[]{:S(2)}) copy-start(s32[1,64]{1,0:T(1,128)} %presence_ref.3) | copy-start | bytes 772
  1.5 30.2 %all-to-all-start = ((bf16[64,16,128]{2,1,0:T(8,128)(2,1)}), bf16[64,16,128]{2,1,0:T(8,128)(2,1)S(1)}, u32[]{:S(2)}, u32[]{:S(2)}) async-start(bf16[64,16,128]{2,1,0:T(8,128)(2,1)} %send.1), calls=%async_computation | async-start | bytes 524288 | tf_op jit(solution)/shard_map/all_to_all | solution.py:279
  19.5 27.3 %copy-start = (s32[1,16,128,128]{3,2,1,0:T(8,128)S(1)}, s32[1,16,128,128]{3,2,1,0:T(8,128)}, u32[]{:S(2)}) copy-start(s32[1,16,128,128]{3,2,1,0:T(8,128)} %masks_ref.1) | copy-start | bytes 3145732
  20.5 9.5 %collective-permute-start = (bf16[400,128]{1,0:T(8,128)(2,1)S(1)}, bf16[400,128]{1,0:T(8,128)(2,1)S(1)}, u32[]{:S(2)}, u32[]{:S(2)}) collective-permute-start(bf16[400,128]{1,0:T(8,128)(2,1)S(1)} %table.1.table_ref), channel_id=1, source_target_pairs={{0,4},{2,6},{4,0},{6,2},{1,5},{3,7},{5,1},{7,3},{8,12},{10,14},{12... | collective-permute-start | bytes 307208 | tf_op jit(solution)/shard_map/ppermute | solution.py:277
  24.3 4.6 %collective-permute-start.1 = (s32[1,64]{1,0:T(1,128)S(1)}, s32[1,64]{1,0:T(1,128)S(1)}, u32[]{:S(2)}, u32[]{:S(2)}) collective-permute-start(s32[1,64]{1,0:T(1,128)S(1)} %copy-done.2), channel_id=1, source_target_pairs={{0,8},{8,0},{16,24},{24,16},{1,9},{9,1},{17,25},{25,17},{2,10},{10... | collective-permute-start | bytes 776 | tf_op jit(solution)/shard_map/ppermute | solution.py:278
  40.6 7.6 %copy-start.1 = (bf16[128,128]{1,0:T(8,128)(2,1)S(1)}, bf16[128,128]{1,0:T(8,128)(2,1)}, u32[]{:S(2)}) copy-start(bf16[128,128]{1,0:T(8,128)(2,1)} %features_ref.1) | copy-start | bytes 98308
  40.6 7.6 %collective-permute-start.2 = (bf16[1824,128]{1,0:T(8,128)(2,1)S(1)}, bf16[1824,128]{1,0:T(8,128)(2,1)S(1)}, u32[]{:S(2)}, u32[]{:S(2)}) collective-permute-start(bf16[1824,128]{1,0:T(8,128)(2,1)S(1)} %pack.1.own_ref), channel_id=1, source_target_pairs={{0,1},{1,0},{2,3},{3,2},{4,5},{5,4},{6,7},{7,6},{8,9},{9,8},{10,11... | collective-permute-start | bytes 1400840 | tf_op jit(solution)/shard_map/ppermute | solution.py:304
  51.6 5.0 %collective-permute-start.3 = (bf16[128,256]{1,0:T(8,128)(2,1)S(1)}, bf16[128,256]{1,0:T(8,128)(2,1)S(1)}, u32[]{:S(2)}, u32[]{:S(2)}) collective-permute-start(bf16[128,256]{1,0:T(8,128)(2,1)S(1)} %attend.1), channel_id=1, source_target_pairs={{0,2},{2,0},{4,6},{6,4},{1,3},{3,1},{5,7},{7,5},{8,10},{10,8},{12,... | collective-permute-start | bytes 196616 | tf_op jit(solution)/shard_map/ppermute | solution.py:327

commit v8 on v7

--- a/solution.py
+++ b/solution.py
@@ -77,10 +77,11 @@
 
 
 def table_kernel(
-    proj_hbm, weight_hbm, source_hbm, target_hbm, table_ref, source_ref, target_ref, sems
+    proj_hbm, weight_hbm, source_hbm, target_hbm, presence_hbm, table_ref, source_ref, target_ref, row_ref, sems
 ):
     width = table_ref.shape[1]
     pairs = [(proj_hbm, table_ref.at[:width]), (source_hbm, source_ref), (target_hbm, target_ref)]
+    pairs.append((presence_hbm, row_ref))
     for i in range(weight_hbm.shape[1] // width):
         pairs.append(
             (
@@ -97,7 +98,11 @@
     block = jnp.zeros((16, width), jnp.float32)
     for i, vector in enumerate(split_rows(source_ref[...]) + split_rows(target_ref[...])):
         block = jnp.where(row == i, vector, block)
-    table_ref[3 * width :] = block.astype(jnp.bfloat16)
+    table_ref[3 * width : 3 * width + 16] = block.astype(jnp.bfloat16)
+    table_ref[3 * width + 16 :] = jnp.zeros((16, width), jnp.bfloat16)
+    table_ref[3 * width + 16 :, : row_ref.shape[1]] = jnp.broadcast_to(
+        row_ref[...].astype(jnp.float32), (16, row_ref.shape[1])
+    ).astype(jnp.bfloat16)
 
 
 def pick_kernel(presence_ref, near_ref, gathered_ref, out_ref, slots_ref):
@@ -115,13 +120,14 @@
             out_ref[member, k] = slots_ref[row, k]
 
 
-def pack_kernel(own_ref, table_ref, far_ref, out_ref):
+def pack_kernel(own_ref, *refs):
+    tables, out_ref = refs[:-1], refs[-1]
     lows, slots, part, width = own_ref.shape
     rows = lows * slots * part
-    size = table_ref.shape[0]
+    size = tables[0].shape[0]
     out_ref[:rows] = own_ref[...].reshape(rows, width)
-    out_ref[rows : rows + size] = table_ref[...]
-    out_ref[rows + size :] = far_ref[...]
+    for i, ref in enumerate(tables):
+        out_ref[rows + i * size : rows + (i + 1) * size] = ref[...]
 
 
 def mask_kernel(presence_ref, masks_ref, out_ref):
@@ -149,10 +155,10 @@
     share = slots * part
     rows = lows * share
     core = lax.axis_index("c")
-    upper = lax.axis_index("yl") // 2
     for ref, side in ((own_ref, core), (other_ref, 1 - core)):
-        tables[cores * upper + side] = ref[rows : rows + size]
-        tables[cores * (1 - upper) + side] = ref[rows + size :]
+        for flip in range(lows):
+            start = rows + flip * size
+            tables[cores * (lax.axis_index("yl") ^ flip) + side] = ref[start : start + size]
     both = jnp.concatenate([tables[h, :width] for h in range(heads)], axis=1)
 
     def project(block):
@@ -167,7 +173,7 @@
     row = lax.broadcasted_iota(jnp.int32, (8 * heads, width), 0)
     target_terms, self_source, spread = [], [], []
     for h in range(heads):
-        wide = tables[h, 3 * width :].astype(jnp.float32)
+        wide = tables[h, 3 * width : 3 * width + 16].astype(jnp.float32)
         source = wide[0:1] + wide[1:2] + wide[2:3]
         target = wide[3:4] + wide[4:5] + wide[5:6]
         mine = local[:, h * width : (h + 1) * width]
@@ -248,9 +254,9 @@
 
     far = [
         pltpu.with_memory_space_constraint(value, pltpu.HBM)
-        for value in (features, proj_weight, out_weight, score_source, score_target)
+        for value in (features, proj_weight, out_weight, score_source, score_target, presence)
     ]
-    size = width + out_weight.shape[1] + 16
+    size = width + out_weight.shape[1] + 32
     send = pl.pallas_call(
         send_kernel,
         out_shape=jax.ShapeDtypeStruct((NODES, part, width), jnp.bfloat16),
@@ -263,23 +269,29 @@
     table = pl.pallas_call(
         table_kernel,
         out_shape=jax.ShapeDtypeStruct((size, width), jnp.bfloat16),
-        in_specs=[raw] * 4,
+        in_specs=[raw] * 5,
         out_specs=vmem,
         scratch_shapes=[
             pltpu.VMEM(score_source.shape, jnp.float32),
             pltpu.VMEM(score_target.shape, jnp.float32),
-            pltpu.SemaphoreType.DMA((5,)),
+            pltpu.VMEM(presence.shape, jnp.int32),
+            pltpu.SemaphoreType.DMA((6,)),
         ],
         compiler_params=pltpu.CompilerParams(vmem_limit_bytes=4 << 20),
         cost_estimate=pl.CostEstimate(flops=0, bytes_accessed=4 * size * width, transcendentals=0),
         name="table",
     )(*far[1:])
-    far_table = lax.ppermute(table, "yl", [(i, i ^ 2) for i in range(lows)])
-    near = lax.ppermute(presence, "x", [(i, i ^ 1) for i in range(SIZES["x"])])
+    diagonal = [
+        (x * lows + yl, (x ^ 1) * lows + (yl ^ 2)) for x in range(SIZES["x"]) for yl in range(lows)
+    ]
+    tables = {0: table, 2: lax.ppermute(table, ("x", "yl"), diagonal)}
+    for flip in (1, 3):
+        tables[flip] = lax.ppermute(table, "yl", [(i, i ^ flip) for i in range(lows)])
+    near = tables[2][size - 16 : size - 15, : presence.shape[1]].astype(jnp.int32)
     gathered = lax.all_to_all(
         send, EVERY, 0, 0, tiled=True, axis_index_groups=node_groups()
     )
-    gathered, far_table, near = lax.optimization_barrier((gathered, far_table, near))
+    gathered, near = lax.optimization_barrier((gathered, near))
     picked = pl.pallas_call(
         pick_kernel,
         out_shape=jax.ShapeDtypeStruct((lows, slots, part, width), jnp.bfloat16),
@@ -290,17 +302,18 @@
         name="pick",
     )(presence, near, gathered)
     swap = [(0, 1), (1, 0)]
+    picked, tables = lax.optimization_barrier((picked, tables))
     own = lax.all_to_all(
         picked, EVERY, 0, 0, tiled=True, axis_index_groups=square_groups()
     )
     packed = pl.pallas_call(
         pack_kernel,
-        out_shape=jax.ShapeDtypeStruct((lows * slots * part + 2 * size, width), jnp.bfloat16),
-        in_specs=[vmem] * 3,
+        out_shape=jax.ShapeDtypeStruct((lows * slots * part + 4 * size, width), jnp.bfloat16),
+        in_specs=[vmem] * 5,
         out_specs=vmem,
         compiler_params=pltpu.CompilerParams(vmem_limit_bytes=4 << 20),
         name="pack",
-    )(own, table, far_table)
+    )(own, *[tables[flip] for flip in range(4)])
     other = lax.ppermute(packed, "c", swap)
     cores = SIZES["c"]
     added = pl.pallas_call(
@@ -312,20 +325,18 @@
         cost_estimate=pl.CostEstimate(flops=slots * tile * tile, bytes_accessed=8 * slots * tile * tile, transcendentals=0),
         name="mask",
     )(presence, tile_masks)
-    partial = pl.pallas_call(
+    return pl.pallas_call(
         attend_kernel,
         out_shape=jax.ShapeDtypeStruct((tile, out_weight.shape[1]), jnp.bfloat16),
         in_specs=[vmem] * 4,
         out_specs=vmem,
         scratch_shapes=[
-            pltpu.VMEM((slots, lows, cores, part, 2 * cores * width), jnp.bfloat16),
-            pltpu.VMEM((2 * cores, size, width), jnp.bfloat16),
+            pltpu.VMEM((slots, lows, cores, part, lows * cores * width), jnp.bfloat16),
+            pltpu.VMEM((lows * cores, size, width), jnp.bfloat16),
         ],
         compiler_params=pltpu.CompilerParams(vmem_limit_bytes=16 << 20),
         name="attend",
     )(packed, other, features, added)
-    beside = lax.ppermute(partial, "yl", [(i, i ^ 1) for i in range(lows)])
-    return (partial.astype(jnp.float32) + beside.astype(jnp.float32)).astype(jnp.bfloat16)
 
 
 def solution(mesh):

time: 57.7 us -> 56.4 us (0.977)
  Pallas kernels: 7.23 us -> 11 us
  waiting for transfers between devices: 7.7 us -> 5.9 us
  starting transfers between devices: 33.4 us -> 31.8 us
  blocking collectives: 8.13 us -> 7.1 us
  other arithmetic: 0.65 us -> 0.01 us
    pallas_call x1, Pallas kernels: 3.35 us -> 7.2 us  [per_device(): pl.pallas_call(attend_kernel, out_shape=jax.ShapeDtypeStruct((tile, out_w...]
    ppermute x1, starting transfers between devices: 6.16 us -> 4.66 us  [per_device(): other = lax.ppermute(packed, 'c', swap)]
    ppermute x3, waiting for transfers between devices: 5.21 us -> 4.13 us  [the longest x2 2.55 us: per_device(): lax.ppermute(table, 'yl', [(i, i ^ flip) for i in range(lows)])]
    all_to_all x1, waiting for transfers between devices: 1.72 us -> 0.69 us  [per_device(): lax.all_to_all(send, EVERY, 0, 0, tiled=True, axis_index_groups=node_grou...]
    all_to_all x1, blocking collectives: 8.13 us -> 7.1 us  [per_device(): lax.all_to_all(picked, EVERY, 0, 0, tiled=True, axis_index_groups=square_...]
    convert_element_type x1, other arithmetic: 0.65 us -> 0.01 us  [per_device(): near = tables[2][size - 16:size - 15, :presence.shape[1]].astype(jnp.int32)]
  transfers between devices with their start and end apart: 5 -> 5, of which waited for: 5 -> 5; matrix products, arithmetic and copies ran while one was open for 0% -> 0% of each run, Pallas kernels for 3% -> 4%
where the time goes in v8:
time: 56.4 us; the launch traced here: 56 us
  starting transfers between devices  31.8 us (56%)
  Pallas kernels  11 us (20%)
  blocking collectives  7.1 us (13%)
  waiting for transfers between devices  5.9 us (10%)
    all_to_all x1, starting transfers between devices, per_device(): lax.all_to_all(send, EVERY, 0, 0, tiled=True, axis_index_groups=node_grou...  18 us
    pallas_call x1, Pallas kernels, per_device(): pl.pallas_call(attend_kernel, out_shape=jax.ShapeDtypeStruct((tile, out_w...  7.2 us
    all_to_all x1, blocking collectives, per_device(): lax.all_to_all(picked, EVERY, 0, 0, tiled=True, axis_index_groups=square_...  7.1 us
    ppermute x1, starting transfers between devices, per_device(): other = lax.ppermute(packed, 'c', swap)  4.66 us
    ppermute x2, starting transfers between devices, per_device(): lax.ppermute(table, 'yl', [(i, i ^ flip) for i in range(lows)])  4.61 us
    ppermute x1, starting transfers between devices, per_device(): tables = {0: table, 2: lax.ppermute(table, ('x', 'yl'), diagonal)}  4.49 us
    ppermute x2, waiting for transfers between devices, per_device(): lax.ppermute(table, 'yl', [(i, i ^ flip) for i in range(lows)])  2.55 us
    ppermute x1, waiting for transfers between devices, per_device(): tables = {0: table, 2: lax.ppermute(table, ('x', 'yl'), diagonal)}  1.58 us
  transfers between devices with their start and end apart: 5, of which 5 were waited for; matrix products, arithmetic and copies ran while one was open for 0% of the time, Pallas kernels for 4%

profile of v8, /device:TPU:1, one launch (start us, length us, event | category | flops | bytes accessed | tf_op | source)
XLA Modules:
  0.0 56.0 jit_solution(2081683096132847909)
XLA Ops:
  0.0 1.4 %send.1 = bf16[64,16,128]{2,1,0:T(8,128)(2,1)} custom-call(bf16[128,128]{1,0:T(8,128)(2,1)} %features_ref.1), custom_call_target="tpu_custom_call" | custom-call | tf_op jit(solution)/shard_map/send/pallas_call | solution.py:260
  1.5 18.0 %all-to-all-start = ((bf16[64,16,128]{2,1,0:T(8,128)(2,1)}), bf16[64,16,128]{2,1,0:T(8,128)(2,1)S(1)}, u32[]{:S(2)}, u32[]{:S(2)}) async-start(bf16[64,16,128]{2,1,0:T(8,128)(2,1)} %send.1), calls=%async_computation | async-start | bytes 524288 | tf_op jit(solution)/shard_map/all_to_all | solution.py:291
  19.5 0.9 %table.1.refs_0_ = bf16[416,128]{1,0:T(8,128)(2,1)S(1)} custom-call(bf16[128,128]{1,0:T(8,128)(2,1)} %proj_hbm.1, bf16[128,256]{1,0:T(8,128)(2,1)} %weight_hbm.1, f32[1,128]{1,0:T(1,128)} %source_hbm.1, f32[1,128]{1,0:T(1,128)} %target_hbm.1, s32[1,64]{1,0:T(1,128)} %presence_ref.3), custom_call_target="tpu_custom_call" | custom-call | bytes 212992 | tf_op jit(solution)/shard_map/table/pallas_call | solution.py:269
  20.4 0.0 copy-start.2
  20.4 4.5 %collective-permute-start = (bf16[416,128]{1,0:T(8,128)(2,1)S(1)}, bf16[416,128]{1,0:T(8,128)(2,1)S(1)}, u32[]{:S(2)}, u32[]{:S(2)}) collective-permute-start(bf16[416,128]{1,0:T(8,128)(2,1)S(1)} %table.1.refs_0_), channel_id=1, source_target_pairs={{0,12},{2,14},{4,8},{6,10},{8,4},{10,6},{12,0},{14,2},{16,28},{18,... | collective-permute-start | bytes 319496 | tf_op jit(solution)/shard_map/ppermute | solution.py:287
  24.9 2.5 %collective-permute-start.2 = (bf16[416,128]{1,0:T(8,128)(2,1)S(1)}, bf16[416,128]{1,0:T(8,128)(2,1)S(1)}, u32[]{:S(2)}, u32[]{:S(2)}) collective-permute-start(bf16[416,128]{1,0:T(8,128)(2,1)S(1)} %table.1.refs_0_), channel_id=1, source_target_pairs={{0,6},{2,4},{4,2},{6,0},{1,7},{3,5},{5,3},{7,1},{8,14},{10,12},{12... | collective-permute-start | bytes 319496 | tf_op jit(solution)/shard_map/ppermute | solution.py:289
  27.5 2.1 %collective-permute-start.1 = (bf16[416,128]{1,0:T(8,128)(2,1)S(1)}, bf16[416,128]{1,0:T(8,128)(2,1)S(1)}, u32[]{:S(2)}, u32[]{:S(2)}) collective-permute-start(bf16[416,128]{1,0:T(8,128)(2,1)S(1)} %table.1.refs_0_), channel_id=1, source_target_pairs={{0,2},{2,0},{4,6},{6,4},{1,3},{3,1},{5,7},{7,5},{8,10},{10,8},{12,... | collective-permute-start | bytes 319496 | tf_op jit(solution)/shard_map/ppermute | solution.py:289
  29.5 1.6 %collective-permute-done.refs_2_ = bf16[416,128]{1,0:T(8,128)(2,1)S(1)} collective-permute-done((bf16[416,128]{1,0:T(8,128)(2,1)S(1)}, bf16[416,128]{1,0:T(8,128)(2,1)S(1)}, u32[]{:S(2)}, u32[]{:S(2)}) %collective-permute-start) | collective-permute-done | bytes 106528 | tf_op jit(solution)/shard_map/ppermute | solution.py:287
  31.1 0.7 %all-to-all-done.gathered_ref = bf16[64,16,128]{2,1,0:T(8,128)(2,1)S(1)} async-done(((bf16[64,16,128]{2,1,0:T(8,128)(2,1)}), bf16[64,16,128]{2,1,0:T(8,128)(2,1)S(1)}, u32[]{:S(2)}, u32[]{:S(2)}) %all-to-all-start) | async-done | bytes 262176 | tf_op jit(solution)/shard_map/all_to_all | solution.py:291
  31.8 0.0 copy-done.2
  31.8 0.8 %pick.1 = bf16[4,16,16,128]{3,2,1,0:T(8,128)(2,1)S(1)} custom-call(s32[1,64]{1,0:T(1,128)S(1)} %copy-done.2, s32[1,64]{1,0:T(1,128)S(1)} %slice_convert_fusion.near_ref, bf16[64,16,128]{2,1,0:T(8,128)(2,1)S(1)} %all-to-all-done.gathered_ref), custom_call_target="tpu_custom_call" | custom-call | tf_op jit(solution)/shard_map/pick/pallas_call | solution.py:295
  32.6 0.0 copy-start
  32.6 0.7 %collective-permute-done.2.refs_3_ = bf16[416,128]{1,0:T(8,128)(2,1)S(1)} collective-permute-done((bf16[416,128]{1,0:T(8,128)(2,1)S(1)}, bf16[416,128]{1,0:T(8,128)(2,1)S(1)}, u32[]{:S(2)}, u32[]{:S(2)}) %collective-permute-start.2) | collective-permute-done | bytes 106528 | tf_op jit(solution)/shard_map/ppermute | solution.py:289
  33.3 1.8 %collective-permute-done.1.refs_1_ = bf16[416,128]{1,0:T(8,128)(2,1)S(1)} collective-permute-done((bf16[416,128]{1,0:T(8,128)(2,1)S(1)}, bf16[416,128]{1,0:T(8,128)(2,1)S(1)}, u32[]{:S(2)}, u32[]{:S(2)}) %collective-permute-start.1) | collective-permute-done | bytes 106528 | tf_op jit(solution)/shard_map/ppermute | solution.py:289
  35.2 7.1 %all_to_all.10.own_ref = bf16[4,16,16,128]{3,2,1,0:T(8,128)(2,1)S(1)} all-to-all(bf16[4,16,16,128]{3,2,1,0:T(8,128)(2,1)S(1)} %pick.1), channel_id=1, replica_groups={{0,2,8,10},{4,6,12,14},{16,18,24,26},{20,22,28,30},{32,34,40,42},{36,38..., dimensions={0} | all-to-all | bytes 524288 | tf_op jit(solution)/shard_map/all_to_all | solution.py:306
  42.3 0.0 copy-start.1
  42.3 4.7 %collective-permute-start.3 = (bf16[2688,128]{1,0:T(8,128)(2,1)S(1)}, bf16[2688,128]{1,0:T(8,128)(2,1)S(1)}, u32[]{:S(2)}, u32[]{:S(2)}) collective-permute-start(bf16[2688,128]{1,0:T(8,128)(2,1)S(1)} %pack.1.own_ref), channel_id=1, source_target_pairs={{0,1},{1,0},{2,3},{3,2},{4,5},{5,4},{6,7},{7,6},{8,9},{9,8},{10,11... | collective-permute-start | bytes 2064392 | tf_op jit(solution)/shard_map/ppermute | solution.py:317
  47.0 0.0 copy-done
  47.0 0.6 %mask.1.added_ref = f32[16,128,128]{2,1,0:T(8,128)S(1)} custom-call(s32[1,64]{1,0:T(1,128)S(1)} %copy-done.2, s32[1,16,128,128]{3,2,1,0:T(8,128)S(1)} %copy-done), custom_call_target="tpu_custom_call" | custom-call | flops 262144 | bytes 2097152 | tf_op jit(solution)/shard_map/mask/pallas_call | solution.py:319
  47.7 1.1 %collective-permute-done.3.other_ref = bf16[2688,128]{1,0:T(8,128)(2,1)S(1)} collective-permute-done((bf16[2688,128]{1,0:T(8,128)(2,1)S(1)}, bf16[2688,128]{1,0:T(8,128)(2,1)S(1)}, u32[]{:S(2)}, u32[]{:S(2)}) %collective-permute-start.3) | collective-permute-done | bytes 688160 | tf_op jit(solution)/shard_map/ppermute | solution.py:317
  48.8 0.0 copy-done.1
  48.8 7.2 %attend.1 = bf16[128,256]{1,0:T(8,128)(2,1)} custom-call(bf16[2688,128]{1,0:T(8,128)(2,1)S(1)} %pack.1.own_ref, bf16[2688,128]{1,0:T(8,128)(2,1)S(1)} %collective-permute-done.3.other_ref, bf16[128,128]{1,0:T(8,128)(2,1)S(1)} %copy-done.1, f32[16,128,128]{2,1,0:T(8,128)S(1)} %mask.1.added_ref), custom_call_target="tpu_custom_call" | custom-call | tf_op jit(solution)/shard_map/attend/pallas_call | solution.py:328
  (2 shorter events, 0.0 us)
Async XLA Ops:
  1.5 30.4 %all-to-all-start = ((bf16[64,16,128]{2,1,0:T(8,128)(2,1)}), bf16[64,16,128]{2,1,0:T(8,128)(2,1)S(1)}, u32[]{:S(2)}, u32[]{:S(2)}) async-start(bf16[64,16,128]{2,1,0:T(8,128)(2,1)} %send.1), calls=%async_computation | async-start | bytes 524288 | tf_op jit(solution)/shard_map/all_to_all | solution.py:291
  20.4 11.4 %copy-start.2 = (s32[1,64]{1,0:T(1,128)S(1)}, s32[1,64]{1,0:T(1,128)}, u32[]{:S(2)}) copy-start(s32[1,64]{1,0:T(1,128)} %presence_ref.3) | copy-start | bytes 772
  20.4 10.7 %collective-permute-start = (bf16[416,128]{1,0:T(8,128)(2,1)S(1)}, bf16[416,128]{1,0:T(8,128)(2,1)S(1)}, u32[]{:S(2)}, u32[]{:S(2)}) collective-permute-start(bf16[416,128]{1,0:T(8,128)(2,1)S(1)} %table.1.refs_0_), channel_id=1, source_target_pairs={{0,12},{2,14},{4,8},{6,10},{8,4},{10,6},{12,0},{14,2},{16,28},{18,... | collective-permute-start | bytes 319496 | tf_op jit(solution)/shard_map/ppermute | solution.py:287
  24.9 8.4 %collective-permute-start.2 = (bf16[416,128]{1,0:T(8,128)(2,1)S(1)}, bf16[416,128]{1,0:T(8,128)(2,1)S(1)}, u32[]{:S(2)}, u32[]{:S(2)}) collective-permute-start(bf16[416,128]{1,0:T(8,128)(2,1)S(1)} %table.1.refs_0_), channel_id=1, source_target_pairs={{0,6},{2,4},{4,2},{6,0},{1,7},{3,5},{5,3},{7,1},{8,14},{10,12},{12... | collective-permute-start | bytes 319496 | tf_op jit(solution)/shard_map/ppermute | solution.py:289
  27.5 7.7 %collective-permute-start.1 = (bf16[416,128]{1,0:T(8,128)(2,1)S(1)}, bf16[416,128]{1,0:T(8,128)(2,1)S(1)}, u32[]{:S(2)}, u32[]{:S(2)}) collective-permute-start(bf16[416,128]{1,0:T(8,128)(2,1)S(1)} %table.1.refs_0_), channel_id=1, source_target_pairs={{0,2},{2,0},{4,6},{6,4},{1,3},{3,1},{5,7},{7,5},{8,10},{10,8},{12,... | collective-permute-start | bytes 319496 | tf_op jit(solution)/shard_map/ppermute | solution.py:289
  32.6 14.4 %copy-start = (s32[1,16,128,128]{3,2,1,0:T(8,128)S(1)}, s32[1,16,128,128]{3,2,1,0:T(8,128)}, u32[]{:S(2)}) copy-start(s32[1,16,128,128]{3,2,1,0:T(8,128)} %masks_ref.1) | copy-start | bytes 3145732
  42.3 6.4 %copy-start.1 = (bf16[128,128]{1,0:T(8,128)(2,1)S(1)}, bf16[128,128]{1,0:T(8,128)(2,1)}, u32[]{:S(2)}) copy-start(bf16[128,128]{1,0:T(8,128)(2,1)} %features_ref.1) | copy-start | bytes 98308
  42.3 6.4 %collective-permute-start.3 = (bf16[2688,128]{1,0:T(8,128)(2,1)S(1)}, bf16[2688,128]{1,0:T(8,128)(2,1)S(1)}, u32[]{:S(2)}, u32[]{:S(2)}) collective-permute-start(bf16[2688,128]{1,0:T(8,128)(2,1)S(1)} %pack.1.own_ref), channel_id=1, source_target_pairs={{0,1},{1,0},{2,3},{3,2},{4,5},{5,4},{6,7},{7,6},{8,9},{9,8},{10,11... | collective-permute-start | bytes 2064392 | tf_op jit(solution)/shard_map/ppermute | solution.py:317

commit v9 on v8

--- a/solution.py
+++ b/solution.py
@@ -77,7 +77,7 @@
 
 
 def table_kernel(
-    proj_hbm, weight_hbm, source_hbm, target_hbm, presence_hbm, table_ref, source_ref, target_ref, row_ref, sems
+    proj_hbm, weight_hbm, source_hbm, target_hbm, presence_hbm, table_ref, source_ref, target_ref, row_ref, sems, between
 ):
     width = table_ref.shape[1]
     pairs = [(proj_hbm, table_ref.at[:width]), (source_hbm, source_ref), (target_hbm, target_ref)]
@@ -92,6 +92,7 @@
     copies = [pltpu.make_async_copy(*pair, sems.at[i]) for i, pair in enumerate(pairs)]
     for copy in copies:
         copy.start()
+    between()
     for copy in copies:
         copy.wait()
     row = lax.broadcasted_iota(jnp.int32, (16, width), 0)
@@ -103,6 +104,17 @@
     table_ref[3 * width + 16 :, : row_ref.shape[1]] = jnp.broadcast_to(
         row_ref[...].astype(jnp.float32), (16, row_ref.shape[1])
     ).astype(jnp.bfloat16)
+
+
+def prepare_kernel(
+    features_hbm, proj_hbm, weight_hbm, source_hbm, target_hbm, presence_hbm,
+    send_ref, table_ref, rows_ref, source_ref, target_ref, row_ref, send_sems, table_sems,
+):
+    table_kernel(
+        proj_hbm, weight_hbm, source_hbm, target_hbm, presence_hbm,
+        table_ref, source_ref, target_ref, row_ref, table_sems,
+        lambda: send_kernel(features_hbm, send_ref, rows_ref, send_sems),
+    )
 
 
 def pick_kernel(presence_ref, near_ref, gathered_ref, out_ref, slots_ref):
@@ -257,30 +269,25 @@
         for value in (features, proj_weight, out_weight, score_source, score_target, presence)
     ]
     size = width + out_weight.shape[1] + 32
-    send = pl.pallas_call(
-        send_kernel,
-        out_shape=jax.ShapeDtypeStruct((NODES, part, width), jnp.bfloat16),
-        in_specs=[raw],
-        out_specs=vmem,
-        scratch_shapes=[pltpu.VMEM((2, part, width), jnp.bfloat16), pltpu.SemaphoreType.DMA((2,))],
-        compiler_params=pltpu.CompilerParams(vmem_limit_bytes=4 << 20),
-        name="send",
-    )(far[0])
-    table = pl.pallas_call(
-        table_kernel,
-        out_shape=jax.ShapeDtypeStruct((size, width), jnp.bfloat16),
-        in_specs=[raw] * 5,
-        out_specs=vmem,
+    send, table = pl.pallas_call(
+        prepare_kernel,
+        out_shape=(
+            jax.ShapeDtypeStruct((NODES, part, width), jnp.bfloat16),
+            jax.ShapeDtypeStruct((size, width), jnp.bfloat16),
+        ),
+        in_specs=[raw] * 6,
+        out_specs=(vmem, vmem),
         scratch_shapes=[
+            pltpu.VMEM((2, part, width), jnp.bfloat16),
             pltpu.VMEM(score_source.shape, jnp.float32),
             pltpu.VMEM(score_target.shape, jnp.float32),
             pltpu.VMEM(presence.shape, jnp.int32),
+            pltpu.SemaphoreType.DMA((2,)),
             pltpu.SemaphoreType.DMA((6,)),
         ],
         compiler_params=pltpu.CompilerParams(vmem_limit_bytes=4 << 20),
-        cost_estimate=pl.CostEstimate(flops=0, bytes_accessed=4 * size * width, transcendentals=0),
-        name="table",
-    )(*far[1:])
+        name="prepare",
+    )(*far)
     diagonal = [
         (x * lows + yl, (x ^ 1) * lows + (yl ^ 2)) for x in range(SIZES["x"]) for yl in range(lows)
     ]

time: 56.4 us -> 56.6 us (level)
  waiting for transfers between devices: 5.9 us -> 6.72 us
  Pallas kernels: 11 us -> 10.3 us
    all_to_all x1, waiting for transfers between devices: 0.69 us -> 1.63 us  [per_device(): lax.all_to_all(send, EVERY, 0, 0, tiled=True, axis_index_groups=node_grou...]
    pallas_call x2 -> x1, Pallas kernels: 2.35 us -> 1.61 us  [per_device(): pl.pallas_call(prepare_kernel, out_shape=(jax.ShapeDtypeStruct((NODES, pa...]
  transfers between devices with their start and end apart: 5 -> 5, of which waited for: 5 -> 4; matrix products, arithmetic and copies ran while one was open for 0% -> 0% of each run, Pallas kernels for 4% -> 3%
where the time goes in v9:
time: 56.6 us; the launch traced here: 56.1 us
  starting transfers between devices  32 us (57%)
  Pallas kernels  10.3 us (18%)
  blocking collectives  6.95 us (12%)
  waiting for transfers between devices  6.72 us (12%)
    all_to_all x1, starting transfers between devices, per_device(): lax.all_to_all(send, EVERY, 0, 0, tiled=True, axis_index_groups=node_grou...  18 us
    pallas_call x1, Pallas kernels, per_device(): pl.pallas_call(attend_kernel, out_shape=jax.ShapeDtypeStruct((tile, out_w...  7.2 us
    all_to_all x1, blocking collectives, per_device(): lax.all_to_all(picked, EVERY, 0, 0, tiled=True, axis_index_groups=square_...  6.95 us
    ppermute x1, starting transfers between devices, per_device(): other = lax.ppermute(packed, 'c', swap)  4.91 us
    ppermute x2, starting transfers between devices, per_device(): lax.ppermute(table, 'yl', [(i, i ^ flip) for i in range(lows)])  4.61 us
    ppermute x1, starting transfers between devices, per_device(): tables = {0: table, 2: lax.ppermute(table, ('x', 'yl'), diagonal)}  4.49 us
    ppermute x2, waiting for transfers between devices, per_device(): lax.ppermute(table, 'yl', [(i, i ^ flip) for i in range(lows)])  2.35 us
    ppermute x1, waiting for transfers between devices, per_device(): tables = {0: table, 2: lax.ppermute(table, ('x', 'yl'), diagonal)}  1.66 us
  transfers between devices with their start and end apart: 5, of which 4 were waited for; matrix products, arithmetic and copies ran while one was open for 0% of the time, Pallas kernels for 3%

profile of v9, /device:TPU:1, one launch (start us, length us, event | category | flops | bytes accessed | tf_op | source)
XLA Modules:
  0.0 56.1 jit_solution(6629322567110811848)
XLA Ops:
  0.0 1.6 %prepare.1 = (bf16[64,16,128]{2,1,0:T(8,128)(2,1)}, bf16[416,128]{1,0:T(8,128)(2,1)S(1)}) custom-call(bf16[128,128]{1,0:T(8,128)(2,1)} %features_ref.1, bf16[128,128]{1,0:T(8,128)(2,1)} %proj_hbm.1, bf16[128,256]{1,0:T(8,128)(2,1)} %weight_hbm.1, f32[1,128]{1,0:T(1,128)} %source_hbm.1, f32[1,128]{1,0:T(1,128)} %target_hbm.1, s32[1,64]{1,0:T(1,128)} %presence_ref.3), custom_call_target="tpu_custom_call" | custom-call | tf_op jit(solution)/shard_map/prepare/pallas_call | solution.py:272
  1.6 18.0 %all-to-all-start = ((bf16[64,16,128]{2,1,0:T(8,128)(2,1)}), bf16[64,16,128]{2,1,0:T(8,128)(2,1)S(1)}, u32[]{:S(2)}, u32[]{:S(2)}) async-start(bf16[64,16,128]{2,1,0:T(8,128)(2,1)} %get-tuple-element.14), calls=%async_computation | async-start | bytes 524288 | tf_op jit(solution)/shard_map/all_to_all | solution.py:298
  19.7 0.0 copy-start.2
  19.7 4.5 %collective-permute-start = (bf16[416,128]{1,0:T(8,128)(2,1)S(1)}, bf16[416,128]{1,0:T(8,128)(2,1)S(1)}, u32[]{:S(2)}, u32[]{:S(2)}) collective-permute-start(bf16[416,128]{1,0:T(8,128)(2,1)S(1)} %get-tuple-element.19.refs_0_), channel_id=1, source_target_pairs={{0,12},{2,14},{4,8},{6,10},{8,4},{10,6},{12,0},{14,2},{16,28},{18,... | collective-permute-start | bytes 319496 | tf_op jit(solution)/shard_map/ppermute | solution.py:294
  24.2 2.5 %collective-permute-start.2 = (bf16[416,128]{1,0:T(8,128)(2,1)S(1)}, bf16[416,128]{1,0:T(8,128)(2,1)S(1)}, u32[]{:S(2)}, u32[]{:S(2)}) collective-permute-start(bf16[416,128]{1,0:T(8,128)(2,1)S(1)} %get-tuple-element.19.refs_0_), channel_id=1, source_target_pairs={{0,6},{2,4},{4,2},{6,0},{1,7},{3,5},{5,3},{7,1},{8,14},{10,12},{12... | collective-permute-start | bytes 319496 | tf_op jit(solution)/shard_map/ppermute | solution.py:296
  26.7 2.1 %collective-permute-start.1 = (bf16[416,128]{1,0:T(8,128)(2,1)S(1)}, bf16[416,128]{1,0:T(8,128)(2,1)S(1)}, u32[]{:S(2)}, u32[]{:S(2)}) collective-permute-start(bf16[416,128]{1,0:T(8,128)(2,1)S(1)} %get-tuple-element.19.refs_0_), channel_id=1, source_target_pairs={{0,2},{2,0},{4,6},{6,4},{1,3},{3,1},{5,7},{7,5},{8,10},{10,8},{12,... | collective-permute-start | bytes 319496 | tf_op jit(solution)/shard_map/ppermute | solution.py:296
  28.8 1.7 %collective-permute-done.refs_2_ = bf16[416,128]{1,0:T(8,128)(2,1)S(1)} collective-permute-done((bf16[416,128]{1,0:T(8,128)(2,1)S(1)}, bf16[416,128]{1,0:T(8,128)(2,1)S(1)}, u32[]{:S(2)}, u32[]{:S(2)}) %collective-permute-start) | collective-permute-done | bytes 106528 | tf_op jit(solution)/shard_map/ppermute | solution.py:294
  30.4 1.6 %all-to-all-done.gathered_ref = bf16[64,16,128]{2,1,0:T(8,128)(2,1)S(1)} async-done(((bf16[64,16,128]{2,1,0:T(8,128)(2,1)}), bf16[64,16,128]{2,1,0:T(8,128)(2,1)S(1)}, u32[]{:S(2)}, u32[]{:S(2)}) %all-to-all-start) | async-done | bytes 262176 | tf_op jit(solution)/shard_map/all_to_all | solution.py:298
  32.1 0.0 copy-done.2
  32.1 0.8 %pick.1 = bf16[4,16,16,128]{3,2,1,0:T(8,128)(2,1)S(1)} custom-call(s32[1,64]{1,0:T(1,128)S(1)} %copy-done.2, s32[1,64]{1,0:T(1,128)S(1)} %slice_convert_fusion.near_ref, bf16[64,16,128]{2,1,0:T(8,128)(2,1)S(1)} %all-to-all-done.gathered_ref), custom_call_target="tpu_custom_call" | custom-call | tf_op jit(solution)/shard_map/pick/pallas_call | solution.py:302
  32.9 0.0 copy-start
  32.9 0.0 collective-permute-done.2.refs_3_
  32.9 2.3 %collective-permute-done.1.refs_1_ = bf16[416,128]{1,0:T(8,128)(2,1)S(1)} collective-permute-done((bf16[416,128]{1,0:T(8,128)(2,1)S(1)}, bf16[416,128]{1,0:T(8,128)(2,1)S(1)}, u32[]{:S(2)}, u32[]{:S(2)}) %collective-permute-start.1) | collective-permute-done | bytes 106528 | tf_op jit(solution)/shard_map/ppermute | solution.py:296
  35.2 7.0 %all_to_all.10.own_ref = bf16[4,16,16,128]{3,2,1,0:T(8,128)(2,1)S(1)} all-to-all(bf16[4,16,16,128]{3,2,1,0:T(8,128)(2,1)S(1)} %pick.1), channel_id=1, replica_groups={{0,2,8,10},{4,6,12,14},{16,18,24,26},{20,22,28,30},{32,34,40,42},{36,38..., dimensions={0} | all-to-all | bytes 524288 | tf_op jit(solution)/shard_map/all_to_all | solution.py:313
  42.2 0.0 copy-start.1
  42.3 4.9 %collective-permute-start.3 = (bf16[2688,128]{1,0:T(8,128)(2,1)S(1)}, bf16[2688,128]{1,0:T(8,128)(2,1)S(1)}, u32[]{:S(2)}, u32[]{:S(2)}) collective-permute-start(bf16[2688,128]{1,0:T(8,128)(2,1)S(1)} %pack.1.own_ref), channel_id=1, source_target_pairs={{0,1},{1,0},{2,3},{3,2},{4,5},{5,4},{6,7},{7,6},{8,9},{9,8},{10,11... | collective-permute-start | bytes 2064392 | tf_op jit(solution)/shard_map/ppermute | solution.py:324
  47.2 0.0 copy-done
  47.2 0.6 %mask.1.added_ref = f32[16,128,128]{2,1,0:T(8,128)S(1)} custom-call(s32[1,64]{1,0:T(1,128)S(1)} %copy-done.2, s32[1,16,128,128]{3,2,1,0:T(8,128)S(1)} %copy-done), custom_call_target="tpu_custom_call" | custom-call | flops 262144 | bytes 2097152 | tf_op jit(solution)/shard_map/mask/pallas_call | solution.py:326
  47.8 1.1 %collective-permute-done.3.other_ref = bf16[2688,128]{1,0:T(8,128)(2,1)S(1)} collective-permute-done((bf16[2688,128]{1,0:T(8,128)(2,1)S(1)}, bf16[2688,128]{1,0:T(8,128)(2,1)S(1)}, u32[]{:S(2)}, u32[]{:S(2)}) %collective-permute-start.3) | collective-permute-done | bytes 688160 | tf_op jit(solution)/shard_map/ppermute | solution.py:324
  48.9 0.0 copy-done.1
  48.9 7.2 %attend.1 = bf16[128,256]{1,0:T(8,128)(2,1)} custom-call(bf16[2688,128]{1,0:T(8,128)(2,1)S(1)} %pack.1.own_ref, bf16[2688,128]{1,0:T(8,128)(2,1)S(1)} %collective-permute-done.3.other_ref, bf16[128,128]{1,0:T(8,128)(2,1)S(1)} %copy-done.1, f32[16,128,128]{2,1,0:T(8,128)S(1)} %mask.1.added_ref), custom_call_target="tpu_custom_call" | custom-call | tf_op jit(solution)/shard_map/attend/pallas_call | solution.py:335
  (2 shorter events, 0.1 us)
Async XLA Ops:
  1.6 30.5 %all-to-all-start = ((bf16[64,16,128]{2,1,0:T(8,128)(2,1)}), bf16[64,16,128]{2,1,0:T(8,128)(2,1)S(1)}, u32[]{:S(2)}, u32[]{:S(2)}) async-start(bf16[64,16,128]{2,1,0:T(8,128)(2,1)} %get-tuple-element.14), calls=%async_computation | async-start | bytes 524288 | tf_op jit(solution)/shard_map/all_to_all | solution.py:298
  19.7 12.4 %copy-start.2 = (s32[1,64]{1,0:T(1,128)S(1)}, s32[1,64]{1,0:T(1,128)}, u32[]{:S(2)}) copy-start(s32[1,64]{1,0:T(1,128)} %presence_ref.3) | copy-start | bytes 772
  19.7 10.8 %collective-permute-start = (bf16[416,128]{1,0:T(8,128)(2,1)S(1)}, bf16[416,128]{1,0:T(8,128)(2,1)S(1)}, u32[]{:S(2)}, u32[]{:S(2)}) collective-permute-start(bf16[416,128]{1,0:T(8,128)(2,1)S(1)} %get-tuple-element.19.refs_0_), channel_id=1, source_target_pairs={{0,12},{2,14},{4,8},{6,10},{8,4},{10,6},{12,0},{14,2},{16,28},{18,... | collective-permute-start | bytes 319496 | tf_op jit(solution)/shard_map/ppermute | solution.py:294
  24.2 8.7 %collective-permute-start.2 = (bf16[416,128]{1,0:T(8,128)(2,1)S(1)}, bf16[416,128]{1,0:T(8,128)(2,1)S(1)}, u32[]{:S(2)}, u32[]{:S(2)}) collective-permute-start(bf16[416,128]{1,0:T(8,128)(2,1)S(1)} %get-tuple-element.19.refs_0_), channel_id=1, source_target_pairs={{0,6},{2,4},{4,2},{6,0},{1,7},{3,5},{5,3},{7,1},{8,14},{10,12},{12... | collective-permute-start | bytes 319496 | tf_op jit(solution)/shard_map/ppermute | solution.py:296
  26.7 8.5 %collective-permute-start.1 = (bf16[416,128]{1,0:T(8,128)(2,1)S(1)}, bf16[416,128]{1,0:T(8,128)(2,1)S(1)}, u32[]{:S(2)}, u32[]{:S(2)}) collective-permute-start(bf16[416,128]{1,0:T(8,128)(2,1)S(1)} %get-tuple-element.19.refs_0_), channel_id=1, source_target_pairs={{0,2},{2,0},{4,6},{6,4},{1,3},{3,1},{5,7},{7,5},{8,10},{10,8},{12,... | collective-permute-start | bytes 319496 | tf_op jit(solution)/shard_map/ppermute | solution.py:296
  32.9 14.3 %copy-start = (s32[1,16,128,128]{3,2,1,0:T(8,128)S(1)}, s32[1,16,128,128]{3,2,1,0:T(8,128)}, u32[]{:S(2)}) copy-start(s32[1,16,128,128]{3,2,1,0:T(8,128)} %masks_ref.1) | copy-start | bytes 3145732
  42.2 6.7 %copy-start.1 = (bf16[128,128]{1,0:T(8,128)(2,1)S(1)}, bf16[128,128]{1,0:T(8,128)(2,1)}, u32[]{:S(2)}) copy-start(bf16[128,128]{1,0:T(8,128)(2,1)} %features_ref.1) | copy-start | bytes 98308
  42.3 6.7 %collective-permute-start.3 = (bf16[2688,128]{1,0:T(8,128)(2,1)S(1)}, bf16[2688,128]{1,0:T(8,128)(2,1)S(1)}, u32[]{:S(2)}, u32[]{:S(2)}) collective-permute-start(bf16[2688,128]{1,0:T(8,128)(2,1)S(1)} %pack.1.own_ref), channel_id=1, source_target_pairs={{0,1},{1,0},{2,3},{3,2},{4,5},{5,4},{6,7},{7,6},{8,9},{9,8},{10,11... | collective-permute-start | bytes 2064392 | tf_op jit(solution)/shard_map/ppermute | solution.py:324
